TPU v7x, 256 devices: a whole 4x4x8 slice. The times are simulated.
256 devices in a mesh: comp: 4 (over z_lo), dom: 64 (over y, x, z_hi, core).
Axes of the slice: x: 4, y: 4, z: 8 (z_hi: 2, z_lo: 4; z = z_hi * 4 + z_lo), core: 2. Of those that a mesh axis runs over, the one named last changes fastest.
Arguments:
- airside_exchange: bfloat16 [4, 4, 65536], P('comp', None, 'dom'), may hold values from -6 to 6
- regrid_matrix_partitions: bfloat16 [4, 512, 4, 128, 128], P('comp', 'dom'), may hold values from -0.25 to 0.25
- regrid_destination_latitude: int32 [4, 512, 4], P('comp', 'dom'), may hold values from 0 to 2047, all different within a row
- thermal_departure: float32 [32, 2048, 128], P(None, ('comp', 'dom')), may hold values from -6 to 6
- diffusivity_coefficient: float32 [31, 2048, 128], P(None, ('comp', 'dom')), may hold values from 0.05 to 3
- elevation_anomaly_profile: float32 [2048, 128], P(('comp', 'dom')), may hold values from -3 to 3
- depth_integrated_volume_flow: float32 [2, 2048, 128], P(None, ('comp', 'dom')), may hold values from -2 to 2
- marine_indicator: int32 [2048, 128], P(('comp', 'dom')), may hold values 0 or 1
Outputs:
- ocean_temperature: float32 [32, 2048, 128], P(None, ('comp', 'dom'))
- ocean_height: float32 [2048, 128], P(('comp', 'dom'))
- atm_surface: bfloat16 [4, 2, 65536], P('comp', None, 'dom')
Inputs may be any that keep to these rules, and one draw needn't show every extreme that they name: `regrid_destination_latitude`: each (section, source block) names 4 different ocean blocks, and every ocean block is named somewhere; ocean block b is grid row b.
All inputs are finite; a program needn't handle non-finite values. No bound on the sum of `marine_indicator` on one device may be relied on, other than what follows from the above.
Results may differ from a plain program's by a relative error of at most 0.0048.
Values may be sent and summed in bfloat16 or wider, within the bound.
No kernel may reach another device: no remote copies, remote signals or barrier semaphores. Data moves between devices by JAX's collectives and lax.ppermute only.
A program may use at most 64 MiB of HBM per device.

v0:
```python
import jax
import jax.numpy as jnp
from jax import lax
from jax.sharding import PartitionSpec as P

NSTEP = 2
NSUB = 8


wave_gain = 0.35
stress_gain = 0.1
fresh_gain = 0.1
spread_gain = 0.2
heating_gain = 0.5


def with_halo(block, sides, width):
    for axis, dim in sides:
        count = lax.axis_size(axis)
        forward = [(i, i + 1) for i in range(count - 1)]
        backward = [(target, source) for source, target in forward]
        low = lax.ppermute(
            lax.slice_in_dim(block, block.shape[dim] - width, None, axis=dim), axis, forward
        )
        high = lax.ppermute(lax.slice_in_dim(block, 0, width, axis=dim), axis, backward)
        block = jnp.concatenate([low, block, high], axis=dim)
    return block


def vertical_solve(explicit, diffusivity_coefficient):
    levels_all = explicit.shape[0]
    solved = []
    ratios = []
    for layer_index in range(levels_all):
        upward = (
            diffusivity_coefficient[layer_index - 1]
            if layer_index > 0
            else jnp.zeros_like(explicit[0])
        )
        downward = (
            diffusivity_coefficient[layer_index]
            if layer_index < levels_all - 1
            else jnp.zeros_like(explicit[0])
        )
        pivots = 1.0 + upward + downward
        if layer_index > 0:
            pivots = pivots - upward * ratios[-1]
            solved.append((explicit[layer_index] + upward * solved[-1]) / pivots)
        else:
            solved.append(explicit[layer_index] / pivots)
        ratios.append(downward / pivots)
    result = [solved[-1]]
    for layer_index in range(levels_all - 2, -1, -1):
        result.append(solved[layer_index] + ratios[layer_index] * result[-1])
    return jnp.stack(result[::-1])


def shards(
    airside_exchange,
    regrid_matrix_partitions,
    regrid_destination_latitude,
    thermal_departure,
    diffusivity_coefficient,
    elevation_anomaly_profile,
    depth_integrated_volume_flow,
    marine_indicator,
):
    groups = lax.axis_size("comp")
    blocks_dom = lax.axis_size("dom")
    rows_here = elevation_anomaly_profile.shape[0]
    width_row = elevation_anomaly_profile.shape[1]
    fields = airside_exchange.shape[1]
    source_blocks = regrid_matrix_partitions.shape[1]
    links = regrid_matrix_partitions.shape[2]
    block_cols = regrid_matrix_partitions.shape[3]
    all_rows = groups * blocks_dom * rows_here
    sources = airside_exchange[0].reshape(fields, source_blocks, block_cols)
    weights = regrid_matrix_partitions[0]
    partial_terms = jnp.einsum(
        "fsa,skab->skfb", sources, weights, preferred_element_type=jnp.float32
    )
    partial_terms = partial_terms.reshape(source_blocks * links, fields, width_row)
    targets = regrid_destination_latitude[0].reshape(-1)
    owner_group = targets // (blocks_dom * rows_here)
    owner_block = targets // rows_here % blocks_dom
    inside_row = targets % rows_here
    placed = owner_block * (groups * rows_here) + owner_group * rows_here + inside_row
    dense_terms = (
        jnp.zeros((all_rows, fields, width_row), jnp.float32).at[placed].add(partial_terms)
    )
    block_sums = lax.psum_scatter(dense_terms, "dom", scatter_dimension=0, tiled=True)
    ocean_flux = lax.psum_scatter(block_sums, "comp", scatter_dimension=0, tiled=True)
    heating = ocean_flux[:, 0, :]
    freshwater = ocean_flux[:, 1, :]
    stress_east = ocean_flux[:, 2, :]
    stress_north = ocean_flux[:, 3, :]
    wet = marine_indicator.astype(jnp.float32)
    face_east = wet * jnp.roll(wet, -1, axis=1)
    height = elevation_anomaly_profile
    flow_east = depth_integrated_volume_flow[0]
    flow_north = depth_integrated_volume_flow[1]
    advected_quantity = thermal_departure
    face_north = None
    for outer_step in range(NSTEP):
        for substep in range(NSUB):
            extended = with_halo(
                jnp.stack([height, flow_north, wet, stress_north]), ((("comp", "dom"), 1),), 1
            )
            edge_height = extended[0]
            edge_north = extended[1]
            edge_wet = extended[2]
            edge_stress = extended[3]
            face_north = edge_wet[:-1] * edge_wet[1:]
            new_east = face_east * (
                flow_east
                - wave_gain * (jnp.roll(height, -1, axis=1) - height)
                + stress_gain * stress_east
            )
            north_rows = face_north * (
                edge_north[:-1]
                - wave_gain * (edge_height[1:] - edge_height[:-1])
                + stress_gain * edge_stress[:-1]
            )
            height = (
                height
                - wave_gain
                * (new_east - jnp.roll(new_east, 1, axis=1) + north_rows[1:] - north_rows[:-1])
                + fresh_gain * freshwater * wet
            )
            flow_east = new_east
            flow_north = north_rows[1:]
        edge_tracer = with_halo(advected_quantity, ((("comp", "dom"), 1),), 1)
        along_east = face_east * (jnp.roll(advected_quantity, -1, axis=2) - advected_quantity)
        along_north = face_north * (edge_tracer[:, 1:] - edge_tracer[:, :-1])
        laplace = (
            along_east - jnp.roll(along_east, 1, axis=2) + along_north[:, 1:] - along_north[:, :-1]
        )
        explicit = advected_quantity + spread_gain * laplace
        explicit = explicit.at[0].add(heating_gain * heating * wet)
        advected_quantity = vertical_solve(explicit, diffusivity_coefficient)
    surface = jnp.stack([advected_quantity[0], height]).astype(jnp.bfloat16)
    shard_rows = lax.all_gather(surface, ("comp", "dom"), axis=1, tiled=True)
    count_rows = shard_rows.shape[1]
    selector = (targets[:, None] == jnp.arange(count_rows, dtype=jnp.int32)[None, :]).astype(
        jnp.bfloat16
    )
    picked = jnp.einsum("nr,frb->nfb", selector, shard_rows, preferred_element_type=jnp.float32)
    chosen = picked.astype(jnp.bfloat16).reshape(source_blocks, links, 2, width_row)
    returned = jnp.einsum("skfb,skab->fsa", chosen, weights, preferred_element_type=jnp.float32)
    return (
        advected_quantity,
        height,
        returned.reshape(1, 2, source_blocks * block_cols).astype(jnp.bfloat16),
    )


def solution(mesh):
    return jax.shard_map(
        shards,
        mesh=mesh,
        in_specs=(
            P("comp", None, "dom"),
            P("comp", "dom", None, None, None),
            P("comp", "dom", None),
            P(None, ("comp", "dom"), None),
            P(None, ("comp", "dom"), None),
            P(("comp", "dom"), None),
            P(None, ("comp", "dom"), None),
            P(("comp", "dom"), None),
        ),
        out_specs=(
            P(None, ("comp", "dom"), None),
            P(("comp", "dom"), None),
            P("comp", None, "dom"),
        ),
        check_vma=False,
    )
```

profile of v0, /device:TPU:1, one launch (start us, length us, event | category | flops | bytes accessed | tf_op | source)
XLA Modules:
  0.0 1095.4 jit_solution(4753517972119351040)
XLA Ops:
  11.7 3.6 scatter_fusion
  15.3 4.5 copy.18
  20.7 5.1 collective-permute-start.16
  25.9 7.0 collective-permute-start.17
  33.0 405.0 %reduce-scatter.3.cloned.1.call-done = f32[32,4,128]{2,0,1:T(8,128)} async-done(((f32[2048,4,128]{2,0,1:T(8,128)}), f32[32,4,128]{2,0,1:T(8,128)}) %reduce-scatter.3.cloned.1.call-update) | async-done | bytes 65552 | tf_op jit(solution)/shard_map/reduce_scatter | solution.py:91
  438.2 26.7 %reduce-scatter.5.cloned.1.call-done = f32[8,4,128]{2,0,1:T(8,128)} async-done(((f32[32,4,128]{2,0,1:T(8,128)}), f32[8,4,128]{2,0,1:T(8,128)}) %reduce-scatter.5.cloned.1.call-update) | async-done | bytes 16400 | tf_op jit(solution)/shard_map/reduce_scatter | solution.py:92
  465.7 7.5 collective-permute-start
  476.2 5.8 collective-permute-done.1
  484.9 2.4 collective-permute-start.3
  488.1 5.6 collective-permute-done.3
  495.9 2.4 collective-permute-start.5
  499.1 5.6 collective-permute-done.5
  506.9 2.4 collective-permute-start.7
  510.1 6.5 collective-permute-done.7
  518.8 2.4 collective-permute-start.9
  522.0 6.5 collective-permute-done.9
  530.6 2.4 collective-permute-start.11
  533.9 6.5 collective-permute-done.11
  542.5 2.4 collective-permute-start.13
  545.7 6.5 collective-permute-done.13
  554.4 2.4 collective-permute-start.15
  557.6 6.5 collective-permute-done.15
  572.1 8.0 collective-permute-start.35
  580.3 2.4 collective-permute-start.20
  584.8 7.6 collective-permute-done.21
  597.2 7.2 collective-permute-done.23
  609.1 7.2 collective-permute-done.25
  620.9 7.2 collective-permute-done.27
  632.8 7.2 collective-permute-done.29
  644.7 7.2 collective-permute-done.31
  656.6 7.6 collective-permute-done.33
  666.4 420.0 %all-gather.2.cloned.1.call-done = bf16[2,2048,128]{2,1,0:T(8,128)(2,1)} async-done(((bf16[2,8,128]{2,1,0:T(8,128)(2,1)}), bf16[2,2048,128]{2,1,0:T(8,128)(2,1)}) %all-gather.2.cloned.1.call-update) | async-done | bytes 1048592 | tf_op jit(solution)/shard_map/all_gather | solution.py:142
  (301 shorter events, 73.4 us)
Async XLA Ops:
  7.2 430.8 %reduce-scatter.3.cloned.1.call-start = ((), (), s32[]{:S(2)}) async-start(), calls=%async_computation.2 | async-start | bytes 4259840 | tf_op jit(solution)/shard_map/reduce_scatter | solution.py:91
  19.8 445.1 %reduce-scatter.5.cloned.1.call-start = ((), (), s32[]{:S(2)}) async-start(), calls=%async_computation.3 | async-start | bytes 81920 | tf_op jit(solution)/shard_map/reduce_scatter | solution.py:92
  20.7 543.4 %collective-permute-start.16 = (f32[32,1,128]{2,1,0:T(1,128)S(1)}, f32[32,1,128]{2,1,0:T(1,128)S(1)}, u32[]{:S(2)}, u32[]{:S(2)}) collective-permute-start(f32[32,1,128]{2,1,0:T(1,128)S(1)} %get-tuple-element.179), channel_id=1, source_target_pairs={{1,0},{2,1},{3,2},{4,3},{5,4},{6,5},{7,6},{8,7},{9,8},{10,9},{11,1... | collective-permute-start | bytes 49160 | tf_op jit(solution)/shard_map/ppermute | solution.py:25
  25.9 538.3 %collective-permute-start.17 = (f32[32,1,128]{2,1,0:T(1,128)S(1)}, f32[32,1,128]{2,1,0:T(1,128)S(1)}, u32[]{:S(2)}, u32[]{:S(2)}) collective-permute-start(f32[32,1,128]{2,1,0:T(1,128)S(1)} %get-tuple-element.178), channel_id=1, source_target_pairs={{0,1},{1,2},{2,3},{3,4},{4,5},{5,6},{6,7},{7,8},{8,9},{9,10},{10,1... | collective-permute-start | bytes 49160 | tf_op jit(solution)/shard_map/ppermute | solution.py:22
  438.0 648.3 %all-gather.2.cloned.1.call-start = ((), (), s32[]{:S(2)}) async-start(), calls=%async_computation.4 | async-start | bytes 1052672 | tf_op jit(solution)/shard_map/all_gather | solution.py:142
  465.7 10.5 collective-permute-start
  473.2 8.8 collective-permute-start.1
  482.9 5.2 collective-permute-start.2
  484.9 8.8 collective-permute-start.3
  493.9 5.2 collective-permute-start.4
  495.9 8.8 collective-permute-start.5
  504.9 5.2 collective-permute-start.6
  506.9 9.7 collective-permute-start.7
  516.8 5.2 collective-permute-start.8
  518.8 9.7 collective-permute-start.9
  528.7 5.2 collective-permute-start.10
  530.6 9.7 collective-permute-start.11
  540.6 5.2 collective-permute-start.12
  542.5 9.7 collective-permute-start.13
  552.4 5.2 collective-permute-start.14
  554.4 9.7 collective-permute-start.15
  565.5 14.6 %collective-permute-start.18 = (f32[4,1,128]{2,1,0:T(1,128)S(1)}, f32[4,1,128]{2,1,0:T(1,128)S(1)}, u32[]{:S(2)}, u32[]{:S(2)}) collective-permute-start(f32[4,1,128]{2,1,0:T(1,128)S(1)} %get-tuple-element.211), channel_id=1, source_target_pairs={{0,1},{1,2},{2,3},{3,4},{4,5},{5,6},{6,7},{7,8},{8,9},{9,10},{10,1... | collective-permute-start | bytes 6152 | tf_op jit(solution)/shard_map/ppermute | solution.py:22
  567.4 12.7 %collective-permute-start.19 = (f32[4,1,128]{2,1,0:T(1,128)S(1)}, f32[4,1,128]{2,1,0:T(1,128)S(1)}, u32[]{:S(2)}, u32[]{:S(2)}) collective-permute-start(f32[4,1,128]{2,1,0:T(1,128)S(1)} %get-tuple-element.210), channel_id=1, source_target_pairs={{1,0},{2,1},{3,2},{4,3},{5,4},{6,5},{7,6},{8,7},{9,8},{10,9},{11,1... | collective-permute-start | bytes 6152 | tf_op jit(solution)/shard_map/ppermute | solution.py:25
  570.2 94.7 %collective-permute-start.34 = (f32[32,1,128]{2,1,0:T(1,128)S(1)}, f32[32,1,128]{2,1,0:T(1,128)S(1)}, u32[]{:S(2)}, u32[]{:S(2)}) collective-permute-start(f32[32,1,128]{2,1,0:T(1,128)S(1)} %get-tuple-element.177), channel_id=1, source_target_pairs={{1,0},{2,1},{3,2},{4,3},{5,4},{6,5},{7,6},{8,7},{9,8},{10,9},{11,1... | collective-permute-start | bytes 49160 | tf_op jit(solution)/shard_map/ppermute | solution.py:25
  572.1 92.8 %collective-permute-start.35 = (f32[32,1,128]{2,1,0:T(1,128)S(1)}, f32[32,1,128]{2,1,0:T(1,128)S(1)}, u32[]{:S(2)}, u32[]{:S(2)}) collective-permute-start(f32[32,1,128]{2,1,0:T(1,128)S(1)} %get-tuple-element.176), channel_id=1, source_target_pairs={{0,1},{1,2},{2,3},{3,4},{4,5},{5,6},{6,7},{7,8},{8,9},{9,10},{10,1... | collective-permute-start | bytes 49160 | tf_op jit(solution)/shard_map/ppermute | solution.py:22
  582.8 9.7 collective-permute-start.21
  594.6 9.7 collective-permute-start.23
  606.5 9.7 collective-permute-start.25
  618.4 9.7 collective-permute-start.27
  630.3 9.7 collective-permute-start.29
  642.2 9.7 collective-permute-start.31
  654.1 10.1 collective-permute-start.33
  (15 other events, 1950.0 us)
Sparse Core Ops, SparseCore 0:
  20.0 417.9 reduce-scatter.2
  440.5 24.4 reduce-scatter.4
  666.1 420.2 all-gather.1
where the time goes:
time: 1100 us
  waiting for transfers between devices  952 us (87%)
  starting transfers between devices  96.4 us (9%)
  other arithmetic  15.4 us (1%)
  between operations  15 us (1%)
  local copies, waits for them, and re-layouts  12.8 us (1%)
    all_gather x1, waiting for transfers between devices, shards(): shard_rows = lax.all_gather(surface, ('comp', 'dom'), axis=1, tiled=True)  420 us
    reduce_scatter x1, waiting for transfers between devices, shards(): lax.psum_scatter(dense_terms, 'dom', scatter_dimension=0, tiled=True)  405 us
    ppermute x18, waiting for transfers between devices, with_halo(): lax.ppermute(lax.slice_in_dim(block, 0, width, axis=dim), axis, backward)  101 us
    ppermute x18, starting transfers between devices, with_halo(): lax.ppermute(lax.slice_in_dim(block, block.shape[dim] - width, None, axis...  52.2 us
    ppermute x18, starting transfers between devices, with_halo(): lax.ppermute(lax.slice_in_dim(block, 0, width, axis=dim), axis, backward)  44.1 us
    reduce_scatter x1, waiting for transfers between devices, shards(): lax.psum_scatter(block_sums, 'comp', scatter_dimension=0, tiled=True)  26.7 us
  transfers between devices with their start and end apart: 39, of which 18 were waited for; matrix products, arithmetic and copies ran while one was open for 1% of the time, Pallas kernels for 0%

commit v1 on v0

v1 whole, which is shorter than its diff:
```python
import numpy as np
import jax
import jax.numpy as jnp
from jax import lax
from jax.experimental import pallas as pl
from jax.experimental.pallas import tpu as pltpu
from jax.sharding import Mesh, PartitionSpec as P

NSTEP = 2
NSUB = 8

wave_gain = 0.35
stress_gain = 0.1
fresh_gain = 0.1
spread_gain = 0.2
heating_gain = 0.5

ALL = ("c", "y", "x", "h", "k")
PLANE = ("y", "x")
LINE = ("c", "h", "k")
ROWS = 8
LANES = 128
LEVELS = 32
TERMS = 32
GROUP = 16
SLAB = 64
BF = jnp.bfloat16
F32 = jnp.float32

vmem = pl.BlockSpec(memory_space=pltpu.VMEM)
smem = pl.BlockSpec(memory_space=pltpu.SMEM)


def call(kernel, outs, ins, scratch=(), name=None):
    return pl.pallas_call(
        kernel,
        out_shape=outs,
        in_specs=ins,
        out_specs=jax.tree.map(lambda _: vmem, outs),
        scratch_shapes=list(scratch),
        name=name,
    )


def shaped(shape, kind):
    return jax.ShapeDtypeStruct(shape, kind)


def east(v):
    return pltpu.roll(v, LANES - 1, axis=v.ndim - 1)


def west(v):
    return pltpu.roll(v, 1, axis=v.ndim - 1)


def north(v):
    return pltpu.roll(v, v.shape[0] - 1, axis=0)


def south(v):
    return pltpu.roll(v, 1, axis=0)


def pack_edges(tracer, mixing, height, flow, wet, up, down, around):
    own = jnp.concatenate([height[...], flow[0], flow[1], wet[...].astype(F32)], axis=0)
    zero = jnp.zeros((1, LANES), F32)
    around[...] = own
    up[0:32] = own
    up[32:64] = tracer[:, ROWS - 2, :]
    up[64:96] = tracer[:, ROWS - 1, :]
    up[96:127] = mixing[:, ROWS - 1, :]
    up[127:128] = zero
    down[0:32] = own
    down[32:64] = tracer[:, 0, :]
    down[64:96] = tracer[:, 1, :]
    down[96:127] = mixing[:, 0, :]
    down[127:128] = zero


def sort_terms(place, received, message, rows_named):
    spot = place[0]
    lines = lax.broadcasted_iota(jnp.int32, (4 * SLAB, LANES), 0)
    line_row = (lines >> 6) * 512 + spot * 32 - 16 + (lines & (SLAB - 1))
    sums = [None] * 4
    for q in range(4):
        coded = sum(received[4 * q + i, 128:144, :].astype(F32) for i in range(4))
        named = coded[0:1] * 64.0 + coded[1:2]
        rows_named[q : q + 1, :] = named
        picks = jnp.where(line_row == named.astype(jnp.int32), 1.0, 0.0).astype(BF)
        for f in range(4):
            some = received[4 * q : 4 * q + 4, f * 32 : f * 32 + 32, :].reshape(LANES, LANES)
            part = jnp.dot(picks, some, preferred_element_type=F32)
            sums[f] = part if sums[f] is None else sums[f] + part
    for c in range(4):
        for s in range(4):
            base = c * SLAB + 16 + s * ROWS
            pieces = [
                sums[f][base + o : base + o + ROWS] for f in (1, 2, 3) for o in (0, 8, 16, -16, -8)
            ] + [sums[0][base + o : base + o + ROWS] for o in (0, 8, -8)]
            message[c * 4 + s] = jnp.concatenate(pieces, axis=0).astype(BF)


def first_step(tracer, mixing, wet_own, before, after, base, reply, factors, halo, mix_halo, work):
    halo[...] = jnp.zeros_like(halo)
    mix_halo[...] = jnp.zeros_like(mix_halo)
    halo[pl.ds(0, LEVELS, stride=ROWS), :] = after[32:64]
    halo[pl.ds(1, LEVELS, stride=ROWS), :] = after[64:96]
    halo[pl.ds(6, LEVELS, stride=ROWS), :] = before[32:64]
    halo[pl.ds(7, LEVELS, stride=ROWS), :] = before[64:96]
    mix_halo[pl.ds(0, LEVELS, stride=ROWS), :] = after[96:128]
    mix_halo[pl.ds(7, LEVELS, stride=ROWS), :] = before[96:128]
    lower = lax.broadcasted_iota(jnp.int32, (ROWS, LANES), 0) < 4
    wet = jnp.concatenate(
        [wet_own[...].astype(F32), jnp.where(lower, after[24:32], before[24:32])], axis=0
    )
    face_e = wet * east(wet)
    face_n = wet * north(wet)
    face_w = west(face_e)
    face_s = south(face_n)

    def level(ref, own, l):
        return jnp.concatenate([own[l], ref[l * ROWS : (l + 1) * ROWS, :]], axis=0)

    zero = jnp.zeros((2 * ROWS, LANES), F32)
    over, ratio, solved, gone = zero, zero, zero, zero
    for l in range(LEVELS):
        t = level(halo, tracer, l)
        explicit = t + spread_gain * (
            face_e * (east(t) - t)
            - face_w * (t - west(t))
            + face_n * (north(t) - t)
            - face_s * (t - south(t))
        )
        under = level(mix_halo, mixing, l) if l < LEVELS - 1 else zero
        inverse = 1.0 / (1.0 + under + over * (1.0 - ratio))
        carry = over * inverse
        ratio = under * inverse
        solved = explicit * inverse + carry * solved
        gone = carry * gone if l else inverse
        factors[0, l] = inverse[0:ROWS]
        factors[1, l] = carry[0:ROWS]
        factors[2, l] = ratio[0:ROWS]
        work[l] = ratio
        base[l] = solved
        reply[l] = gone
        over = under
    for l in range(LEVELS - 2, -1, -1):
        solved = base[l] + work[l] * solved
        gone = reply[l] + work[l] * gone
        base[l] = solved
        reply[l] = gone


def ocean(
    flux, height, flow, wet_own, before2, before, after, after2, base, reply, factors,
    tracer_out, height_out, message, work,
):
    def ring(i, own):
        r = slice(i * ROWS, (i + 1) * ROWS)
        return jnp.concatenate([own, after[r], after2[r], before2[r], before[r]], axis=0)

    total = flux[0].astype(F32)
    for p in range(1, GROUP):
        total = total + flux[p].astype(F32)
    wet = ring(3, wet_own[...].astype(F32))
    rain = fresh_gain * total[0:40] * wet
    push_e = stress_gain * total[40:80]
    push_n = stress_gain * total[80:120]
    h = ring(0, height[...])
    flow_e = ring(1, flow[0])
    flow_n = ring(2, flow[1])
    face_e = wet * east(wet)
    face_n = wet * north(wet)
    face_w, flow_w, push_w = west(face_e), west(flow_e), west(push_e)
    face_s, flow_s, push_s = south(face_n), south(flow_n), south(push_n)
    for _ in range(NSTEP * NSUB):
        flow_e = face_e * (flow_e - wave_gain * (east(h) - h) + push_e)
        flow_w = face_w * (flow_w - wave_gain * (h - west(h)) + push_w)
        flow_n = face_n * (flow_n - wave_gain * (north(h) - h) + push_n)
        flow_s = face_s * (flow_s - wave_gain * (h - south(h)) + push_s)
        h = h - wave_gain * (flow_e - flow_w + flow_n - flow_s) + rain
    height_out[...] = h[0:ROWS]

    wet16 = jnp.concatenate([wet[0:ROWS], jnp.where(
        lax.broadcasted_iota(jnp.int32, (ROWS, LANES), 0) < 4, wet[8:16], wet[32:40])], axis=0)
    heat = jnp.concatenate([total[120:128], jnp.where(
        lax.broadcasted_iota(jnp.int32, (ROWS, LANES), 0) < 4, total[128:136], total[136:144])], axis=0)
    warm = heating_gain * heat * wet16
    fe, fw, fn, fs = face_e[0:ROWS], face_w[0:ROWS], face_n[0:ROWS], face_s[0:ROWS]
    solved = None
    for l in range(LEVELS):
        both = base[l] + reply[l] * warm
        t = both[0:ROWS]
        explicit = t + spread_gain * (
            fe * (east(t) - t)
            - fw * (t - west(t))
            + fn * (north(both)[0:ROWS] - t)
            - fs * (t - south(both)[0:ROWS])
        )
        if l == 0:
            explicit = explicit + warm[0:ROWS]
            solved = explicit * factors[0, l]
        else:
            solved = explicit * factors[0, l] + factors[1, l] * solved
        work[l] = solved
    tracer_out[LEVELS - 1] = solved
    for l in range(LEVELS - 2, -1, -1):
        solved = work[l] + factors[2, l] * solved
        tracer_out[l] = solved
    top = jnp.concatenate([solved, h[0:ROWS]], axis=0).astype(BF)
    for p in range(GROUP):
        message[p] = top


def answer(place, rows_named, received, message):
    spot = place[0]
    have = received[...].reshape(GROUP * 16, LANES)
    lines = lax.broadcasted_iota(jnp.int32, (GROUP * 16, LANES), 0)
    line_row = (lines >> 6) * 512 + spot * 32 + ((lines >> 4) & 3) * ROWS + (lines & 7)
    second = (lines & 8) != 0
    for q in range(4):
        named = rows_named[q : q + 1, :].astype(jnp.int32)
        same = line_row == named
        for f in range(2):
            picks = jnp.where(same & (second == bool(f)), 1.0, 0.0).astype(BF)
            out = lax.dot_general(
                picks, have, (((0,), (0,)), ((), ())), preferred_element_type=F32
            ).astype(BF)
            message[4 * q : 4 * q + 4, f * 32 : f * 32 + 32, :] = out.reshape(4, 32, LANES)


def collect(received, chosen):
    total = received[0].astype(F32)
    for p in range(1, GROUP):
        total = total + received[p].astype(F32)
    chosen[...] = total.astype(BF)


def shards(airside, matrices, latitude, tracer, mixing, height, flow, marine):
    sources = airside[0].reshape(4, 8, LANES)
    weights = matrices[0]
    targets = latitude[0].reshape(-1)
    spot = lax.axis_index(PLANE)
    place = spot.astype(jnp.int32).reshape(1)
    count = lax.axis_size(ALL)

    up, down, around = call(
        pack_edges,
        (shaped((128, LANES), F32), shaped((128, LANES), F32), shaped((32, LANES), F32)),
        [vmem] * 5,
        name="pack_edges",
    )(tracer, mixing, height, flow, marine)

    def moved(value, step):
        pairs = [(i, i + step) for i in range(count) if 0 <= i + step < count]
        return lax.ppermute(value, ALL, pairs)

    before = moved(up, 1)
    after = moved(down, -1)
    before2 = moved(around, 2)
    after2 = moved(around, -2)

    terms = jnp.einsum("fsa,skab->fskb", sources, weights, preferred_element_type=F32)
    terms = terms.astype(BF).reshape(128, LANES)
    lanes = jnp.arange(LANES, dtype=jnp.int32)
    spread = jnp.where(lanes // TERMS == spot % 4, jnp.tile(targets, 4), 0)
    coded = jnp.stack([spread // 64, spread % 64]).astype(BF)
    coded = jnp.concatenate([coded, jnp.zeros((14, LANES), BF)])
    first = jnp.concatenate([terms, coded])
    first = jnp.broadcast_to(first[None], (GROUP, 144, LANES))
    first = lax.all_to_all(first, PLANE, 0, 0, tiled=True)

    second, rows_named = call(
        sort_terms,
        (shaped((GROUP, 144, LANES), BF), shaped((ROWS, LANES), F32)),
        [smem, vmem],
        name="sort_terms",
    )(place, first)
    second = lax.all_to_all(second, LINE, 0, 0, tiled=True)

    base, reply, factors = call(
        first_step,
        (
            shaped((LEVELS, 2 * ROWS, LANES), F32),
            shaped((LEVELS, 2 * ROWS, LANES), F32),
            shaped((3, LEVELS, ROWS, LANES), F32),
        ),
        [vmem] * 5,
        [
            pltpu.VMEM((LEVELS * ROWS, LANES), F32),
            pltpu.VMEM((LEVELS * ROWS, LANES), F32),
            pltpu.VMEM((LEVELS, 2 * ROWS, LANES), F32),
        ],
        name="first_step",
    )(tracer, mixing, marine, before, after)

    tracer_new, height_new, third = call(
        ocean,
        (
            shaped((LEVELS, ROWS, LANES), F32),
            shaped((ROWS, LANES), F32),
            shaped((GROUP, 16, LANES), BF),
        ),
        [vmem] * 11,
        [pltpu.VMEM((LEVELS, ROWS, LANES), F32)],
        name="ocean",
    )(second, height, flow, marine, before2, before, after, after2, base, reply, factors)
    third = lax.all_to_all(third, LINE, 0, 0, tiled=True)

    fourth = call(
        answer, shaped((GROUP, 64, LANES), BF), [smem, vmem, vmem], name="answer"
    )(place, rows_named, third)
    fourth = lax.all_to_all(fourth, PLANE, 0, 0, tiled=True)

    chosen = call(collect, shaped((64, LANES), BF), [vmem], name="collect")(fourth)
    returned = jnp.einsum(
        "fskb,skab->fsa", chosen.reshape(2, 8, 4, LANES), weights, preferred_element_type=F32
    )
    return tracer_new, height_new, returned.reshape(1, 2, 8 * LANES).astype(BF)


def solution(mesh):
    split = Mesh(mesh.devices.reshape(4, 4, 4, 2, 2), ALL)
    dom = ("y", "x", "h", "k")
    return jax.shard_map(
        shards,
        mesh=split,
        in_specs=(
            P("c", None, dom),
            P("c", dom, None, None, None),
            P("c", dom, None),
            P(None, ALL, None),
            P(None, ALL, None),
            P(ALL, None),
            P(None, ALL, None),
            P(ALL, None),
        ),
        out_specs=(P(None, ALL, None), P(ALL, None), P("c", None, dom)),
        check_vma=False,
    )
```

time: 1100 us -> 101 us (0.09)
  waiting for transfers between devices: 952 us -> 1.05 us
  starting transfers between devices: 96.4 us -> 28.9 us
  blocking collectives: 0 us -> 50.4 us
  other arithmetic: 15.4 us -> 0.12 us
  between operations: 15 us -> 0.8 us
  Pallas kernels: 0 us -> 13.4 us
    reduce_scatter x2 -> x0, waiting for transfers between devices: 432 us -> none  [the longest x1 405 us: shards(): lax.psum_scatter(dense_terms, 'dom', scatter_dimension=0, tiled=True)]
    all_gather x1 -> x0, waiting for transfers between devices: 420 us -> none  [shards(): shard_rows = lax.all_gather(surface, ('comp', 'dom'), axis=1, tiled=True)]
    ppermute x36 -> x4, waiting for transfers between devices: 101 us -> 1.05 us  [moved(): return lax.ppermute(value, ALL, pairs)]
    ppermute x36 -> x4, starting transfers between devices: 96.3 us -> 18.5 us  [moved(): return lax.ppermute(value, ALL, pairs)]
    all_to_all x0 -> x3, blocking collectives: none -> 50.4 us  [the longest x1 19 us: shards(): third = lax.all_to_all(third, LINE, 0, 0, tiled=True)]
    pallas_call x0 -> x6, Pallas kernels: none -> 13.4 us  [the longest x1 3.44 us: shards(): call(ocean, (shaped((LEVELS, ROWS, LANES), F32), shaped((ROWS, LANES), F3...]
  transfers between devices with their start and end apart: 39 -> 5, of which waited for: 18 -> 1; matrix products, arithmetic and copies ran while one was open for 1% -> 0% of each run, Pallas kernels for 0% -> 4%
where the time goes in v1:
time: 101 us; the launch traced here: 99.9 us
  blocking collectives  50.4 us (50%)
  starting transfers between devices  28.9 us (29%)
  Pallas kernels  13.4 us (13%)
  local copies, waits for them, and re-layouts  3.28 us (3%)
  matrix products  1.94 us (2%)
  waiting for transfers between devices  1.05 us (1%)
    all_to_all x1, blocking collectives, shards(): third = lax.all_to_all(third, LINE, 0, 0, tiled=True)  19 us
    all_to_all x1, blocking collectives, shards(): first = lax.all_to_all(first, PLANE, 0, 0, tiled=True)  18.8 us
    ppermute x4, starting transfers between devices, moved(): return lax.ppermute(value, ALL, pairs)  18.5 us
    all_to_all x1, blocking collectives, shards(): fourth = lax.all_to_all(fourth, PLANE, 0, 0, tiled=True)  12.6 us
    all_to_all x1, starting transfers between devices, shards(): second = lax.all_to_all(second, LINE, 0, 0, tiled=True)  10.4 us
    pallas_call x1, Pallas kernels, shards(): call(ocean, (shaped((LEVELS, ROWS, LANES), F32), shaped((ROWS, LANES), F3...  3.44 us
    unnamed x17, local copies, waits for them, and re-layouts  2.93 us
    pallas_call x1, Pallas kernels, shards(): call(first_step, (shaped((LEVELS, 2 * ROWS, LANES), F32), shaped((LEVELS,...  2.46 us
  transfers between devices with their start and end apart: 5, of which 1 were waited for; matrix products, arithmetic and copies ran while one was open for 0% of the time, Pallas kernels for 4%

profile of v1, /device:TPU:1, one launch (start us, length us, event | category | flops | bytes accessed | tf_op | source)
XLA Modules:
  0.0 99.9 jit_solution(6805791007079853959)
XLA Ops:
  0.6 0.0 copy-start
  0.7 0.8 copy-done.7
  1.4 0.1 copy.16
  1.5 0.1 tile.10
  1.6 0.1 tile.12
  1.7 0.2 copy-done
  1.9 0.5 copy-done.6
  2.4 0.2 fusion
  2.6 0.1 pad.3.clone
  2.7 0.1 maximum_maximum_fusion
  2.8 0.1 broadcast_in_dim.12
  2.9 18.8 %all_to_all.20.received = bf16[16,144,128]{2,1,0:T(8,128)(2,1)} all-to-all(bf16[16,144,128]{2,1,0:T(8,128)(2,1)S(1)} %broadcast_in_dim.12), channel_id=1, replica_groups=mesh['c'=4,'y'=4,'x'=4,'h'=2,'k'=2] {'y','x'}, dimensions={0} | all-to-all | bytes 1179648 | tf_op jit(solution)/shard_map/all_to_all | solution.py:272
  21.7 2.3 %sort_terms.1 = (bf16[16,144,128]{2,1,0:T(8,128)(2,1)}, f32[8,128]{1,0:T(8,128)}) custom-call(s32[1]{0:T(128)} %bitcast.place, bf16[16,144,128]{2,1,0:T(8,128)(2,1)} %all_to_all.20.received), custom_call_target="tpu_custom_call" | custom-call | tf_op jit(solution)/shard_map/sort_terms/pallas_call | solution.py:274
  24.0 10.4 %all-to-all-start.1 = ((bf16[16,144,128]{2,1,0:T(8,128)(2,1)}), bf16[16,144,128]{2,1,0:T(8,128)(2,1)S(1)}, u32[]{:S(2)}, u32[]{:S(2)}) async-start(bf16[16,144,128]{2,1,0:T(8,128)(2,1)} %get-tuple-element.14), calls=%async_computation.1 | async-start | bytes 1179648 | tf_op jit(solution)/shard_map/all_to_all | solution.py:280
  34.4 1.7 %pack_edges.1 = (f32[128,128]{1,0:T(8,128)}, f32[128,128]{1,0:T(8,128)}, f32[32,128]{1,0:T(8,128)}) custom-call(f32[32,8,128]{2,1,0:T(8,128)} %tracer.3, f32[31,8,128]{2,1,0:T(8,128)} %mixing.3, f32[8,128]{1,0:T(8,128)} %height.3, f32[2,8,128]{2,1,0:T(8,128)} %flow.3, s32[8,128]{1,0:T(8,128)} %wet_own.3), custom_call_target="tpu_custom_call" | custom-call | tf_op jit(solution)/shard_map/pack_edges/pallas_call | solution.py:248
  36.1 7.4 %collective-permute-start.1 = (f32[128,128]{1,0:T(8,128)}, f32[128,128]{1,0:T(8,128)S(1)}, u32[]{:S(2)}, u32[]{:S(2)}) collective-permute-start(f32[128,128]{1,0:T(8,128)} %get-tuple-element.16), channel_id=1, source_target_pairs={{0,1},{1,2},{2,3},{3,4},{4,5},{5,6},{6,7},{7,8},{8,9},{9,10},{10,1... | collective-permute-start | bytes 196616 | tf_op jit(solution)/shard_map/ppermute | solution.py:257
  43.5 1.9 %collective-permute-start.2 = (f32[128,128]{1,0:T(8,128)}, f32[128,128]{1,0:T(8,128)S(1)}, u32[]{:S(2)}, u32[]{:S(2)}) collective-permute-start(f32[128,128]{1,0:T(8,128)} %get-tuple-element.17), channel_id=1, source_target_pairs={{1,0},{2,1},{3,2},{4,3},{5,4},{6,5},{7,6},{8,7},{9,8},{10,9},{11,1... | collective-permute-start | bytes 196616 | tf_op jit(solution)/shard_map/ppermute | solution.py:257
  45.5 1.3 %collective-permute-start.3 = (f32[32,128]{1,0:T(8,128)}, f32[32,128]{1,0:T(8,128)S(1)}, u32[]{:S(2)}, u32[]{:S(2)}) collective-permute-start(f32[32,128]{1,0:T(8,128)} %get-tuple-element.15), channel_id=1, source_target_pairs={{2,0},{3,1},{4,2},{5,3},{6,4},{7,5},{8,6},{9,7},{10,8},{11,9},{12,... | collective-permute-start | bytes 49160 | tf_op jit(solution)/shard_map/ppermute | solution.py:257
  46.8 7.9 %collective-permute-start = (f32[32,128]{1,0:T(8,128)}, f32[32,128]{1,0:T(8,128)S(1)}, u32[]{:S(2)}, u32[]{:S(2)}) collective-permute-start(f32[32,128]{1,0:T(8,128)} %get-tuple-element.15), channel_id=1, source_target_pairs={{0,2},{1,3},{2,4},{3,5},{4,6},{5,7},{6,8},{7,9},{8,10},{9,11},{10,... | collective-permute-start | bytes 49160 | tf_op jit(solution)/shard_map/ppermute | solution.py:257
  54.7 1.0 %collective-permute-done.2.after = f32[128,128]{1,0:T(8,128)S(1)} collective-permute-done((f32[128,128]{1,0:T(8,128)}, f32[128,128]{1,0:T(8,128)S(1)}, u32[]{:S(2)}, u32[]{:S(2)}) %collective-permute-start.2) | collective-permute-done | bytes 65568 | tf_op jit(solution)/shard_map/ppermute | solution.py:257
  55.7 0.6 copy-done.3
  56.3 2.5 %first_step.1 = (f32[32,16,128]{2,1,0:T(8,128)}, f32[32,16,128]{2,1,0:T(8,128)}, f32[3,32,8,128]{3,2,1,0:T(8,128)}) custom-call(f32[32,8,128]{2,1,0:T(8,128)} %tracer.3, f32[31,8,128]{2,1,0:T(8,128)} %mixing.3, s32[8,128]{1,0:T(8,128)} %wet_own.3, f32[128,128]{1,0:T(8,128)} %copy-done.2, f32[128,128]{1,0:T(8,128)} %copy-done.3), custom_call_target="tpu_custom_call" | custom-call | tf_op jit(solution)/shard_map/first_step/pallas_call | solution.py:282
  58.8 0.0 collective-permute-done.3.after2
  58.9 0.6 copy-done.4
  59.4 0.0 copy-done.5
  59.4 0.2 copy-done.1
  59.7 3.4 %ocean.1 = (f32[32,8,128]{2,1,0:T(8,128)}, f32[8,128]{1,0:T(8,128)}, bf16[16,16,128]{2,1,0:T(8,128)(2,1)}) custom-call(bf16[16,144,128]{2,1,0:T(8,128)(2,1)} %copy-done.1, f32[8,128]{1,0:T(8,128)} %height.3, f32[2,8,128]{2,1,0:T(8,128)} %flow.3, s32[8,128]{1,0:T(8,128)} %wet_own.3, f32[32,128]{1,0:T(8,128)} %copy-done.5, f32[128,128]{1,0:T(8,128)} %copy-done.2, ...), custom_call_target="tpu_custom_call" | custom-call | tf_op jit(solution)/shard_map/ocean/pallas_call | solution.py:298
  63.1 19.0 %all_to_all.21.received = bf16[16,16,128]{2,1,0:T(8,128)(2,1)} all-to-all(bf16[16,16,128]{2,1,0:T(8,128)(2,1)} %get-tuple-element.24), channel_id=1, replica_groups=mesh['c'=4,'y'=4,'x'=4,'h'=2,'k'=2] {'c','h','k'}, dimensions={0} | all-to-all | bytes 131072 | tf_op jit(solution)/shard_map/all_to_all | solution.py:309
  82.1 1.9 %answer.1 = bf16[16,64,128]{2,1,0:T(8,128)(2,1)} custom-call(s32[1]{0:T(128)} %bitcast.place, f32[8,128]{1,0:T(8,128)} %get-tuple-element.23.rows_named, bf16[16,16,128]{2,1,0:T(8,128)(2,1)} %all_to_all.21.received), custom_call_target="tpu_custom_call" | custom-call | tf_op jit(solution)/shard_map/answer/pallas_call | solution.py:311
  84.0 12.6 %all_to_all.22.received = bf16[16,64,128]{2,1,0:T(8,128)(2,1)} all-to-all(bf16[16,64,128]{2,1,0:T(8,128)(2,1)} %answer.1), channel_id=1, replica_groups=mesh['c'=4,'y'=4,'x'=4,'h'=2,'k'=2] {'y','x'}, dimensions={0} | all-to-all | bytes 524288 | tf_op jit(solution)/shard_map/all_to_all | solution.py:314
  96.7 1.6 %collect.1 = bf16[64,128]{1,0:T(8,128)(2,1)} custom-call(bf16[16,64,128]{2,1,0:T(8,128)(2,1)} %all_to_all.22.received), custom_call_target="tpu_custom_call" | custom-call | tf_op jit(solution)/shard_map/collect/pallas_call | solution.py:316
  98.2 1.7 %fusion.2 = bf16[1,2,1024]{2,1,0:T(2,128)(2,1)} fusion(bf16[1,8,4,128,128]{4,3,2,1,0:T(8,128)(2,1)S(1)} %copy-done, bf16[2,8,4,128]{3,2,1,0:T(4,128)(2,1)} %bitcast.29), kind=kOutput, calls=%fused_computation.4 | convolution fusion | flops 2099200 | bytes 1069056 | tf_op jit(solution)/shard_map/fskb,skab->fsa/dot_general | solution.py:317
  (16 shorter events, 0.1 us)
Async XLA Ops:
  0.6 1.2 %copy-start = (bf16[1,8,4,128,128]{4,3,2,1,0:T(8,128)(2,1)S(1)}, bf16[1,8,4,128,128]{4,3,2,1,0:T(8,128)(2,1)}, u32[]{:S(2)}) copy-start(bf16[1,8,4,128,128]{4,3,2,1,0:T(8,128)(2,1)} %param.9) | copy-start | bytes 3145732
  0.7 0.8 copy-start.7
  1.6 0.8 copy-start.6
  24.0 34.8 %all-to-all-start.1 = ((bf16[16,144,128]{2,1,0:T(8,128)(2,1)}), bf16[16,144,128]{2,1,0:T(8,128)(2,1)S(1)}, u32[]{:S(2)}, u32[]{:S(2)}) async-start(bf16[16,144,128]{2,1,0:T(8,128)(2,1)} %get-tuple-element.14), calls=%async_computation.1 | async-start | bytes 1179648 | tf_op jit(solution)/shard_map/all_to_all | solution.py:280
  36.1 18.6 %collective-permute-start.1 = (f32[128,128]{1,0:T(8,128)}, f32[128,128]{1,0:T(8,128)S(1)}, u32[]{:S(2)}, u32[]{:S(2)}) collective-permute-start(f32[128,128]{1,0:T(8,128)} %get-tuple-element.16), channel_id=1, source_target_pairs={{0,1},{1,2},{2,3},{3,4},{4,5},{5,6},{6,7},{7,8},{8,9},{9,10},{10,1... | collective-permute-start | bytes 196616 | tf_op jit(solution)/shard_map/ppermute | solution.py:257
  43.5 12.2 %collective-permute-start.2 = (f32[128,128]{1,0:T(8,128)}, f32[128,128]{1,0:T(8,128)S(1)}, u32[]{:S(2)}, u32[]{:S(2)}) collective-permute-start(f32[128,128]{1,0:T(8,128)} %get-tuple-element.17), channel_id=1, source_target_pairs={{1,0},{2,1},{3,2},{4,3},{5,4},{6,5},{7,6},{8,7},{9,8},{10,9},{11,1... | collective-permute-start | bytes 196616 | tf_op jit(solution)/shard_map/ppermute | solution.py:257
  45.5 13.4 %collective-permute-start.3 = (f32[32,128]{1,0:T(8,128)}, f32[32,128]{1,0:T(8,128)S(1)}, u32[]{:S(2)}, u32[]{:S(2)}) collective-permute-start(f32[32,128]{1,0:T(8,128)} %get-tuple-element.15), channel_id=1, source_target_pairs={{2,0},{3,1},{4,2},{5,3},{6,4},{7,5},{8,6},{9,7},{10,8},{11,9},{12,... | collective-permute-start | bytes 49160 | tf_op jit(solution)/shard_map/ppermute | solution.py:257
  46.8 12.1 %collective-permute-start = (f32[32,128]{1,0:T(8,128)}, f32[32,128]{1,0:T(8,128)S(1)}, u32[]{:S(2)}, u32[]{:S(2)}) collective-permute-start(f32[32,128]{1,0:T(8,128)} %get-tuple-element.15), channel_id=1, source_target_pairs={{0,2},{1,3},{2,4},{3,5},{4,6},{5,7},{6,8},{7,9},{8,10},{9,11},{10,... | collective-permute-start | bytes 49160 | tf_op jit(solution)/shard_map/ppermute | solution.py:257
  54.7 1.1 %copy-start.2 = (f32[128,128]{1,0:T(8,128)}, f32[128,128]{1,0:T(8,128)S(1)}, u32[]{:S(2)}) copy-start(f32[128,128]{1,0:T(8,128)S(1)} %collective-permute-done.1.before) | copy-start | bytes 196612
  55.7 0.6 copy-start.3
  58.8 0.6 copy-start.4
  58.8 0.6 copy-start.5
  58.8 0.8 copy-start.1

commit v2 on v1

--- a/solution.py
+++ b/solution.py
@@ -46,6 +46,14 @@
     return jax.ShapeDtypeStruct(shape, kind)
 
 
+def inside(shape, kind):
+    return pltpu.VMEM(shape, kind)
+
+
+def near(value):
+    return pltpu.with_memory_space_constraint(value, pltpu.VMEM)
+
+
 def east(v):
     return pltpu.roll(v, LANES - 1, axis=v.ndim - 1)
 
@@ -62,27 +70,78 @@
     return pltpu.roll(v, 1, axis=0)
 
 
-def pack_edges(tracer, mixing, height, flow, wet, up, down, around):
-    own = jnp.concatenate([height[...], flow[0], flow[1], wet[...].astype(F32)], axis=0)
+def pack_edges(quarter, tracer, mixing, height, flow, wet, edges, leaving):
+    own = jnp.concatenate([height[...], flow[0], flow[1], wet[...].astype(F32)], axis=0).astype(BF)
     zero = jnp.zeros((1, LANES), F32)
-    around[...] = own
-    up[0:32] = own
-    up[32:64] = tracer[:, ROWS - 2, :]
-    up[64:96] = tracer[:, ROWS - 1, :]
-    up[96:127] = mixing[:, ROWS - 1, :]
-    up[127:128] = zero
-    down[0:32] = own
-    down[32:64] = tracer[:, 0, :]
-    down[64:96] = tracer[:, 1, :]
-    down[96:127] = mixing[:, 0, :]
-    down[127:128] = zero
-
-
-def sort_terms(place, received, message, rows_named):
+    for i, (first, second, rim) in enumerate(((6, 7, 7), (0, 1, 0))):
+        edges[i, 0:32] = own
+        edges[i, 32:64] = tracer[:, first, :].astype(BF)
+        edges[i, 64:96] = tracer[:, second, :].astype(BF)
+        edges[i, 96:128] = jnp.concatenate([mixing[:, rim, :], zero], axis=0).astype(BF)
+    leaving[...] = edges[jnp.where(quarter[0] >= 2, 0, 1)]
+
+
+def pair_edges(quarter, edges, arrived, _after, message):
+    mine = quarter[0]
+    message[0:32] = edges[0, 0:32]
+    message[32:64] = arrived[0:32]
+    message[64:160] = edges[mine & 1, 32:128]
+
+    @pl.when(mine == 1)
+    def _():
+        message[160:256] = edges[0, 32:128]
+
+    @pl.when(mine == 2)
+    def _():
+        message[160:256] = edges[1, 32:128]
+
+    @pl.when((mine == 0) | (mine == 3))
+    def _():
+        message[160:256] = arrived[32:128]
+
+
+def far_edges(quarter, edges, arrived, partner, message):
+    core = quarter[0] & 1
+    own = pl.multiple_of(32 * core, 32)
+    other = pl.multiple_of(32 - 32 * core, 32)
+    message[pl.ds(own, 32)] = edges[0, 0:32]
+    message[pl.ds(other, 32)] = partner[0:32]
+    message[pl.ds(64 + own, 32)] = arrived[0:32]
+    message[pl.ds(64 + other, 32)] = partner[32:64]
+    message[128:224] = partner[160:256]
+
+
+def edge_sides(mine, partner, far):
+    first = (mine & 1) == 0
+    near_edge = partner[64:160].astype(F32)
+    far_edge = far[128:224].astype(F32)
+    return jnp.where(first, far_edge, near_edge), jnp.where(first, near_edge, far_edge)
+
+
+def strips(mine, partner, far):
+    first = (mine & 1) == 0
+    shift = 32 * (mine & 1)
+    prev = jnp.where(mine < 2, 64, 0)
+    follow = 64 - prev
+
+    def part(start):
+        return far[pl.ds(pl.multiple_of(start, 32), 32)].astype(F32)
+
+    beside = partner[0:32].astype(F32)
+    before2 = part(prev + shift)
+    before = jnp.where(first, part(prev + 32), beside)
+    after = jnp.where(first, beside, part(follow))
+    after2 = part(follow + shift)
+    return before2, before, after, after2
+
+
+def sort_terms(place, received, _arrived, message, rows_named):
     spot = place[0]
     lines = lax.broadcasted_iota(jnp.int32, (4 * SLAB, LANES), 0)
     line_row = (lines >> 6) * 512 + spot * 32 - 16 + (lines & (SLAB - 1))
     sums = [None] * 4
+    tile = lax.broadcasted_iota(jnp.int32, (ROWS, LANES), 0)
+    head, last = tile == 0, tile == ROWS - 1
     for q in range(4):
         coded = sum(received[4 * q + i, 128:144, :].astype(F32) for i in range(4))
         named = coded[0:1] * 64.0 + coded[1:2]
@@ -95,24 +154,34 @@
     for c in range(4):
         for s in range(4):
             base = c * SLAB + 16 + s * ROWS
-            pieces = [
-                sums[f][base + o : base + o + ROWS] for f in (1, 2, 3) for o in (0, 8, 16, -16, -8)
-            ] + [sums[0][base + o : base + o + ROWS] for o in (0, 8, -8)]
+            pieces = []
+            for f in (1, 2, 3):
+                for o in (0, 8, 16, -16, -8):
+                    piece = sums[f][base + o : base + o + ROWS]
+                    if f == 1 and o == 16:
+                        piece = jnp.where(last, north(sums[0][base + 8 : base + 16]), piece)
+                    if f == 1 and o == -16:
+                        piece = jnp.where(head, south(sums[0][base - 8 : base]), piece)
+                    pieces.append(piece)
+            pieces.append(sums[0][base : base + ROWS])
             message[c * 4 + s] = jnp.concatenate(pieces, axis=0).astype(BF)
 
 
-def first_step(tracer, mixing, wet_own, before, after, base, reply, factors, halo, mix_halo, work):
+def first_step(quarter, tracer, mixing, wet_own, partner, far, base, reply, factors, halo, mix_halo, work):
+    mine = quarter[0]
+    before, after = edge_sides(mine, partner, far)
+    _, wet_before, wet_after, _ = (strip[24:32] for strip in strips(mine, partner, far))
     halo[...] = jnp.zeros_like(halo)
     mix_halo[...] = jnp.zeros_like(mix_halo)
-    halo[pl.ds(0, LEVELS, stride=ROWS), :] = after[32:64]
-    halo[pl.ds(1, LEVELS, stride=ROWS), :] = after[64:96]
-    halo[pl.ds(6, LEVELS, stride=ROWS), :] = before[32:64]
-    halo[pl.ds(7, LEVELS, stride=ROWS), :] = before[64:96]
-    mix_halo[pl.ds(0, LEVELS, stride=ROWS), :] = after[96:128]
-    mix_halo[pl.ds(7, LEVELS, stride=ROWS), :] = before[96:128]
+    halo[pl.ds(0, LEVELS, stride=ROWS), :] = after[0:32]
+    halo[pl.ds(1, LEVELS, stride=ROWS), :] = after[32:64]
+    halo[pl.ds(6, LEVELS, stride=ROWS), :] = before[0:32]
+    halo[pl.ds(7, LEVELS, stride=ROWS), :] = before[32:64]
+    mix_halo[pl.ds(0, LEVELS, stride=ROWS), :] = after[64:96]
+    mix_halo[pl.ds(7, LEVELS, stride=ROWS), :] = before[64:96]
     lower = lax.broadcasted_iota(jnp.int32, (ROWS, LANES), 0) < 4
     wet = jnp.concatenate(
-        [wet_own[...].astype(F32), jnp.where(lower, after[24:32], before[24:32])], axis=0
+        [wet_own[...].astype(F32), jnp.where(lower, wet_after, wet_before)], axis=0
     )
     face_e = wet * east(wet)
     face_n = wet * north(wet)
@@ -153,9 +222,12 @@
 
 
 def ocean(
-    flux, height, flow, wet_own, before2, before, after, after2, base, reply, factors,
+    quarter, flux, height, flow, wet_own, partner, far, base, reply, factors,
     tracer_out, height_out, message, work,
 ):
+    mine = quarter[0]
+    before2, before, after, after2 = strips(mine, partner, far)
+
     def ring(i, own):
         r = slice(i * ROWS, (i + 1) * ROWS)
         return jnp.concatenate([own, after[r], after2[r], before2[r], before[r]], axis=0)
@@ -184,8 +256,10 @@
 
     wet16 = jnp.concatenate([wet[0:ROWS], jnp.where(
         lax.broadcasted_iota(jnp.int32, (ROWS, LANES), 0) < 4, wet[8:16], wet[32:40])], axis=0)
-    heat = jnp.concatenate([total[120:128], jnp.where(
-        lax.broadcasted_iota(jnp.int32, (ROWS, LANES), 0) < 4, total[128:136], total[136:144])], axis=0)
+    tile = lax.broadcasted_iota(jnp.int32, (ROWS, LANES), 0)
+    after_heat = jnp.where(tile == 0, south(total[16:24]), 0.0)
+    before_heat = jnp.where(tile == ROWS - 1, north(total[24:32]), 0.0)
+    heat = jnp.concatenate([total[120:128], after_heat + before_heat], axis=0)
     warm = heating_gain * heat * wet16
     fe, fw, fn, fs = face_e[0:ROWS], face_w[0:ROWS], face_n[0:ROWS], face_s[0:ROWS]
     solved = None
@@ -245,21 +319,20 @@
     place = spot.astype(jnp.int32).reshape(1)
     count = lax.axis_size(ALL)
 
-    up, down, around = call(
+    quarter = lax.axis_index(("h", "k")).astype(jnp.int32).reshape(1)
+    edges, leaving = call(
         pack_edges,
-        (shaped((128, LANES), F32), shaped((128, LANES), F32), shaped((32, LANES), F32)),
-        [vmem] * 5,
+        (inside((2, 128, LANES), BF), inside((128, LANES), BF)),
+        [smem] + [vmem] * 5,
         name="pack_edges",
-    )(tracer, mixing, height, flow, marine)
-
-    def moved(value, step):
-        pairs = [(i, i + step) for i in range(count) if 0 <= i + step < count]
-        return lax.ppermute(value, ALL, pairs)
-
-    before = moved(up, 1)
-    after = moved(down, -1)
-    before2 = moved(around, 2)
-    after2 = moved(around, -2)
+    )(quarter, tracer, mixing, height, flow, marine)
+    pairs = []
+    for i in range(count):
+        j = i + 4 if i % 4 >= 2 else i - 4
+        if 0 <= j < count:
+            pairs.append((i, j))
+    arrived = near(lax.ppermute(leaving, ALL, pairs))
+    edges = near(edges)
 
     terms = jnp.einsum("fsa,skab->fskb", sources, weights, preferred_element_type=F32)
     terms = terms.astype(BF).reshape(128, LANES)
@@ -269,51 +342,61 @@
     coded = jnp.concatenate([coded, jnp.zeros((14, LANES), BF)])
     first = jnp.concatenate([terms, coded])
     first = jnp.broadcast_to(first[None], (GROUP, 144, LANES))
-    first = lax.all_to_all(first, PLANE, 0, 0, tiled=True)
+    first = near(lax.all_to_all(first, PLANE, 0, 0, tiled=True))
 
     second, rows_named = call(
         sort_terms,
-        (shaped((GROUP, 144, LANES), BF), shaped((ROWS, LANES), F32)),
-        [smem, vmem],
+        (inside((GROUP, 128, LANES), BF), inside((ROWS, LANES), F32)),
+        [smem, vmem, vmem],
         name="sort_terms",
-    )(place, first)
-    second = lax.all_to_all(second, LINE, 0, 0, tiled=True)
+    )(place, first, arrived)
+    rows_named = near(rows_named)
+    second = near(lax.all_to_all(second, LINE, 0, 0, tiled=True))
+
+    partner = call(
+        pair_edges, inside((256, LANES), BF), [smem, vmem, vmem, vmem], name="pair_edges"
+    )(quarter, edges, arrived, rows_named)
+    partner = near(lax.ppermute(partner, ALL, [(i, i ^ 1) for i in range(count)]))
+    far = call(
+        far_edges, inside((224, LANES), BF), [smem, vmem, vmem, vmem], name="far_edges"
+    )(quarter, edges, arrived, partner)
+    far = near(lax.ppermute(far, ALL, [(i, i ^ 2) for i in range(count)]))
 
     base, reply, factors = call(
         first_step,
         (
-            shaped((LEVELS, 2 * ROWS, LANES), F32),
-            shaped((LEVELS, 2 * ROWS, LANES), F32),
-            shaped((3, LEVELS, ROWS, LANES), F32),
+            inside((LEVELS, 2 * ROWS, LANES), F32),
+            inside((LEVELS, 2 * ROWS, LANES), F32),
+            inside((3, LEVELS, ROWS, LANES), F32),
         ),
-        [vmem] * 5,
+        [smem] + [vmem] * 5,
         [
             pltpu.VMEM((LEVELS * ROWS, LANES), F32),
             pltpu.VMEM((LEVELS * ROWS, LANES), F32),
             pltpu.VMEM((LEVELS, 2 * ROWS, LANES), F32),
         ],
         name="first_step",
-    )(tracer, mixing, marine, before, after)
+    )(quarter, tracer, mixing, marine, partner, far)
 
     tracer_new, height_new, third = call(
         ocean,
         (
             shaped((LEVELS, ROWS, LANES), F32),
             shaped((ROWS, LANES), F32),
-            shaped((GROUP, 16, LANES), BF),
+            inside((GROUP, 16, LANES), BF),
         ),
-        [vmem] * 11,
+        [smem] + [vmem] * 9,
         [pltpu.VMEM((LEVELS, ROWS, LANES), F32)],
         name="ocean",
-    )(second, height, flow, marine, before2, before, after, after2, base, reply, factors)
-    third = lax.all_to_all(third, LINE, 0, 0, tiled=True)
+    )(quarter, second, height, flow, marine, partner, far, near(base), near(reply), near(factors))
+    third = near(lax.all_to_all(third, LINE, 0, 0, tiled=True))
 
     fourth = call(
-        answer, shaped((GROUP, 64, LANES), BF), [smem, vmem, vmem], name="answer"
+        answer, inside((GROUP, 64, LANES), BF), [smem, vmem, vmem], name="answer"
     )(place, rows_named, third)
-    fourth = lax.all_to_all(fourth, PLANE, 0, 0, tiled=True)
-
-    chosen = call(collect, shaped((64, LANES), BF), [vmem], name="collect")(fourth)
+    fourth = near(lax.all_to_all(fourth, PLANE, 0, 0, tiled=True))
+
+    chosen = call(collect, inside((64, LANES), BF), [vmem], name="collect")(fourth)
     returned = jnp.einsum(
         "fskb,skab->fsa", chosen.reshape(2, 8, 4, LANES), weights, preferred_element_type=F32
     )

time: 101 us -> 82 us (0.81)
  blocking collectives: 50.4 us -> 23.4 us
  waiting for transfers between devices: 1.05 us -> 21.2 us
  Pallas kernels: 13.4 us -> 6.86 us
  starting transfers between devices: 28.9 us -> 25.3 us
    all_to_all x3 -> x2, blocking collectives: 50.4 us -> 23.4 us  [the longest x1 12.2 us: shards(): third = near(lax.all_to_all(third, LINE, 0, 0, tiled=True))]
    ppermute x4 -> x3, waiting for transfers between devices: 1.05 us -> 18.6 us  [the longest x1 11.3 us: shards(): far = near(lax.ppermute(far, ALL, [(i, i ^ 2) for i in range(count)]))]
    ppermute x4 -> x3, starting transfers between devices: 18.5 us -> 6.78 us  [the longest x1 5.3 us: shards(): far = near(lax.ppermute(far, ALL, [(i, i ^ 2) for i in range(count)]))]
    all_to_all x1 -> x2, starting transfers between devices: 10.4 us -> 18.5 us  [the longest x1 10.9 us: shards(): second = near(lax.all_to_all(second, LINE, 0, 0, tiled=True))]
    pallas_call x5 -> x7, Pallas kernels: 10 us -> 4.21 us  [the longest x1 1.47 us: shards(): call(first_step, (inside((LEVELS, 2 * ROWS, LANES), F32), inside((LEVELS,...]
    all_to_all x1 -> x2, waiting for transfers between devices: 0.01 us -> 2.62 us  [the longest x1 2.62 us: shards(): first = near(lax.all_to_all(first, PLANE, 0, 0, tiled=True))]
    unnamed x17 -> x7, local copies, waits for them, and re-layouts: 2.93 us -> 1.48 us
  transfers between devices with their start and end apart: 5 -> 5, of which waited for: 1 -> 4; matrix products, arithmetic and copies ran while one was open for 0% -> 0% of each run, Pallas kernels for 4% -> 3%
where the time goes in v2:
time: 82 us; the launch traced here: 81.5 us
  starting transfers between devices  25.3 us (31%)
  blocking collectives  23.4 us (29%)
  waiting for transfers between devices  21.2 us (26%)
  Pallas kernels  6.86 us (8%)
  local copies, waits for them, and re-layouts  2.65 us (3%)
  matrix products  1.23 us (2%)
    all_to_all x1, blocking collectives, shards(): third = near(lax.all_to_all(third, LINE, 0, 0, tiled=True))  12.2 us
    ppermute x1, waiting for transfers between devices, shards(): far = near(lax.ppermute(far, ALL, [(i, i ^ 2) for i in range(count)]))  11.3 us
    all_to_all x1, blocking collectives, shards(): fourth = near(lax.all_to_all(fourth, PLANE, 0, 0, tiled=True))  11.2 us
    all_to_all x1, starting transfers between devices, shards(): second = near(lax.all_to_all(second, LINE, 0, 0, tiled=True))  10.9 us
    all_to_all x1, starting transfers between devices, shards(): first = near(lax.all_to_all(first, PLANE, 0, 0, tiled=True))  7.57 us
    ppermute x1, waiting for transfers between devices, shards(): arrived = near(lax.ppermute(leaving, ALL, pairs))  6.12 us
    ppermute x1, starting transfers between devices, shards(): far = near(lax.ppermute(far, ALL, [(i, i ^ 2) for i in range(count)]))  5.3 us
    pallas_call x1, Pallas kernels, shards(): call(ocean, (shaped((LEVELS, ROWS, LANES), F32), shaped((ROWS, LANES), F3...  2.65 us
  transfers between devices with their start and end apart: 5, of which 4 were waited for; matrix products, arithmetic and copies ran while one was open for 0% of the time, Pallas kernels for 3%

profile of v2, /device:TPU:1, one launch (start us, length us, event | category | flops | bytes accessed | tf_op | source)
XLA Modules:
  0.0 81.5 jit_solution(4183247013999009824)
XLA Ops:
  0.6 0.0 copy-start
  0.7 0.0 copy-start.2
  0.7 0.8 copy-done.2
  1.4 0.1 copy.16
  1.5 0.1 tile.10
  1.6 0.0 copy-start.1
  1.6 0.1 tile.12
  1.7 0.2 copy-done
  1.9 0.5 copy-done.1
  2.4 0.2 fusion
  2.6 0.1 pad.3.clone
  2.7 0.1 maximum_maximum_fusion
  2.8 0.9 %broadcast_in_dim.12 = bf16[16,144,128]{2,1,0:T(8,128)(2,1)} broadcast(bf16[144,128]{1,0:T(8,128)(2,1)S(1)} %maximum_maximum_fusion), dimensions={1,2} | broadcast | bytes 626688 | tf_op jit(solution)/shard_map/broadcast_in_dim | solution.py:344
  3.7 7.6 %all-to-all-start = ((bf16[16,144,128]{2,1,0:T(8,128)(2,1)}), bf16[16,144,128]{2,1,0:T(8,128)(2,1)S(1)}, u32[]{:S(2)}, u32[]{:S(2)}) async-start(bf16[16,144,128]{2,1,0:T(8,128)(2,1)} %broadcast_in_dim.12), calls=%async_computation | async-start | bytes 1179648 | tf_op jit(solution)/shard_map/all_to_all | solution.py:345
  11.3 1.1 %pack_edges.1 = (bf16[2,128,128]{2,1,0:T(8,128)(2,1)S(1)}, bf16[128,128]{1,0:T(8,128)(2,1)S(1)}) custom-call(s32[1]{0:T(128)} %bitcast.quarter, f32[32,8,128]{2,1,0:T(8,128)} %tracer.3, f32[31,8,128]{2,1,0:T(8,128)} %mixing.3, f32[8,128]{1,0:T(8,128)} %height.3, f32[2,8,128]{2,1,0:T(8,128)} %flow.3, s32[8,128]{1,0:T(8,128)} %wet_own.3), custom_call_target="tpu_custom_call" | custom-call | tf_op jit(solution)/shard_map/pack_edges/pallas_call | solution.py:323
  12.4 1.3 %collective-permute-start = (bf16[128,128]{1,0:T(8,128)(2,1)S(1)}, bf16[128,128]{1,0:T(8,128)(2,1)S(1)}, u32[]{:S(2)}, u32[]{:S(2)}) collective-permute-start(bf16[128,128]{1,0:T(8,128)(2,1)S(1)} %get-tuple-element.13), channel_id=1, source_target_pairs={{2,6},{3,7},{4,0},{5,1},{6,10},{7,11},{8,4},{9,5},{10,14},{11,15},... | collective-permute-start | bytes 98312 | tf_op jit(solution)/shard_map/ppermute | solution.py:334
  13.7 6.1 %collective-permute-done._arrived.arrived = bf16[128,128]{1,0:T(8,128)(2,1)S(1)} collective-permute-done((bf16[128,128]{1,0:T(8,128)(2,1)S(1)}, bf16[128,128]{1,0:T(8,128)(2,1)S(1)}, u32[]{:S(2)}, u32[]{:S(2)}) %collective-permute-start) | collective-permute-done | bytes 32800 | tf_op jit(solution)/shard_map/ppermute | solution.py:334
  19.8 2.6 %all-to-all-done.received = bf16[16,144,128]{2,1,0:T(8,128)(2,1)S(1)} async-done(((bf16[16,144,128]{2,1,0:T(8,128)(2,1)}), bf16[16,144,128]{2,1,0:T(8,128)(2,1)S(1)}, u32[]{:S(2)}, u32[]{:S(2)}) %all-to-all-start) | async-done | bytes 589856 | tf_op jit(solution)/shard_map/all_to_all | solution.py:345
  22.4 1.2 %sort_terms.1 = (bf16[16,128,128]{2,1,0:T(8,128)(2,1)}, f32[8,128]{1,0:T(8,128)S(1)}) custom-call(s32[1]{0:T(128)} %bitcast.1.place, bf16[16,144,128]{2,1,0:T(8,128)(2,1)S(1)} %all-to-all-done.received, bf16[128,128]{1,0:T(8,128)(2,1)S(1)} %collective-permute-done._arrived.arrived), custom_call_target="tpu_custom_call" | custom-call | tf_op jit(solution)/shard_map/sort_terms/pallas_call | solution.py:347
  23.6 10.9 %all-to-all-start.1 = ((bf16[16,128,128]{2,1,0:T(8,128)(2,1)}), bf16[16,128,128]{2,1,0:T(8,128)(2,1)S(1)}, u32[]{:S(2)}, u32[]{:S(2)}) async-start(bf16[16,128,128]{2,1,0:T(8,128)(2,1)} %get-tuple-element.14), calls=%async_computation.1 | async-start | bytes 1048576 | tf_op jit(solution)/shard_map/all_to_all | solution.py:354
  34.5 0.2 collective-permute-start.1
  34.7 1.1 %collective-permute-done.1.partner = bf16[256,128]{1,0:T(8,128)(2,1)S(1)} collective-permute-done((bf16[256,128]{1,0:T(8,128)(2,1)S(1)}, bf16[256,128]{1,0:T(8,128)(2,1)S(1)}, u32[]{:S(2)}, u32[]{:S(2)}) %collective-permute-start.1) | collective-permute-done | bytes 65568 | tf_op jit(solution)/shard_map/ppermute | solution.py:359
  35.9 5.3 %collective-permute-start.2 = (bf16[224,128]{1,0:T(8,128)(2,1)S(1)}, bf16[224,128]{1,0:T(8,128)(2,1)S(1)}, u32[]{:S(2)}, u32[]{:S(2)}) collective-permute-start(bf16[224,128]{1,0:T(8,128)(2,1)S(1)} %far_edges.1), channel_id=1, source_target_pairs={{0,2},{1,3},{2,0},{3,1},{4,6},{5,7},{6,4},{7,5},{8,10},{9,11},{10,... | collective-permute-start | bytes 172040 | tf_op jit(solution)/shard_map/ppermute | solution.py:363
  41.2 11.3 %collective-permute-done.2.far = bf16[224,128]{1,0:T(8,128)(2,1)S(1)} collective-permute-done((bf16[224,128]{1,0:T(8,128)(2,1)S(1)}, bf16[224,128]{1,0:T(8,128)(2,1)S(1)}, u32[]{:S(2)}, u32[]{:S(2)}) %collective-permute-start.2) | collective-permute-done | bytes 57376 | tf_op jit(solution)/shard_map/ppermute | solution.py:363
  52.5 1.5 %first_step.1 = (f32[32,16,128]{2,1,0:T(8,128)S(1)}, f32[32,16,128]{2,1,0:T(8,128)S(1)}, f32[3,32,8,128]{3,2,1,0:T(8,128)S(1)}) custom-call(s32[1]{0:T(128)} %bitcast.quarter, f32[32,8,128]{2,1,0:T(8,128)} %tracer.3, f32[31,8,128]{2,1,0:T(8,128)} %mixing.3, s32[8,128]{1,0:T(8,128)} %wet_own.3, bf16[256,128]{1,0:T(8,128)(2,1)S(1)} %collective-permute-done.1.partner, ...), custom_call_target="tpu_custom_call" | custom-call | tf_op jit(solution)/shard_map/first_step/pallas_call | solution.py:365
  54.0 0.0 all-to-all-done.1.flux
  54.0 2.7 %ocean.1 = (f32[32,8,128]{2,1,0:T(8,128)}, f32[8,128]{1,0:T(8,128)}, bf16[16,16,128]{2,1,0:T(8,128)(2,1)S(1)}) custom-call(s32[1]{0:T(128)} %bitcast.quarter, bf16[16,128,128]{2,1,0:T(8,128)(2,1)S(1)} %all-to-all-done.1.flux, f32[8,128]{1,0:T(8,128)} %height.3, f32[2,8,128]{2,1,0:T(8,128)} %flow.3, s32[8,128]{1,0:T(8,128)} %wet_own.3, ...), custom_call_target="tpu_custom_call" | custom-call | tf_op jit(solution)/shard_map/ocean/pallas_call | solution.py:381
  56.7 12.2 %all_to_all.20.received = bf16[16,16,128]{2,1,0:T(8,128)(2,1)S(1)} all-to-all(bf16[16,16,128]{2,1,0:T(8,128)(2,1)S(1)} %get-tuple-element.22), channel_id=1, replica_groups=mesh['c'=4,'y'=4,'x'=4,'h'=2,'k'=2] {'c','h','k'}, dimensions={0} | all-to-all | bytes 131072 | tf_op jit(solution)/shard_map/all_to_all | solution.py:392
  68.9 0.4 answer.1
  69.3 11.2 %all_to_all.21.received = bf16[16,64,128]{2,1,0:T(8,128)(2,1)S(1)} all-to-all(bf16[16,64,128]{2,1,0:T(8,128)(2,1)S(1)} %answer.1), channel_id=1, replica_groups=mesh['c'=4,'y'=4,'x'=4,'h'=2,'k'=2] {'y','x'}, dimensions={0} | all-to-all | bytes 524288 | tf_op jit(solution)/shard_map/all_to_all | solution.py:397
  80.5 1.0 %fusion.2 = bf16[1,2,1024]{2,1,0:T(2,128)(2,1)} fusion(bf16[1,8,4,128,128]{4,3,2,1,0:T(8,128)(2,1)S(1)} %copy-done, bf16[2,8,4,128]{3,2,1,0:T(4,128)(2,1)S(1)} %bitcast.29), kind=kOutput, calls=%fused_computation.4 | convolution fusion | flops 2099200 | bytes 1069056 | tf_op jit(solution)/shard_map/fskb,skab->fsa/dot_general | solution.py:400
  (8 shorter events, 0.1 us)
Async XLA Ops:
  0.6 1.2 %copy-start = (bf16[1,8,4,128,128]{4,3,2,1,0:T(8,128)(2,1)S(1)}, bf16[1,8,4,128,128]{4,3,2,1,0:T(8,128)(2,1)}, u32[]{:S(2)}) copy-start(bf16[1,8,4,128,128]{4,3,2,1,0:T(8,128)(2,1)} %param.9) | copy-start | bytes 3145732
  0.7 0.8 copy-start.2
  1.6 0.8 copy-start.1
  3.7 18.7 %all-to-all-start = ((bf16[16,144,128]{2,1,0:T(8,128)(2,1)}), bf16[16,144,128]{2,1,0:T(8,128)(2,1)S(1)}, u32[]{:S(2)}, u32[]{:S(2)}) async-start(bf16[16,144,128]{2,1,0:T(8,128)(2,1)} %broadcast_in_dim.12), calls=%async_computation | async-start | bytes 1179648 | tf_op jit(solution)/shard_map/all_to_all | solution.py:345
  12.4 7.4 %collective-permute-start = (bf16[128,128]{1,0:T(8,128)(2,1)S(1)}, bf16[128,128]{1,0:T(8,128)(2,1)S(1)}, u32[]{:S(2)}, u32[]{:S(2)}) collective-permute-start(bf16[128,128]{1,0:T(8,128)(2,1)S(1)} %get-tuple-element.13), channel_id=1, source_target_pairs={{2,6},{3,7},{4,0},{5,1},{6,10},{7,11},{8,4},{9,5},{10,14},{11,15},... | collective-permute-start | bytes 98312 | tf_op jit(solution)/shard_map/ppermute | solution.py:334
  23.6 30.4 %all-to-all-start.1 = ((bf16[16,128,128]{2,1,0:T(8,128)(2,1)}), bf16[16,128,128]{2,1,0:T(8,128)(2,1)S(1)}, u32[]{:S(2)}, u32[]{:S(2)}) async-start(bf16[16,128,128]{2,1,0:T(8,128)(2,1)} %get-tuple-element.14), calls=%async_computation.1 | async-start | bytes 1048576 | tf_op jit(solution)/shard_map/all_to_all | solution.py:354
  34.5 1.3 %collective-permute-start.1 = (bf16[256,128]{1,0:T(8,128)(2,1)S(1)}, bf16[256,128]{1,0:T(8,128)(2,1)S(1)}, u32[]{:S(2)}, u32[]{:S(2)}) collective-permute-start(bf16[256,128]{1,0:T(8,128)(2,1)S(1)} %pair_edges.1), channel_id=1, source_target_pairs={{0,1},{1,0},{2,3},{3,2},{4,5},{5,4},{6,7},{7,6},{8,9},{9,8},{10,11... | collective-permute-start | bytes 196616 | tf_op jit(solution)/shard_map/ppermute | solution.py:359
  35.9 16.6 %collective-permute-start.2 = (bf16[224,128]{1,0:T(8,128)(2,1)S(1)}, bf16[224,128]{1,0:T(8,128)(2,1)S(1)}, u32[]{:S(2)}, u32[]{:S(2)}) collective-permute-start(bf16[224,128]{1,0:T(8,128)(2,1)S(1)} %far_edges.1), channel_id=1, source_target_pairs={{0,2},{1,3},{2,0},{3,1},{4,6},{5,7},{6,4},{7,5},{8,10},{9,11},{10,... | collective-permute-start | bytes 172040 | tf_op jit(solution)/shard_map/ppermute | solution.py:363

commit v3 on v2

--- a/solution.py
+++ b/solution.py
@@ -1,4 +1,3 @@
-import numpy as np
 import jax
 import jax.numpy as jnp
 from jax import lax
@@ -29,16 +28,17 @@
 
 vmem = pl.BlockSpec(memory_space=pltpu.VMEM)
 smem = pl.BlockSpec(memory_space=pltpu.SMEM)
-
-
-def call(kernel, outs, ins, scratch=(), name=None):
+far = pl.BlockSpec(memory_space=pltpu.HBM)
+
+
+def call(kernel, outs, ins, scratch=(), out_specs=None, room=12 << 10):
     return pl.pallas_call(
         kernel,
         out_shape=outs,
         in_specs=ins,
-        out_specs=jax.tree.map(lambda _: vmem, outs),
+        out_specs=jax.tree.map(lambda _: vmem, outs) if out_specs is None else out_specs,
         scratch_shapes=list(scratch),
-        name=name,
+        compiler_params=pltpu.CompilerParams(vmem_limit_bytes=room << 10),
     )
 
 
@@ -70,68 +70,125 @@
     return pltpu.roll(v, 1, axis=0)
 
 
-def pack_edges(quarter, tracer, mixing, height, flow, wet, edges, leaving):
-    own = jnp.concatenate([height[...], flow[0], flow[1], wet[...].astype(F32)], axis=0).astype(BF)
+def prepare(
+    place, quarter, tracer_far, mixing_far, height_far, flow_far, wet_far, targets_far, sources_far,
+    weights_far, leaving, both, own, weights, message,
+    tracer, mixing, wet, targets, sources, flat, packet, done,
+):
+    def load(source, target, i):
+        copy = pltpu.make_async_copy(source, target, done.at[i])
+        copy.start()
+        return copy
+
+    edges = [
+        load(tracer_far, tracer, 0),
+        load(mixing_far, mixing, 1),
+        load(height_far, own.at[0:8], 2),
+        load(flow_far.at[0], own.at[8:16], 3),
+        load(flow_far.at[1], own.at[16:24], 4),
+        load(wet_far, wet, 5),
+    ]
+    small = [load(targets_far, targets, 6), load(sources_far, sources, 7)]
+    large = [load(weights_far.at[s], weights.at[s], 8 + s) for s in range(8)]
+    for copy in edges:
+        copy.wait()
+    own[24:32] = wet[...].astype(F32)
     zero = jnp.zeros((1, LANES), F32)
     for i, (first, second, rim) in enumerate(((6, 7, 7), (0, 1, 0))):
-        edges[i, 0:32] = own
-        edges[i, 32:64] = tracer[:, first, :].astype(BF)
-        edges[i, 64:96] = tracer[:, second, :].astype(BF)
-        edges[i, 96:128] = jnp.concatenate([mixing[:, rim, :], zero], axis=0).astype(BF)
-    leaving[...] = edges[jnp.where(quarter[0] >= 2, 0, 1)]
-
-
-def pair_edges(quarter, edges, arrived, _after, message):
+        both[i, 0:32] = tracer[:, first, :].astype(BF)
+        both[i, 32:64] = tracer[:, second, :].astype(BF)
+        both[i, 64:96] = jnp.concatenate([mixing[:, rim, :], zero], axis=0).astype(BF)
+    leaving[0:32] = own[...].astype(BF)
+    leaving[32:128] = both[jnp.where(quarter[0] >= 2, 0, 1)]
+    for copy in small:
+        copy.wait()
+    lane = lax.broadcasted_iota(jnp.int32, (4, LANES), 1)
+    link = lax.broadcasted_iota(jnp.int32, (4, LANES), 0)
+    mine = (lane >> 5 == (place[0] & 3)) & ((lane & 3) == link)
+    named = jnp.zeros((4, LANES), jnp.int32)
+    for s in range(8):
+        column = jnp.broadcast_to(targets[:, s : s + 1], (4, LANES))
+        named = named + jnp.where(mine & ((lane & 31) >> 2 == s), column, 0)
+    named = jnp.broadcast_to(jnp.sum(named, axis=0, keepdims=True), (ROWS, LANES))
+    line = lax.broadcasted_iota(jnp.int32, (ROWS, LANES), 0)
+    coded = jnp.where(line == 0, named >> 6, jnp.where(line == 1, named & 63, 0)).astype(F32)
+    coded = jnp.concatenate([coded, jnp.zeros((ROWS, LANES), F32)], axis=0).astype(BF)
+    packet[128:144] = coded
+    blank = jnp.zeros((4, LANES), F32)
+    for s in range(0, 8, 2):
+        some = [sources[:, i * LANES : (i + 1) * LANES].astype(F32) for i in (s, s + 1)]
+        left = jnp.concatenate(
+            [
+                jnp.concatenate([some[0], blank], axis=1),
+                jnp.concatenate([blank, some[1]], axis=1),
+            ],
+            axis=0,
+        ).astype(BF)
+        large[s].wait()
+        large[s + 1].wait()
+        for k in (0, 2):
+            right = jnp.concatenate(
+                [
+                    jnp.concatenate([weights[i, k], weights[i, k + 1]], axis=1)
+                    for i in (s, s + 1)
+                ],
+                axis=0,
+            )
+            out = jnp.dot(left, right, preferred_element_type=F32)
+            for i in range(2):
+                for j in range(2):
+                    flat[pl.ds((s + i) * 4 + k + j, 4, stride=TERMS), :] = out[
+                        4 * i : 4 * i + 4, j * LANES : (j + 1) * LANES
+                    ]
+    packet[0:128] = flat[...].astype(BF)
+    sent = [load(packet, message.at[p], p) for p in range(GROUP)]
+    for copy in sent:
+        copy.wait()
+
+
+def quad_edges(quarter, leaving, both, arrived, message):
     mine = quarter[0]
-    message[0:32] = edges[0, 0:32]
+    message[0:32] = leaving[0:32]
     message[32:64] = arrived[0:32]
-    message[64:160] = edges[mine & 1, 32:128]
-
-    @pl.when(mine == 1)
+    ends = (mine == 0) | (mine == 3)
+
+    @pl.when(ends)
     def _():
-        message[160:256] = edges[0, 32:128]
-
-    @pl.when(mine == 2)
+        message[64:160] = arrived[32:128]
+
+    @pl.when(jnp.logical_not(ends))
     def _():
-        message[160:256] = edges[1, 32:128]
-
-    @pl.when((mine == 0) | (mine == 3))
-    def _():
-        message[160:256] = arrived[32:128]
-
-
-def far_edges(quarter, edges, arrived, partner, message):
-    core = quarter[0] & 1
-    own = pl.multiple_of(32 * core, 32)
-    other = pl.multiple_of(32 - 32 * core, 32)
-    message[pl.ds(own, 32)] = edges[0, 0:32]
-    message[pl.ds(other, 32)] = partner[0:32]
-    message[pl.ds(64 + own, 32)] = arrived[0:32]
-    message[pl.ds(64 + other, 32)] = partner[32:64]
-    message[128:224] = partner[160:256]
-
-
-def edge_sides(mine, partner, far):
+        message[64:160] = both[(mine + 1) & 1]
+
+
+def pair_edges(quarter, leaving, both, opposite, _after, message):
+    message[0:32] = leaving[0:32]
+    message[32:96] = opposite[0:64]
+    message[96:192] = both[quarter[0] & 1]
+    message[192:288] = opposite[64:160]
+
+
+def edge_sides(mine, partner):
     first = (mine & 1) == 0
-    near_edge = partner[64:160].astype(F32)
-    far_edge = far[128:224].astype(F32)
+    near_edge = partner[96:192].astype(F32)
+    far_edge = partner[192:288].astype(F32)
     return jnp.where(first, far_edge, near_edge), jnp.where(first, near_edge, far_edge)
 
 
-def strips(mine, partner, far):
+def strips(mine, opposite, partner):
     first = (mine & 1) == 0
-    shift = 32 * (mine & 1)
-    prev = jnp.where(mine < 2, 64, 0)
-    follow = 64 - prev
-
-    def part(start):
-        return far[pl.ds(pl.multiple_of(start, 32), 32)].astype(F32)
-
+    low = mine < 2
     beside = partner[0:32].astype(F32)
-    before2 = part(prev + shift)
-    before = jnp.where(first, part(prev + 32), beside)
-    after = jnp.where(first, beside, part(follow))
-    after2 = part(follow + shift)
+    ours = (opposite[0:32].astype(F32), opposite[32:64].astype(F32))
+    theirs = (partner[32:64].astype(F32), partner[64:96].astype(F32))
+    prev_own = jnp.where(low, ours[1], ours[0])
+    prev_other = jnp.where(low, theirs[1], theirs[0])
+    next_own = jnp.where(low, ours[0], ours[1])
+    next_other = jnp.where(low, theirs[0], theirs[1])
+    before2 = prev_own
+    before = jnp.where(first, prev_other, beside)
+    after = jnp.where(first, beside, next_other)
+    after2 = next_own
     return before2, before, after, after2
 
 
@@ -167,10 +224,10 @@
             message[c * 4 + s] = jnp.concatenate(pieces, axis=0).astype(BF)
 
 
-def first_step(quarter, tracer, mixing, wet_own, partner, far, base, reply, factors, halo, mix_halo, work):
+def first_step(quarter, tracer, mixing, own, opposite, partner, base, reply, factors, halo, mix_halo, work):
     mine = quarter[0]
-    before, after = edge_sides(mine, partner, far)
-    _, wet_before, wet_after, _ = (strip[24:32] for strip in strips(mine, partner, far))
+    before, after = edge_sides(mine, partner)
+    _, wet_before, wet_after, _ = (strip[24:32] for strip in strips(mine, opposite, partner))
     halo[...] = jnp.zeros_like(halo)
     mix_halo[...] = jnp.zeros_like(mix_halo)
     halo[pl.ds(0, LEVELS, stride=ROWS), :] = after[0:32]
@@ -181,7 +238,7 @@
     mix_halo[pl.ds(7, LEVELS, stride=ROWS), :] = before[64:96]
     lower = lax.broadcasted_iota(jnp.int32, (ROWS, LANES), 0) < 4
     wet = jnp.concatenate(
-        [wet_own[...].astype(F32), jnp.where(lower, wet_after, wet_before)], axis=0
+        [own[24:32], jnp.where(lower, wet_after, wet_before)], axis=0
     )
     face_e = wet * east(wet)
     face_n = wet * north(wet)
@@ -222,11 +279,11 @@
 
 
 def ocean(
-    quarter, flux, height, flow, wet_own, partner, far, base, reply, factors,
+    quarter, flux, own, opposite, partner, base, reply, factors,
     tracer_out, height_out, message, work,
 ):
     mine = quarter[0]
-    before2, before, after, after2 = strips(mine, partner, far)
+    before2, before, after, after2 = strips(mine, opposite, partner)
 
     def ring(i, own):
         r = slice(i * ROWS, (i + 1) * ROWS)
@@ -235,13 +292,13 @@
     total = flux[0].astype(F32)
     for p in range(1, GROUP):
         total = total + flux[p].astype(F32)
-    wet = ring(3, wet_own[...].astype(F32))
+    wet = ring(3, own[24:32])
     rain = fresh_gain * total[0:40] * wet
     push_e = stress_gain * total[40:80]
     push_n = stress_gain * total[80:120]
-    h = ring(0, height[...])
-    flow_e = ring(1, flow[0])
-    flow_n = ring(2, flow[1])
+    h = ring(0, own[0:8])
+    flow_e = ring(1, own[8:16])
+    flow_n = ring(2, own[16:24])
     face_e = wet * east(wet)
     face_n = wet * north(wet)
     face_w, flow_w, push_w = west(face_e), west(flow_e), west(push_e)
@@ -304,63 +361,105 @@
             message[4 * q : 4 * q + 4, f * 32 : f * 32 + 32, :] = out.reshape(4, 32, LANES)
 
 
-def collect(received, chosen):
+def finish(received, weights, tracer, height, out, tracer_out, height_out, flat, done):
+    saves = [
+        pltpu.make_async_copy(tracer, tracer_out, done.at[0]),
+        pltpu.make_async_copy(height, height_out, done.at[1]),
+    ]
+    for save in saves:
+        save.start()
     total = received[0].astype(F32)
     for p in range(1, GROUP):
         total = total + received[p].astype(F32)
-    chosen[...] = total.astype(BF)
+    flat[...] = total
+    for s in range(0, 8, 2):
+        answer = None
+        for k in (0, 2):
+            left = jnp.concatenate(
+                [
+                    jnp.concatenate(
+                        [flat[pl.ds(i * 4 + j, 2, stride=TERMS), :] for j in (k, k + 1)], axis=1
+                    )
+                    for i in (s, s + 1)
+                ],
+                axis=0,
+            ).astype(BF)
+            right = jnp.concatenate(
+                [
+                    jnp.concatenate([weights[i, k], weights[i, k + 1]], axis=1)
+                    for i in (s, s + 1)
+                ],
+                axis=0,
+            )
+            part = lax.dot_general(
+                left, right, (((1,), (1,)), ((), ())), preferred_element_type=F32
+            )
+            answer = part if answer is None else answer + part
+        out[:, s * LANES : (s + 1) * LANES] = answer[0:2, 0:LANES].astype(BF)
+        out[:, (s + 1) * LANES : (s + 2) * LANES] = answer[2:4, LANES:].astype(BF)
+    for save in saves:
+        save.wait()
 
 
 def shards(airside, matrices, latitude, tracer, mixing, height, flow, marine):
-    sources = airside[0].reshape(4, 8, LANES)
-    weights = matrices[0]
-    targets = latitude[0].reshape(-1)
-    spot = lax.axis_index(PLANE)
-    place = spot.astype(jnp.int32).reshape(1)
+    spot = lax.axis_index(PLANE).astype(jnp.int32)
+    turn = lax.axis_index(("h", "k")).astype(jnp.int32)
+    place, quarter = spot.reshape(1), turn.reshape(1)
     count = lax.axis_size(ALL)
 
-    quarter = lax.axis_index(("h", "k")).astype(jnp.int32).reshape(1)
-    edges, leaving = call(
-        pack_edges,
-        (inside((2, 128, LANES), BF), inside((128, LANES), BF)),
-        [smem] + [vmem] * 5,
-        name="pack_edges",
-    )(quarter, tracer, mixing, height, flow, marine)
+    leaving, both, own, weights, first = call(
+        prepare,
+        (
+            inside((128, LANES), BF),
+            inside((2, 96, LANES), BF),
+            inside((32, LANES), F32),
+            inside((8, 4, LANES, LANES), BF),
+            shaped((GROUP, 144, LANES), BF),
+        ),
+        [smem, smem] + [far] * 8,
+        [
+            pltpu.VMEM((LEVELS, ROWS, LANES), F32),
+            pltpu.VMEM((LEVELS - 1, ROWS, LANES), F32),
+            pltpu.VMEM((ROWS, LANES), jnp.int32),
+            pltpu.VMEM((4, 8), jnp.int32),
+            pltpu.VMEM((4, 8 * LANES), BF),
+            pltpu.VMEM((4 * TERMS, LANES), F32),
+            pltpu.VMEM((144, LANES), BF),
+            pltpu.SemaphoreType.DMA((16,)),
+        ],
+        out_specs=(vmem, vmem, vmem, vmem, far),
+        room=60 * 1024,
+    )(
+        place, quarter, tracer, mixing, height, flow, marine,
+        latitude[0].T, airside[0], matrices[0],
+    )
+    leaving, both, own, weights = map(near, (leaving, both, own, weights))
     pairs = []
     for i in range(count):
-        j = i + 4 if i % 4 >= 2 else i - 4
+        j = i + 4 if i & 2 else i - 4
         if 0 <= j < count:
             pairs.append((i, j))
     arrived = near(lax.ppermute(leaving, ALL, pairs))
-    edges = near(edges)
-
-    terms = jnp.einsum("fsa,skab->fskb", sources, weights, preferred_element_type=F32)
-    terms = terms.astype(BF).reshape(128, LANES)
-    lanes = jnp.arange(LANES, dtype=jnp.int32)
-    spread = jnp.where(lanes // TERMS == spot % 4, jnp.tile(targets, 4), 0)
-    coded = jnp.stack([spread // 64, spread % 64]).astype(BF)
-    coded = jnp.concatenate([coded, jnp.zeros((14, LANES), BF)])
-    first = jnp.concatenate([terms, coded])
-    first = jnp.broadcast_to(first[None], (GROUP, 144, LANES))
     first = near(lax.all_to_all(first, PLANE, 0, 0, tiled=True))
+
+    opposite = call(
+        quad_edges, inside((160, LANES), BF), [smem] + [vmem] * 3
+    )(quarter, leaving, both, arrived)
+    leaving_quad = opposite
+    opposite = near(lax.ppermute(leaving_quad, ALL, [(i, i ^ 2) for i in range(count)]))
 
     second, rows_named = call(
         sort_terms,
         (inside((GROUP, 128, LANES), BF), inside((ROWS, LANES), F32)),
         [smem, vmem, vmem],
-        name="sort_terms",
-    )(place, first, arrived)
+    )(place, first, near(leaving_quad))
     rows_named = near(rows_named)
     second = near(lax.all_to_all(second, LINE, 0, 0, tiled=True))
 
     partner = call(
-        pair_edges, inside((256, LANES), BF), [smem, vmem, vmem, vmem], name="pair_edges"
-    )(quarter, edges, arrived, rows_named)
+        pair_edges, inside((288, LANES), BF), [smem] + [vmem] * 4
+    )(quarter, leaving, both, opposite, rows_named)
     partner = near(lax.ppermute(partner, ALL, [(i, i ^ 1) for i in range(count)]))
-    far = call(
-        far_edges, inside((224, LANES), BF), [smem, vmem, vmem, vmem], name="far_edges"
-    )(quarter, edges, arrived, partner)
-    far = near(lax.ppermute(far, ALL, [(i, i ^ 2) for i in range(count)]))
 
     base, reply, factors = call(
         first_step,
@@ -375,32 +474,37 @@
             pltpu.VMEM((LEVELS * ROWS, LANES), F32),
             pltpu.VMEM((LEVELS, 2 * ROWS, LANES), F32),
         ],
-        name="first_step",
-    )(quarter, tracer, mixing, marine, partner, far)
+    )(quarter, tracer, mixing, own, opposite, partner)
 
     tracer_new, height_new, third = call(
         ocean,
         (
+            inside((LEVELS, ROWS, LANES), F32),
+            inside((ROWS, LANES), F32),
+            inside((GROUP, 16, LANES), BF),
+        ),
+        [smem] + [vmem] * 7,
+        [pltpu.VMEM((LEVELS, ROWS, LANES), F32)],
+    )(quarter, second, own, opposite, partner, near(base), near(reply), near(factors))
+    third = near(lax.all_to_all(third, LINE, 0, 0, tiled=True))
+
+    fourth = call(
+        answer, inside((GROUP, 64, LANES), BF), [smem, vmem, vmem]
+    )(place, rows_named, third)
+    fourth = near(lax.all_to_all(fourth, PLANE, 0, 0, tiled=True))
+
+    returned, tracer_new, height_new = call(
+        finish,
+        (
+            shaped((2, 8 * LANES), BF),
             shaped((LEVELS, ROWS, LANES), F32),
             shaped((ROWS, LANES), F32),
-            inside((GROUP, 16, LANES), BF),
         ),
-        [smem] + [vmem] * 9,
-        [pltpu.VMEM((LEVELS, ROWS, LANES), F32)],
-        name="ocean",
-    )(quarter, second, height, flow, marine, partner, far, near(base), near(reply), near(factors))
-    third = near(lax.all_to_all(third, LINE, 0, 0, tiled=True))
-
-    fourth = call(
-        answer, inside((GROUP, 64, LANES), BF), [smem, vmem, vmem], name="answer"
-    )(place, rows_named, third)
-    fourth = near(lax.all_to_all(fourth, PLANE, 0, 0, tiled=True))
-
-    chosen = call(collect, inside((64, LANES), BF), [vmem], name="collect")(fourth)
-    returned = jnp.einsum(
-        "fskb,skab->fsa", chosen.reshape(2, 8, 4, LANES), weights, preferred_element_type=F32
-    )
-    return tracer_new, height_new, returned.reshape(1, 2, 8 * LANES).astype(BF)
+        [vmem] * 4,
+        [pltpu.VMEM((2 * TERMS, LANES), F32), pltpu.SemaphoreType.DMA((2,))],
+        out_specs=(vmem, far, far),
+    )(fourth, weights, near(tracer_new), near(height_new))
+    return tracer_new, height_new, returned[None]
 
 
 def solution(mesh):

time: 82 us -> 80.5 us (0.982)
  local copies, waits for them, and re-layouts: 2.65 us -> 0.01 us
  waiting for transfers between devices: 21.2 us -> 22.6 us
  starting transfers between devices: 25.3 us -> 26.7 us
  matrix products: 1.23 us -> 0 us
  blocking collectives: 23.4 us -> 22.4 us
    pallas_call x6, Pallas kernels: 4.17 us -> 5.94 us  [the longest x1 2.79 us: shards(): call(prepare, (inside((128, LANES), BF), inside((2, 96, LANES), BF), insi...]
    unnamed x7 -> x4, local copies, waits for them, and re-layouts: 1.48 us -> 0.01 us
    ppermute x1, starting transfers between devices: 0.2 us -> 1.46 us  [shards(): lax.ppermute(partner, ALL, [(i, i ^ 1) for i in range(count)])]
    dot_general x2 -> x0, matrix products: 1.23 us -> none  [the longest x1 0.99 us: shards(): jnp.einsum('fskb,skab->fsa', chosen.reshape(2, 8, 4, LANES), weights, pre...]
    ppermute x1, waiting for transfers between devices: 6.12 us -> 7.21 us  [shards(): arrived = near(lax.ppermute(leaving, ALL, pairs))]
    all_to_all x1, blocking collectives: 12.2 us -> 11.2 us  [shards(): third = near(lax.all_to_all(third, LINE, 0, 0, tiled=True))]
    pallas_call x1, Pallas kernels: 1.47 us -> 0.49 us  [shards(): call(first_step, (inside((LEVELS, 2 * ROWS, LANES), F32), inside((LEVELS,...]
    broadcast_in_dim x2 -> x0, local copies, waits for them, and re-layouts: 0.9 us -> none  [the longest x1 0.9 us: shards(): first = jnp.broadcast_to(first[None], (GROUP, 144, LANES))]
  transfers between devices with their start and end apart: 5 -> 5, of which waited for: 4 -> 4; matrix products, arithmetic and copies ran while one was open for 0% -> 0% of each run, Pallas kernels for 3% -> 1%
where the time goes in v3:
time: 80.5 us; the launch traced here: 80.1 us
  starting transfers between devices  26.7 us (33%)
  waiting for transfers between devices  22.6 us (28%)
  blocking collectives  22.4 us (28%)
  Pallas kernels  7.65 us (10%)
    ppermute x1, waiting for transfers between devices, shards(): lax.ppermute(leaving_quad, ALL, [(i, i ^ 2) for i in range(count)])  11.9 us
    all_to_all x1, blocking collectives, shards(): third = near(lax.all_to_all(third, LINE, 0, 0, tiled=True))  11.2 us
    all_to_all x1, blocking collectives, shards(): fourth = near(lax.all_to_all(fourth, PLANE, 0, 0, tiled=True))  11.2 us
    all_to_all x1, starting transfers between devices, shards(): second = near(lax.all_to_all(second, LINE, 0, 0, tiled=True))  11 us
    all_to_all x1, starting transfers between devices, shards(): first = near(lax.all_to_all(first, PLANE, 0, 0, tiled=True))  7.58 us
    ppermute x1, waiting for transfers between devices, shards(): arrived = near(lax.ppermute(leaving, ALL, pairs))  7.21 us
    ppermute x1, starting transfers between devices, shards(): lax.ppermute(leaving_quad, ALL, [(i, i ^ 2) for i in range(count)])  5.35 us
    pallas_call x1, Pallas kernels, shards(): call(prepare, (inside((128, LANES), BF), inside((2, 96, LANES), BF), insi...  2.79 us
  transfers between devices with their start and end apart: 5, of which 4 were waited for; matrix products, arithmetic and copies ran while one was open for 0% of the time, Pallas kernels for 1%

profile of v3, /device:TPU:1, one launch (start us, length us, event | category | flops | bytes accessed | tf_op | source)
XLA Modules:
  0.0 80.1 jit_solution(2098039875872906690)
XLA Ops:
  0.6 2.8 %shard_map.103 = (bf16[128,128]{1,0:T(8,128)(2,1)S(1)}, bf16[2,96,128]{2,1,0:T(8,128)(2,1)S(1)}, f32[32,128]{1,0:T(8,128)S(1)}, bf16[8,4,128,128]{3,2,1,0:T(8,128)(2,1)S(1)}, bf16[16,144,128]{2,1,0:T(8,128)(2,1)}) custom-call(s32[1]{0:T(128)} %bitcast.place, s32[1]{0:T(128)} %bitcast.1.quarter, f32[32,8,128]{2,1,0:T(8,128)} %tracer.1, f32[31,8,128]{2,1,0:T(8,128)} %mixing.1, ...), custom_call_target="tpu_custom_call" | custom-call | tf_op jit(solution)/shard_map/pallas_call | solution.py:410
  3.4 7.6 %all-to-all-start = ((bf16[16,144,128]{2,1,0:T(8,128)(2,1)}), bf16[16,144,128]{2,1,0:T(8,128)(2,1)S(1)}, u32[]{:S(2)}, u32[]{:S(2)}) async-start(bf16[16,144,128]{2,1,0:T(8,128)(2,1)} %get-tuple-element.19), calls=%async_computation | async-start | bytes 1179648 | tf_op jit(solution)/shard_map/all_to_all | solution.py:443
  11.0 1.3 %collective-permute-start = (bf16[128,128]{1,0:T(8,128)(2,1)S(1)}, bf16[128,128]{1,0:T(8,128)(2,1)S(1)}, u32[]{:S(2)}, u32[]{:S(2)}) collective-permute-start(bf16[128,128]{1,0:T(8,128)(2,1)S(1)} %get-tuple-element.20.leaving), channel_id=1, source_target_pairs={{2,6},{3,7},{4,0},{5,1},{6,10},{7,11},{8,4},{9,5},{10,14},{11,15},... | collective-permute-start | bytes 98312 | tf_op jit(solution)/shard_map/ppermute | solution.py:442
  12.3 7.2 %collective-permute-done.arrived = bf16[128,128]{1,0:T(8,128)(2,1)S(1)} collective-permute-done((bf16[128,128]{1,0:T(8,128)(2,1)S(1)}, bf16[128,128]{1,0:T(8,128)(2,1)S(1)}, u32[]{:S(2)}, u32[]{:S(2)}) %collective-permute-start) | collective-permute-done | bytes 32800 | tf_op jit(solution)/shard_map/ppermute | solution.py:442
  19.5 2.6 %all-to-all-done.received = bf16[16,144,128]{2,1,0:T(8,128)(2,1)S(1)} async-done(((bf16[16,144,128]{2,1,0:T(8,128)(2,1)}), bf16[16,144,128]{2,1,0:T(8,128)(2,1)S(1)}, u32[]{:S(2)}, u32[]{:S(2)}) %all-to-all-start) | async-done | bytes 589856 | tf_op jit(solution)/shard_map/all_to_all | solution.py:443
  22.2 1.2 %shard_map.105 = (bf16[16,128,128]{2,1,0:T(8,128)(2,1)}, f32[8,128]{1,0:T(8,128)S(1)}) custom-call(s32[1]{0:T(128)} %bitcast.place, bf16[16,144,128]{2,1,0:T(8,128)(2,1)S(1)} %all-to-all-done.received, bf16[160,128]{1,0:T(8,128)(2,1)S(1)} %shard_map.104._arrived), custom_call_target="tpu_custom_call" | custom-call | tf_op jit(solution)/shard_map/pallas_call | solution.py:451
  23.4 0.0 copy-start.1
  23.4 11.0 %all-to-all-start.1 = ((bf16[16,128,128]{2,1,0:T(8,128)(2,1)}), bf16[16,128,128]{2,1,0:T(8,128)(2,1)S(1)}, u32[]{:S(2)}, u32[]{:S(2)}) async-start(bf16[16,128,128]{2,1,0:T(8,128)(2,1)} %get-tuple-element.23), calls=%async_computation.1 | async-start | bytes 1048576 | tf_op jit(solution)/shard_map/all_to_all | solution.py:457
  34.4 0.0 copy-start
  34.4 5.3 %collective-permute-start.1 = (bf16[160,128]{1,0:T(8,128)(2,1)S(1)}, bf16[160,128]{1,0:T(8,128)(2,1)S(1)}, u32[]{:S(2)}, u32[]{:S(2)}) collective-permute-start(bf16[160,128]{1,0:T(8,128)(2,1)S(1)} %shard_map.104._arrived), channel_id=1, source_target_pairs={{0,2},{1,3},{2,0},{3,1},{4,6},{5,7},{6,4},{7,5},{8,10},{9,11},{10,... | collective-permute-start | bytes 122888 | tf_op jit(solution)/shard_map/ppermute | solution.py:449
  39.8 11.9 %collective-permute-done.1.opposite = bf16[160,128]{1,0:T(8,128)(2,1)S(1)} collective-permute-done((bf16[160,128]{1,0:T(8,128)(2,1)S(1)}, bf16[160,128]{1,0:T(8,128)(2,1)S(1)}, u32[]{:S(2)}, u32[]{:S(2)}) %collective-permute-start.1) | collective-permute-done | bytes 40992 | tf_op jit(solution)/shard_map/ppermute | solution.py:449
  51.7 1.5 %collective-permute-start.2 = (bf16[288,128]{1,0:T(8,128)(2,1)S(1)}, bf16[288,128]{1,0:T(8,128)(2,1)S(1)}, u32[]{:S(2)}, u32[]{:S(2)}) collective-permute-start(bf16[288,128]{1,0:T(8,128)(2,1)S(1)} %shard_map.106), channel_id=1, source_target_pairs={{0,1},{1,0},{2,3},{3,2},{4,5},{5,4},{6,7},{7,6},{8,9},{9,8},{10,11... | collective-permute-start | bytes 221192 | tf_op jit(solution)/shard_map/ppermute | solution.py:462
  53.1 0.9 %collective-permute-done.2.partner = bf16[288,128]{1,0:T(8,128)(2,1)S(1)} collective-permute-done((bf16[288,128]{1,0:T(8,128)(2,1)S(1)}, bf16[288,128]{1,0:T(8,128)(2,1)S(1)}, u32[]{:S(2)}, u32[]{:S(2)}) %collective-permute-start.2) | collective-permute-done | bytes 73760 | tf_op jit(solution)/shard_map/ppermute | solution.py:462
  54.0 0.0 copy-done.1
  54.0 0.0 copy-done
  54.0 0.5 shard_map.107
  54.5 0.0 all-to-all-done.1.flux
  54.5 1.4 %shard_map.108 = (f32[32,8,128]{2,1,0:T(8,128)S(1)}, f32[8,128]{1,0:T(8,128)S(1)}, bf16[16,16,128]{2,1,0:T(8,128)(2,1)S(1)}) custom-call(s32[1]{0:T(128)} %bitcast.1.quarter, bf16[16,128,128]{2,1,0:T(8,128)(2,1)S(1)} %all-to-all-done.1.flux, f32[32,128]{1,0:T(8,128)S(1)} %get-tuple-element.24.own, bf16[160,128]{1,0:T(8,128)(2,1)S(1)} %collective-permute-done.1.opposite, ...), custom_call_target="tpu_custom_call" | custom-call | tf_op jit(solution)/shard_map/pallas_call | solution.py:479
  55.9 11.2 %all_to_all.20.received = bf16[16,16,128]{2,1,0:T(8,128)(2,1)S(1)} all-to-all(bf16[16,16,128]{2,1,0:T(8,128)(2,1)S(1)} %get-tuple-element.28), channel_id=1, replica_groups=mesh['c'=4,'y'=4,'x'=4,'h'=2,'k'=2] {'c','h','k'}, dimensions={0} | all-to-all | bytes 131072 | tf_op jit(solution)/shard_map/all_to_all | solution.py:489
  67.1 0.4 shard_map.109
  67.5 11.2 %all_to_all.21.received = bf16[16,64,128]{2,1,0:T(8,128)(2,1)S(1)} all-to-all(bf16[16,64,128]{2,1,0:T(8,128)(2,1)S(1)} %shard_map.109), channel_id=1, replica_groups=mesh['c'=4,'y'=4,'x'=4,'h'=2,'k'=2] {'y','x'}, dimensions={0} | all-to-all | bytes 524288 | tf_op jit(solution)/shard_map/all_to_all | solution.py:494
  78.6 1.4 %shard_map.110 = (bf16[2,1024]{1,0:T(2,128)(2,1)}, f32[32,8,128]{2,1,0:T(8,128)}, f32[8,128]{1,0:T(8,128)}) custom-call(bf16[16,64,128]{2,1,0:T(8,128)(2,1)S(1)} %all_to_all.21.received, bf16[8,4,128,128]{3,2,1,0:T(8,128)(2,1)S(1)} %get-tuple-element.29.weights, f32[32,8,128]{2,1,0:T(8,128)S(1)} %get-tuple-element.30.tracer, ...), custom_call_target="tpu_custom_call" | custom-call | tf_op jit(solution)/shard_map/pallas_call | solution.py:496
  (2 shorter events, 0.0 us)
Async XLA Ops:
  3.4 18.7 %all-to-all-start = ((bf16[16,144,128]{2,1,0:T(8,128)(2,1)}), bf16[16,144,128]{2,1,0:T(8,128)(2,1)S(1)}, u32[]{:S(2)}, u32[]{:S(2)}) async-start(bf16[16,144,128]{2,1,0:T(8,128)(2,1)} %get-tuple-element.19), calls=%async_computation | async-start | bytes 1179648 | tf_op jit(solution)/shard_map/all_to_all | solution.py:443
  11.0 8.5 %collective-permute-start = (bf16[128,128]{1,0:T(8,128)(2,1)S(1)}, bf16[128,128]{1,0:T(8,128)(2,1)S(1)}, u32[]{:S(2)}, u32[]{:S(2)}) collective-permute-start(bf16[128,128]{1,0:T(8,128)(2,1)S(1)} %get-tuple-element.20.leaving), channel_id=1, source_target_pairs={{2,6},{3,7},{4,0},{5,1},{6,10},{7,11},{8,4},{9,5},{10,14},{11,15},... | collective-permute-start | bytes 98312 | tf_op jit(solution)/shard_map/ppermute | solution.py:442
  23.4 30.6 %copy-start.1 = (f32[31,8,128]{2,1,0:T(8,128)S(1)}, f32[31,8,128]{2,1,0:T(8,128)}, u32[]{:S(2)}) copy-start(f32[31,8,128]{2,1,0:T(8,128)} %mixing.1) | copy-start | bytes 380932
  23.4 31.1 %all-to-all-start.1 = ((bf16[16,128,128]{2,1,0:T(8,128)(2,1)}), bf16[16,128,128]{2,1,0:T(8,128)(2,1)S(1)}, u32[]{:S(2)}, u32[]{:S(2)}) async-start(bf16[16,128,128]{2,1,0:T(8,128)(2,1)} %get-tuple-element.23), calls=%async_computation.1 | async-start | bytes 1048576 | tf_op jit(solution)/shard_map/all_to_all | solution.py:457
  34.4 19.6 %copy-start = (f32[32,8,128]{2,1,0:T(8,128)S(1)}, f32[32,8,128]{2,1,0:T(8,128)}, u32[]{:S(2)}) copy-start(f32[32,8,128]{2,1,0:T(8,128)} %tracer.1) | copy-start | bytes 393220
  34.4 17.2 %collective-permute-start.1 = (bf16[160,128]{1,0:T(8,128)(2,1)S(1)}, bf16[160,128]{1,0:T(8,128)(2,1)S(1)}, u32[]{:S(2)}, u32[]{:S(2)}) collective-permute-start(bf16[160,128]{1,0:T(8,128)(2,1)S(1)} %shard_map.104._arrived), channel_id=1, source_target_pairs={{0,2},{1,3},{2,0},{3,1},{4,6},{5,7},{6,4},{7,5},{8,10},{9,11},{10,... | collective-permute-start | bytes 122888 | tf_op jit(solution)/shard_map/ppermute | solution.py:449
  51.7 2.4 %collective-permute-start.2 = (bf16[288,128]{1,0:T(8,128)(2,1)S(1)}, bf16[288,128]{1,0:T(8,128)(2,1)S(1)}, u32[]{:S(2)}, u32[]{:S(2)}) collective-permute-start(bf16[288,128]{1,0:T(8,128)(2,1)S(1)} %shard_map.106), channel_id=1, source_target_pairs={{0,1},{1,0},{2,3},{3,2},{4,5},{5,4},{6,7},{7,6},{8,9},{9,8},{10,11... | collective-permute-start | bytes 221192 | tf_op jit(solution)/shard_map/ppermute | solution.py:462

commit v4 on v3

--- a/solution.py
+++ b/solution.py
@@ -99,7 +99,7 @@
         both[i, 32:64] = tracer[:, second, :].astype(BF)
         both[i, 64:96] = jnp.concatenate([mixing[:, rim, :], zero], axis=0).astype(BF)
     leaving[0:32] = own[...].astype(BF)
-    leaving[32:128] = both[jnp.where(quarter[0] >= 2, 0, 1)]
+    leaving[32:128] = both[1 - (quarter[0] & 1)]
     for copy in small:
         copy.wait()
     lane = lax.broadcasted_iota(jnp.int32, (4, LANES), 1)
@@ -146,26 +146,21 @@
         copy.wait()
 
 
-def quad_edges(quarter, leaving, both, arrived, message):
+def pair_edges(quarter, leaving, both, opposite, outer, _after, message):
     mine = quarter[0]
     message[0:32] = leaving[0:32]
-    message[32:64] = arrived[0:32]
+    message[32:64] = opposite[0:32]
+    message[64:96] = outer[0:32]
+    message[96:192] = both[mine & 1]
     ends = (mine == 0) | (mine == 3)
 
     @pl.when(ends)
     def _():
-        message[64:160] = arrived[32:128]
+        message[192:288] = opposite[32:128]
 
     @pl.when(jnp.logical_not(ends))
     def _():
-        message[64:160] = both[(mine + 1) & 1]
-
-
-def pair_edges(quarter, leaving, both, opposite, _after, message):
-    message[0:32] = leaving[0:32]
-    message[32:96] = opposite[0:64]
-    message[96:192] = both[quarter[0] & 1]
-    message[192:288] = opposite[64:160]
+        message[192:288] = outer[32:128]
 
 
 def edge_sides(mine, partner):
@@ -175,11 +170,11 @@
     return jnp.where(first, far_edge, near_edge), jnp.where(first, near_edge, far_edge)
 
 
-def strips(mine, opposite, partner):
+def strips(mine, opposite, outer, partner):
     first = (mine & 1) == 0
     low = mine < 2
     beside = partner[0:32].astype(F32)
-    ours = (opposite[0:32].astype(F32), opposite[32:64].astype(F32))
+    ours = (opposite[0:32].astype(F32), outer[0:32].astype(F32))
     theirs = (partner[32:64].astype(F32), partner[64:96].astype(F32))
     prev_own = jnp.where(low, ours[1], ours[0])
     prev_other = jnp.where(low, theirs[1], theirs[0])
@@ -192,7 +187,7 @@
     return before2, before, after, after2
 
 
-def sort_terms(place, received, _arrived, message, rows_named):
+def sort_terms(place, received, message, rows_named):
     spot = place[0]
     lines = lax.broadcasted_iota(jnp.int32, (4 * SLAB, LANES), 0)
     line_row = (lines >> 6) * 512 + spot * 32 - 16 + (lines & (SLAB - 1))
@@ -209,25 +204,33 @@
             part = jnp.dot(picks, some, preferred_element_type=F32)
             sums[f] = part if sums[f] is None else sums[f] + part
     for c in range(4):
-        for s in range(4):
-            base = c * SLAB + 16 + s * ROWS
-            pieces = []
-            for f in (1, 2, 3):
-                for o in (0, 8, 16, -16, -8):
-                    piece = sums[f][base + o : base + o + ROWS]
-                    if f == 1 and o == 16:
-                        piece = jnp.where(last, north(sums[0][base + 8 : base + 16]), piece)
-                    if f == 1 and o == -16:
-                        piece = jnp.where(head, south(sums[0][base - 8 : base]), piece)
-                    pieces.append(piece)
-            pieces.append(sums[0][base : base + ROWS])
-            message[c * 4 + s] = jnp.concatenate(pieces, axis=0).astype(BF)
-
-
-def first_step(quarter, tracer, mixing, own, opposite, partner, base, reply, factors, halo, mix_halo, work):
+        for h in range(2):
+            base = c * SLAB + 16 + h * 16
+            heat, rain, push_e, push_n = (
+                sums[f][base - 16 : base + 32] for f in range(4)
+            )
+            pieces = [
+                jnp.where(head, south(heat[8:16]), rain[0:8]),
+                rain[8:40],
+                jnp.where(last, north(heat[32:40]), rain[40:48]),
+                push_e,
+                push_n,
+                heat[16:32],
+            ]
+            message[c * 2 + h] = jnp.concatenate(pieces, axis=0).astype(BF)
+
+
+def add_up(received, total):
+    some = received[0].astype(F32)
+    for p in range(1, 8):
+        some = some + received[p].astype(F32)
+    total[...] = some
+
+
+def first_step(quarter, tracer, mixing, own, opposite, outer, partner, base, reply, factors, halo, mix_halo, work):
     mine = quarter[0]
     before, after = edge_sides(mine, partner)
-    _, wet_before, wet_after, _ = (strip[24:32] for strip in strips(mine, opposite, partner))
+    _, wet_before, wet_after, _ = (strip[24:32] for strip in strips(mine, opposite, outer, partner))
     halo[...] = jnp.zeros_like(halo)
     mix_halo[...] = jnp.zeros_like(mix_halo)
     halo[pl.ds(0, LEVELS, stride=ROWS), :] = after[0:32]
@@ -279,23 +282,28 @@
 
 
 def ocean(
-    quarter, flux, own, opposite, partner, base, reply, factors,
+    quarter, flux, flux_beside, own, opposite, outer, partner, base, reply, factors,
     tracer_out, height_out, message, work,
 ):
     mine = quarter[0]
-    before2, before, after, after2 = strips(mine, opposite, partner)
+    before2, before, after, after2 = strips(mine, opposite, outer, partner)
 
     def ring(i, own):
         r = slice(i * ROWS, (i + 1) * ROWS)
         return jnp.concatenate([own, after[r], after2[r], before2[r], before[r]], axis=0)
 
-    total = flux[0].astype(F32)
-    for p in range(1, GROUP):
-        total = total + flux[p].astype(F32)
+    first = (mine & 1) == 0
+    total = flux[...] + flux_beside[...]
+
+    def window(start):
+        blocks = [total[start + i * ROWS : start + (i + 1) * ROWS] for i in range(6)]
+        parts = [jnp.where(first, blocks[i], blocks[i + 1]) for i in (2, 3, 4, 0, 1)]
+        return jnp.concatenate(parts, axis=0)
+
     wet = ring(3, own[24:32])
-    rain = fresh_gain * total[0:40] * wet
-    push_e = stress_gain * total[40:80]
-    push_n = stress_gain * total[80:120]
+    rain = fresh_gain * window(0) * wet
+    push_e = stress_gain * window(48)
+    push_n = stress_gain * window(96)
     h = ring(0, own[0:8])
     flow_e = ring(1, own[8:16])
     flow_n = ring(2, own[16:24])
@@ -314,9 +322,11 @@
     wet16 = jnp.concatenate([wet[0:ROWS], jnp.where(
         lax.broadcasted_iota(jnp.int32, (ROWS, LANES), 0) < 4, wet[8:16], wet[32:40])], axis=0)
     tile = lax.broadcasted_iota(jnp.int32, (ROWS, LANES), 0)
-    after_heat = jnp.where(tile == 0, south(total[16:24]), 0.0)
-    before_heat = jnp.where(tile == ROWS - 1, north(total[24:32]), 0.0)
-    heat = jnp.concatenate([total[120:128], after_heat + before_heat], axis=0)
+    heat_low, heat_high = total[144:152], total[152:160]
+    after_heat = jnp.where(first, heat_high, south(total[40:48]))
+    before_heat = jnp.where(first, north(total[0:8]), heat_low)
+    halo_heat = jnp.where(tile == 0, after_heat, jnp.where(tile == ROWS - 1, before_heat, 0.0))
+    heat = jnp.concatenate([jnp.where(first, heat_low, heat_high), halo_heat], axis=0)
     warm = heating_gain * heat * wet16
     fe, fw, fn, fs = face_e[0:ROWS], face_w[0:ROWS], face_n[0:ROWS], face_s[0:ROWS]
     solved = None
@@ -434,31 +444,26 @@
         latitude[0].T, airside[0], matrices[0],
     )
     leaving, both, own, weights = map(near, (leaving, both, own, weights))
+    first = near(lax.all_to_all(first, PLANE, 0, 0, tiled=True))
+    opposite = near(lax.ppermute(leaving, ALL, [(i, i ^ 2) for i in range(count)]))
     pairs = []
     for i in range(count):
-        j = i + 4 if i & 2 else i - 4
+        j = i + 2 if i & 2 else i - 2
         if 0 <= j < count:
             pairs.append((i, j))
-    arrived = near(lax.ppermute(leaving, ALL, pairs))
-    first = near(lax.all_to_all(first, PLANE, 0, 0, tiled=True))
-
-    opposite = call(
-        quad_edges, inside((160, LANES), BF), [smem] + [vmem] * 3
-    )(quarter, leaving, both, arrived)
-    leaving_quad = opposite
-    opposite = near(lax.ppermute(leaving_quad, ALL, [(i, i ^ 2) for i in range(count)]))
+    outer = near(lax.ppermute(leaving, ALL, pairs))
 
     second, rows_named = call(
-        sort_terms,
-        (inside((GROUP, 128, LANES), BF), inside((ROWS, LANES), F32)),
-        [smem, vmem, vmem],
-    )(place, first, near(leaving_quad))
+        sort_terms, (inside((8, 160, LANES), BF), inside((ROWS, LANES), F32)), [smem, vmem]
+    )(place, first)
     rows_named = near(rows_named)
-    second = near(lax.all_to_all(second, LINE, 0, 0, tiled=True))
+    second = near(lax.all_to_all(second, ("c", "h"), 0, 0, tiled=True))
+    flux = near(call(add_up, inside((160, LANES), F32), [vmem])(second))
+    flux_beside = near(lax.ppermute(flux, ALL, [(i, i ^ 1) for i in range(count)]))
 
     partner = call(
-        pair_edges, inside((288, LANES), BF), [smem] + [vmem] * 4
-    )(quarter, leaving, both, opposite, rows_named)
+        pair_edges, inside((288, LANES), BF), [smem] + [vmem] * 5
+    )(quarter, leaving, both, opposite, outer, rows_named)
     partner = near(lax.ppermute(partner, ALL, [(i, i ^ 1) for i in range(count)]))
 
     base, reply, factors = call(
@@ -468,13 +473,13 @@
             inside((LEVELS, 2 * ROWS, LANES), F32),
             inside((3, LEVELS, ROWS, LANES), F32),
         ),
-        [smem] + [vmem] * 5,
+        [smem] + [vmem] * 6,
         [
             pltpu.VMEM((LEVELS * ROWS, LANES), F32),
             pltpu.VMEM((LEVELS * ROWS, LANES), F32),
             pltpu.VMEM((LEVELS, 2 * ROWS, LANES), F32),
         ],
-    )(quarter, tracer, mixing, own, opposite, partner)
+    )(quarter, tracer, mixing, own, opposite, outer, partner)
 
     tracer_new, height_new, third = call(
         ocean,
@@ -483,9 +488,9 @@
             inside((ROWS, LANES), F32),
             inside((GROUP, 16, LANES), BF),
         ),
-        [smem] + [vmem] * 7,
+        [smem] + [vmem] * 9,
         [pltpu.VMEM((LEVELS, ROWS, LANES), F32)],
-    )(quarter, second, own, opposite, partner, near(base), near(reply), near(factors))
+    )(quarter, flux, flux_beside, own, opposite, outer, partner, near(base), near(reply), near(factors))
     third = near(lax.all_to_all(third, LINE, 0, 0, tiled=True))
 
     fourth = call(

time: 80.5 us -> 78.8 us (0.979)
  blocking collectives: 22.4 us -> 43.7 us
  waiting for transfers between devices: 22.6 us -> 2.61 us
  starting transfers between devices: 26.7 us -> 23.9 us
    all_to_all x0 -> x1, blocking collectives: none -> 18.9 us  [shards(): first = near(lax.all_to_all(first, PLANE, 0, 0, tiled=True))]
    ppermute x2 -> x3, waiting for transfers between devices: 19.1 us -> 1.7 us  [the longest x1 1.69 us: shards(): lax.ppermute(leaving, ALL, [(i, i ^ 2) for i in range(count)])]
    all_to_all x2 -> x1, starting transfers between devices: 18.6 us -> 8.19 us  [shards(): second = near(lax.all_to_all(second, ('c', 'h'), 0, 0, tiled=True))]
    ppermute x2 -> x3, starting transfers between devices: 6.64 us -> 11.9 us  [the longest x1 6.82 us: shards(): lax.ppermute(leaving, ALL, [(i, i ^ 2) for i in range(count)])]
    all_to_all x2 -> x1, waiting for transfers between devices: 2.61 us -> 0.01 us  [shards(): second = near(lax.all_to_all(second, ('c', 'h'), 0, 0, tiled=True))]
    ppermute x1, starting transfers between devices: 1.46 us -> 3.77 us  [shards(): lax.ppermute(partner, ALL, [(i, i ^ 1) for i in range(count)])]
    all_to_all x1, blocking collectives: 11.2 us -> 12.8 us  [shards(): fourth = near(lax.all_to_all(fourth, PLANE, 0, 0, tiled=True))]
  transfers between devices with their start and end apart: 5 -> 5, of which waited for: 4 -> 2; matrix products, arithmetic and copies ran while one was open for 0% -> 0% of each run, Pallas kernels for 1% -> 1%
where the time goes in v4:
time: 78.8 us; the launch traced here: 78.4 us
  blocking collectives  43.7 us (55%)
  starting transfers between devices  23.9 us (30%)
  Pallas kernels  7.62 us (10%)
  waiting for transfers between devices  2.61 us (3%)
    all_to_all x1, blocking collectives, shards(): first = near(lax.all_to_all(first, PLANE, 0, 0, tiled=True))  18.9 us
    all_to_all x1, blocking collectives, shards(): fourth = near(lax.all_to_all(fourth, PLANE, 0, 0, tiled=True))  12.8 us
    all_to_all x1, blocking collectives, shards(): third = near(lax.all_to_all(third, LINE, 0, 0, tiled=True))  11.9 us
    all_to_all x1, starting transfers between devices, shards(): second = near(lax.all_to_all(second, ('c', 'h'), 0, 0, tiled=True))  8.19 us
    ppermute x1, starting transfers between devices, shards(): lax.ppermute(leaving, ALL, [(i, i ^ 2) for i in range(count)])  6.82 us
    ppermute x1, starting transfers between devices, shards(): lax.ppermute(flux, ALL, [(i, i ^ 1) for i in range(count)])  4.43 us
    ppermute x1, starting transfers between devices, shards(): lax.ppermute(partner, ALL, [(i, i ^ 1) for i in range(count)])  3.77 us
    pallas_call x1, Pallas kernels, shards(): call(prepare, (inside((128, LANES), BF), inside((2, 96, LANES), BF), insi...  2.8 us
  transfers between devices with their start and end apart: 5, of which 2 were waited for; matrix products, arithmetic and copies ran while one was open for 0% of the time, Pallas kernels for 1%

profile of v4, /device:TPU:1, one launch (start us, length us, event | category | flops | bytes accessed | tf_op | source)
XLA Modules:
  0.0 78.4 jit_solution(5986608043543535993)
XLA Ops:
  0.6 2.8 %shard_map.103 = (bf16[128,128]{1,0:T(8,128)(2,1)S(1)}, bf16[2,96,128]{2,1,0:T(8,128)(2,1)S(1)}, f32[32,128]{1,0:T(8,128)S(1)}, bf16[8,4,128,128]{3,2,1,0:T(8,128)(2,1)S(1)}, bf16[16,144,128]{2,1,0:T(8,128)(2,1)}) custom-call(s32[1]{0:T(128)} %bitcast.place, s32[1]{0:T(128)} %bitcast.1.quarter, f32[32,8,128]{2,1,0:T(8,128)} %tracer.1, f32[31,8,128]{2,1,0:T(8,128)} %mixing.1, ...), custom_call_target="tpu_custom_call" | custom-call | tf_op jit(solution)/shard_map/pallas_call | solution.py:420
  3.4 18.9 %all_to_all.20.received = bf16[16,144,128]{2,1,0:T(8,128)(2,1)S(1)} all-to-all(bf16[16,144,128]{2,1,0:T(8,128)(2,1)} %get-tuple-element.19), channel_id=1, replica_groups=mesh['c'=4,'y'=4,'x'=4,'h'=2,'k'=2] {'y','x'}, dimensions={0} | all-to-all | bytes 1179648 | tf_op jit(solution)/shard_map/all_to_all | solution.py:447
  22.4 1.1 %shard_map.104 = (bf16[8,160,128]{2,1,0:T(8,128)(2,1)}, f32[8,128]{1,0:T(8,128)S(1)}) custom-call(s32[1]{0:T(128)} %bitcast.place, bf16[16,144,128]{2,1,0:T(8,128)(2,1)S(1)} %all_to_all.20.received), custom_call_target="tpu_custom_call" | custom-call | tf_op jit(solution)/shard_map/pallas_call | solution.py:456
  23.5 8.2 %all-to-all-start.1 = ((bf16[8,160,128]{2,1,0:T(8,128)(2,1)}), bf16[8,160,128]{2,1,0:T(8,128)(2,1)S(1)}, u32[]{:S(2)}, u32[]{:S(2)}) async-start(bf16[8,160,128]{2,1,0:T(8,128)(2,1)} %get-tuple-element.21), calls=%async_computation.1 | async-start | bytes 655360 | tf_op jit(solution)/shard_map/all_to_all | solution.py:460
  31.7 0.7 collective-permute-start.2
  32.3 6.8 %collective-permute-start.1 = (bf16[128,128]{1,0:T(8,128)(2,1)S(1)}, bf16[128,128]{1,0:T(8,128)(2,1)S(1)}, u32[]{:S(2)}, u32[]{:S(2)}) collective-permute-start(bf16[128,128]{1,0:T(8,128)(2,1)S(1)} %get-tuple-element.23.leaving), channel_id=1, source_target_pairs={{0,2},{1,3},{2,0},{3,1},{4,6},{5,7},{6,4},{7,5},{8,10},{9,11},{10,... | collective-permute-start | bytes 98312 | tf_op jit(solution)/shard_map/ppermute | solution.py:448
  39.2 0.0 all-to-all-done.1.received
  39.2 0.0 copy-start.1
  39.2 0.0 copy-start
  39.2 4.4 %collective-permute-start = (f32[160,128]{1,0:T(8,128)S(1)}, f32[160,128]{1,0:T(8,128)S(1)}, u32[]{:S(2)}, u32[]{:S(2)}) collective-permute-start(f32[160,128]{1,0:T(8,128)S(1)} %shard_map.105.flux), channel_id=1, source_target_pairs={{0,1},{1,0},{2,3},{3,2},{4,5},{5,4},{6,7},{7,6},{8,9},{9,8},{10,11... | collective-permute-start | bytes 245768 | tf_op jit(solution)/shard_map/ppermute | solution.py:462
  43.7 0.0 collective-permute-done.2.outer
  43.7 1.7 %collective-permute-done.1.opposite = bf16[128,128]{1,0:T(8,128)(2,1)S(1)} collective-permute-done((bf16[128,128]{1,0:T(8,128)(2,1)S(1)}, bf16[128,128]{1,0:T(8,128)(2,1)S(1)}, u32[]{:S(2)}, u32[]{:S(2)}) %collective-permute-start.1) | collective-permute-done | bytes 32800 | tf_op jit(solution)/shard_map/ppermute | solution.py:448
  45.4 3.8 %collective-permute-start.3 = (bf16[288,128]{1,0:T(8,128)(2,1)S(1)}, bf16[288,128]{1,0:T(8,128)(2,1)S(1)}, u32[]{:S(2)}, u32[]{:S(2)}) collective-permute-start(bf16[288,128]{1,0:T(8,128)(2,1)S(1)} %shard_map.106), channel_id=1, source_target_pairs={{0,1},{1,0},{2,3},{3,2},{4,5},{5,4},{6,7},{7,6},{8,9},{9,8},{10,11... | collective-permute-start | bytes 221192 | tf_op jit(solution)/shard_map/ppermute | solution.py:467
  49.1 0.9 %collective-permute-done.3.partner = bf16[288,128]{1,0:T(8,128)(2,1)S(1)} collective-permute-done((bf16[288,128]{1,0:T(8,128)(2,1)S(1)}, bf16[288,128]{1,0:T(8,128)(2,1)S(1)}, u32[]{:S(2)}, u32[]{:S(2)}) %collective-permute-start.3) | collective-permute-done | bytes 73760 | tf_op jit(solution)/shard_map/ppermute | solution.py:467
  50.0 0.0 copy-done.1
  50.0 0.0 copy-done
  50.1 0.5 shard_map.107
  50.5 0.0 collective-permute-done.flux_beside
  50.5 1.4 %shard_map.108 = (f32[32,8,128]{2,1,0:T(8,128)S(1)}, f32[8,128]{1,0:T(8,128)S(1)}, bf16[16,16,128]{2,1,0:T(8,128)(2,1)S(1)}) custom-call(s32[1]{0:T(128)} %bitcast.1.quarter, f32[160,128]{1,0:T(8,128)S(1)} %shard_map.105.flux, f32[160,128]{1,0:T(8,128)S(1)} %collective-permute-done.flux_beside, f32[32,128]{1,0:T(8,128)S(1)} %get-tuple-element.22.own, ...), custom_call_target="tpu_custom_call" | custom-call | tf_op jit(solution)/shard_map/pallas_call | solution.py:484
  51.9 11.9 %all_to_all.21.received = bf16[16,16,128]{2,1,0:T(8,128)(2,1)S(1)} all-to-all(bf16[16,16,128]{2,1,0:T(8,128)(2,1)S(1)} %get-tuple-element.28), channel_id=1, replica_groups=mesh['c'=4,'y'=4,'x'=4,'h'=2,'k'=2] {'c','h','k'}, dimensions={0} | all-to-all | bytes 131072 | tf_op jit(solution)/shard_map/all_to_all | solution.py:494
  63.8 0.4 shard_map.109
  64.2 12.8 %all_to_all.22.received = bf16[16,64,128]{2,1,0:T(8,128)(2,1)S(1)} all-to-all(bf16[16,64,128]{2,1,0:T(8,128)(2,1)S(1)} %shard_map.109), channel_id=1, replica_groups=mesh['c'=4,'y'=4,'x'=4,'h'=2,'k'=2] {'y','x'}, dimensions={0} | all-to-all | bytes 524288 | tf_op jit(solution)/shard_map/all_to_all | solution.py:499
  77.0 1.4 %shard_map.110 = (bf16[2,1024]{1,0:T(2,128)(2,1)}, f32[32,8,128]{2,1,0:T(8,128)}, f32[8,128]{1,0:T(8,128)}) custom-call(bf16[16,64,128]{2,1,0:T(8,128)(2,1)S(1)} %all_to_all.22.received, bf16[8,4,128,128]{3,2,1,0:T(8,128)(2,1)S(1)} %get-tuple-element.29.weights, f32[32,8,128]{2,1,0:T(8,128)S(1)} %get-tuple-element.30.tracer, ...), custom_call_target="tpu_custom_call" | custom-call | tf_op jit(solution)/shard_map/pallas_call | solution.py:501
  (2 shorter events, 0.1 us)
Async XLA Ops:
  23.5 15.7 %all-to-all-start.1 = ((bf16[8,160,128]{2,1,0:T(8,128)(2,1)}), bf16[8,160,128]{2,1,0:T(8,128)(2,1)S(1)}, u32[]{:S(2)}, u32[]{:S(2)}) async-start(bf16[8,160,128]{2,1,0:T(8,128)(2,1)} %get-tuple-element.21), calls=%async_computation.1 | async-start | bytes 655360 | tf_op jit(solution)/shard_map/all_to_all | solution.py:460
  31.7 12.0 %collective-permute-start.2 = (bf16[128,128]{1,0:T(8,128)(2,1)S(1)}, bf16[128,128]{1,0:T(8,128)(2,1)S(1)}, u32[]{:S(2)}, u32[]{:S(2)}) collective-permute-start(bf16[128,128]{1,0:T(8,128)(2,1)S(1)} %get-tuple-element.23.leaving), channel_id=1, source_target_pairs={{2,4},{3,5},{4,2},{5,3},{6,8},{7,9},{8,6},{9,7},{10,12},{11,13},{1... | collective-permute-start | bytes 98312 | tf_op jit(solution)/shard_map/ppermute | solution.py:454
  32.3 13.0 %collective-permute-start.1 = (bf16[128,128]{1,0:T(8,128)(2,1)S(1)}, bf16[128,128]{1,0:T(8,128)(2,1)S(1)}, u32[]{:S(2)}, u32[]{:S(2)}) collective-permute-start(bf16[128,128]{1,0:T(8,128)(2,1)S(1)} %get-tuple-element.23.leaving), channel_id=1, source_target_pairs={{0,2},{1,3},{2,0},{3,1},{4,6},{5,7},{6,4},{7,5},{8,10},{9,11},{10,... | collective-permute-start | bytes 98312 | tf_op jit(solution)/shard_map/ppermute | solution.py:448
  39.2 10.9 %copy-start.1 = (f32[31,8,128]{2,1,0:T(8,128)S(1)}, f32[31,8,128]{2,1,0:T(8,128)}, u32[]{:S(2)}) copy-start(f32[31,8,128]{2,1,0:T(8,128)} %mixing.1) | copy-start | bytes 380932
  39.2 10.8 %copy-start = (f32[32,8,128]{2,1,0:T(8,128)S(1)}, f32[32,8,128]{2,1,0:T(8,128)}, u32[]{:S(2)}) copy-start(f32[32,8,128]{2,1,0:T(8,128)} %tracer.1) | copy-start | bytes 393220
  39.2 11.3 %collective-permute-start = (f32[160,128]{1,0:T(8,128)S(1)}, f32[160,128]{1,0:T(8,128)S(1)}, u32[]{:S(2)}, u32[]{:S(2)}) collective-permute-start(f32[160,128]{1,0:T(8,128)S(1)} %shard_map.105.flux), channel_id=1, source_target_pairs={{0,1},{1,0},{2,3},{3,2},{4,5},{5,4},{6,7},{7,6},{8,9},{9,8},{10,11... | collective-permute-start | bytes 245768 | tf_op jit(solution)/shard_map/ppermute | solution.py:462
  45.4 4.7 %collective-permute-start.3 = (bf16[288,128]{1,0:T(8,128)(2,1)S(1)}, bf16[288,128]{1,0:T(8,128)(2,1)S(1)}, u32[]{:S(2)}, u32[]{:S(2)}) collective-permute-start(bf16[288,128]{1,0:T(8,128)(2,1)S(1)} %shard_map.106), channel_id=1, source_target_pairs={{0,1},{1,0},{2,3},{3,2},{4,5},{5,4},{6,7},{7,6},{8,9},{9,8},{10,11... | collective-permute-start | bytes 221192 | tf_op jit(solution)/shard_map/ppermute | solution.py:467

commit v5 on v4

--- a/solution.py
+++ b/solution.py
@@ -71,35 +71,25 @@
 
 
 def prepare(
-    place, quarter, tracer_far, mixing_far, height_far, flow_far, wet_far, targets_far, sources_far,
-    weights_far, leaving, both, own, weights, message,
-    tracer, mixing, wet, targets, sources, flat, packet, done,
+    place, tracer_far, mixing_far, height_far, flow_far, wet_far, targets_far, sources_far,
+    weights_far, leaving, own, weights, message,
+    tracer, mixing, wet, targets, sources, flat, packet, done, sent,
 ):
-    def load(source, target, i):
-        copy = pltpu.make_async_copy(source, target, done.at[i])
+    def load(source, target, flag):
+        copy = pltpu.make_async_copy(source, target, flag)
         copy.start()
         return copy
 
+    small = [load(targets_far, targets, done.at[6]), load(sources_far, sources, done.at[7])]
+    large = [load(weights_far.at[s], weights.at[s], done.at[8 + s]) for s in range(8)]
     edges = [
-        load(tracer_far, tracer, 0),
-        load(mixing_far, mixing, 1),
-        load(height_far, own.at[0:8], 2),
-        load(flow_far.at[0], own.at[8:16], 3),
-        load(flow_far.at[1], own.at[16:24], 4),
-        load(wet_far, wet, 5),
+        load(tracer_far, tracer, done.at[0]),
+        load(mixing_far, mixing, done.at[1]),
+        load(height_far, own.at[0:8], done.at[2]),
+        load(flow_far.at[0], own.at[8:16], done.at[3]),
+        load(flow_far.at[1], own.at[16:24], done.at[4]),
+        load(wet_far, wet, done.at[5]),
     ]
-    small = [load(targets_far, targets, 6), load(sources_far, sources, 7)]
-    large = [load(weights_far.at[s], weights.at[s], 8 + s) for s in range(8)]
-    for copy in edges:
-        copy.wait()
-    own[24:32] = wet[...].astype(F32)
-    zero = jnp.zeros((1, LANES), F32)
-    for i, (first, second, rim) in enumerate(((6, 7, 7), (0, 1, 0))):
-        both[i, 0:32] = tracer[:, first, :].astype(BF)
-        both[i, 32:64] = tracer[:, second, :].astype(BF)
-        both[i, 64:96] = jnp.concatenate([mixing[:, rim, :], zero], axis=0).astype(BF)
-    leaving[0:32] = own[...].astype(BF)
-    leaving[32:128] = both[1 - (quarter[0] & 1)]
     for copy in small:
         copy.wait()
     lane = lax.broadcasted_iota(jnp.int32, (4, LANES), 1)
@@ -141,49 +131,58 @@
                         4 * i : 4 * i + 4, j * LANES : (j + 1) * LANES
                     ]
     packet[0:128] = flat[...].astype(BF)
-    sent = [load(packet, message.at[p], p) for p in range(GROUP)]
-    for copy in sent:
+    copies = [load(packet, message.at[p], sent.at[p]) for p in range(GROUP)]
+    for copy in edges:
         copy.wait()
-
-
-def pair_edges(quarter, leaving, both, opposite, outer, _after, message):
+    own[24:32] = wet[...].astype(F32)
+    zero = jnp.zeros((1, LANES), F32)
+    for i, (first, second, rim) in enumerate(((6, 7, 7), (0, 1, 0))):
+        at = 32 + 96 * i
+        leaving[at : at + 32] = tracer[:, first, :].astype(BF)
+        leaving[at + 32 : at + 64] = tracer[:, second, :].astype(BF)
+        leaving[at + 64 : at + 96] = jnp.concatenate(
+            [mixing[:, rim, :], zero], axis=0
+        ).astype(BF)
+    leaving[0:32] = own[...].astype(BF)
+    for copy in copies:
+        copy.wait()
+
+
+def chip_edges(quarter, leaving, beside, message):
     mine = quarter[0]
-    message[0:32] = leaving[0:32]
-    message[32:64] = opposite[0:32]
-    message[64:96] = outer[0:32]
-    message[96:192] = both[mine & 1]
-    ends = (mine == 0) | (mine == 3)
-
-    @pl.when(ends)
-    def _():
-        message[192:288] = opposite[32:128]
-
-    @pl.when(jnp.logical_not(ends))
-    def _():
-        message[192:288] = outer[32:128]
-
-
-def edge_sides(mine, partner):
+    core = mine & 1
+    own = pl.multiple_of(32 * core, 32)
+    other = pl.multiple_of(32 - 32 * core, 32)
+    message[pl.ds(own, 32)] = leaving[0:32]
+    message[pl.ds(other, 32)] = beside[0:32]
+    for i, (source, start) in enumerate(
+        ((beside, 32), (beside, 128), (leaving, 128), (leaving, 32))
+    ):
+
+        @pl.when(mine == i)
+        def _(source=source, start=start):
+            message[64:160] = source[start : start + 96]
+
+
+def edge_sides(mine, beside, mixed, shared):
     first = (mine & 1) == 0
-    near_edge = partner[96:192].astype(F32)
-    far_edge = partner[192:288].astype(F32)
+    near_edge = jnp.where(first, beside[128:224].astype(F32), beside[32:128].astype(F32))
+    far_edge = jnp.where(mine < 2, shared[64:160].astype(F32), mixed[64:160].astype(F32))
     return jnp.where(first, far_edge, near_edge), jnp.where(first, near_edge, far_edge)
 
 
-def strips(mine, opposite, outer, partner):
+def strips(mine, beside, mixed, shared):
     first = (mine & 1) == 0
     low = mine < 2
-    beside = partner[0:32].astype(F32)
-    ours = (opposite[0:32].astype(F32), outer[0:32].astype(F32))
-    theirs = (partner[32:64].astype(F32), partner[64:96].astype(F32))
-    prev_own = jnp.where(low, ours[1], ours[0])
-    prev_other = jnp.where(low, theirs[1], theirs[0])
-    next_own = jnp.where(low, ours[0], ours[1])
-    next_other = jnp.where(low, theirs[0], theirs[1])
-    before2 = prev_own
-    before = jnp.where(first, prev_other, beside)
-    after = jnp.where(first, beside, next_other)
-    after2 = next_own
+    ours, theirs = mixed[0:64].astype(F32), shared[0:64].astype(F32)
+    swap = first == low
+    prev = jnp.where(swap, theirs, ours)
+    follow = jnp.where(swap, ours, theirs)
+    partner = beside[0:32].astype(F32)
+    before2 = jnp.where(first, prev[0:32], prev[32:64])
+    before = jnp.where(first, prev[32:64], partner)
+    after = jnp.where(first, partner, follow[0:32])
+    after2 = jnp.where(first, follow[0:32], follow[32:64])
     return before2, before, after, after2
 
 
@@ -227,10 +226,10 @@
     total[...] = some
 
 
-def first_step(quarter, tracer, mixing, own, opposite, outer, partner, base, reply, factors, halo, mix_halo, work):
+def first_step(quarter, tracer, mixing, own, beside, mixed, shared, base, reply, factors, halo, mix_halo, work):
     mine = quarter[0]
-    before, after = edge_sides(mine, partner)
-    _, wet_before, wet_after, _ = (strip[24:32] for strip in strips(mine, opposite, outer, partner))
+    before, after = edge_sides(mine, beside, mixed, shared)
+    _, wet_before, wet_after, _ = (strip[24:32] for strip in strips(mine, beside, mixed, shared))
     halo[...] = jnp.zeros_like(halo)
     mix_halo[...] = jnp.zeros_like(mix_halo)
     halo[pl.ds(0, LEVELS, stride=ROWS), :] = after[0:32]
@@ -282,11 +281,11 @@
 
 
 def ocean(
-    quarter, flux, flux_beside, own, opposite, outer, partner, base, reply, factors,
+    quarter, flux, flux_beside, own, beside, mixed, shared, base, reply, factors,
     tracer_out, height_out, message, work,
 ):
     mine = quarter[0]
-    before2, before, after, after2 = strips(mine, opposite, outer, partner)
+    before2, before, after, after2 = strips(mine, beside, mixed, shared)
 
     def ring(i, own):
         r = slice(i * ROWS, (i + 1) * ROWS)
@@ -311,7 +310,16 @@
     face_n = wet * north(wet)
     face_w, flow_w, push_w = west(face_e), west(flow_e), west(push_e)
     face_s, flow_s, push_s = south(face_n), south(flow_n), south(push_n)
-    for _ in range(NSTEP * NSUB):
+    for turn in range(NSTEP * NSUB):
+        if turn == NSUB:
+
+            def inner(v):
+                return jnp.concatenate([v[0:16], v[32:40]], axis=0)
+
+            h, flow_e, flow_w, flow_n, flow_s = map(inner, (h, flow_e, flow_w, flow_n, flow_s))
+            face_e, face_w, face_n, face_s = map(inner, (face_e, face_w, face_n, face_s))
+            push_e, push_w, push_n, push_s = map(inner, (push_e, push_w, push_n, push_s))
+            rain = inner(rain)
         flow_e = face_e * (flow_e - wave_gain * (east(h) - h) + push_e)
         flow_w = face_w * (flow_w - wave_gain * (h - west(h)) + push_w)
         flow_n = face_n * (flow_n - wave_gain * (north(h) - h) + push_n)
@@ -371,7 +379,7 @@
             message[4 * q : 4 * q + 4, f * 32 : f * 32 + 32, :] = out.reshape(4, 32, LANES)
 
 
-def finish(received, weights, tracer, height, out, tracer_out, height_out, flat, done):
+def finish(received, weights, tracer, height, out_far, tracer_out, height_out, flat, out, done):
     saves = [
         pltpu.make_async_copy(tracer, tracer_out, done.at[0]),
         pltpu.make_async_copy(height, height_out, done.at[1]),
@@ -407,7 +415,9 @@
             answer = part if answer is None else answer + part
         out[:, s * LANES : (s + 1) * LANES] = answer[0:2, 0:LANES].astype(BF)
         out[:, (s + 1) * LANES : (s + 2) * LANES] = answer[2:4, LANES:].astype(BF)
-    for save in saves:
+    last = pltpu.make_async_copy(out, out_far, done.at[2])
+    last.start()
+    for save in (*saves, last):
         save.wait()
 
 
@@ -417,16 +427,15 @@
     place, quarter = spot.reshape(1), turn.reshape(1)
     count = lax.axis_size(ALL)
 
-    leaving, both, own, weights, first = call(
+    leaving, own, weights, first = call(
         prepare,
         (
-            inside((128, LANES), BF),
-            inside((2, 96, LANES), BF),
+            inside((224, LANES), BF),
             inside((32, LANES), F32),
             inside((8, 4, LANES, LANES), BF),
             shaped((GROUP, 144, LANES), BF),
         ),
-        [smem, smem] + [far] * 8,
+        [smem] + [far] * 8,
         [
             pltpu.VMEM((LEVELS, ROWS, LANES), F32),
             pltpu.VMEM((LEVELS - 1, ROWS, LANES), F32),
@@ -436,22 +445,28 @@
             pltpu.VMEM((4 * TERMS, LANES), F32),
             pltpu.VMEM((144, LANES), BF),
             pltpu.SemaphoreType.DMA((16,)),
+            pltpu.SemaphoreType.DMA((16,)),
         ],
-        out_specs=(vmem, vmem, vmem, vmem, far),
+        out_specs=(vmem, vmem, vmem, far),
         room=60 * 1024,
     )(
-        place, quarter, tracer, mixing, height, flow, marine,
+        place, tracer, mixing, height, flow, marine,
         latitude[0].T, airside[0], matrices[0],
     )
-    leaving, both, own, weights = map(near, (leaving, both, own, weights))
+    leaving, own, weights = map(near, (leaving, own, weights))
     first = near(lax.all_to_all(first, PLANE, 0, 0, tiled=True))
-    opposite = near(lax.ppermute(leaving, ALL, [(i, i ^ 2) for i in range(count)]))
+    flip = [(i, i ^ 1) for i in range(count)]
     pairs = []
     for i in range(count):
-        j = i + 2 if i & 2 else i - 2
+        up = bool(i & 2) == bool(i & 1)
+        j = i + 2 if up else i - 2
         if 0 <= j < count:
             pairs.append((i, j))
-    outer = near(lax.ppermute(leaving, ALL, pairs))
+    beside = near(lax.ppermute(leaving, ALL, flip))
+    mixed = call(
+        chip_edges, inside((160, LANES), BF), [smem] + [vmem] * 2
+    )(quarter, leaving, beside)
+    mixed = near(lax.ppermute(near(mixed), ALL, pairs))
 
     second, rows_named = call(
         sort_terms, (inside((8, 160, LANES), BF), inside((ROWS, LANES), F32)), [smem, vmem]
@@ -459,12 +474,9 @@
     rows_named = near(rows_named)
     second = near(lax.all_to_all(second, ("c", "h"), 0, 0, tiled=True))
     flux = near(call(add_up, inside((160, LANES), F32), [vmem])(second))
-    flux_beside = near(lax.ppermute(flux, ALL, [(i, i ^ 1) for i in range(count)]))
-
-    partner = call(
-        pair_edges, inside((288, LANES), BF), [smem] + [vmem] * 5
-    )(quarter, leaving, both, opposite, outer, rows_named)
-    partner = near(lax.ppermute(partner, ALL, [(i, i ^ 1) for i in range(count)]))
+    flux_beside = near(lax.ppermute(flux, ALL, flip))
+
+    shared = near(lax.ppermute(mixed, ALL, flip))
 
     base, reply, factors = call(
         first_step,
@@ -479,7 +491,7 @@
             pltpu.VMEM((LEVELS * ROWS, LANES), F32),
             pltpu.VMEM((LEVELS, 2 * ROWS, LANES), F32),
         ],
-    )(quarter, tracer, mixing, own, opposite, outer, partner)
+    )(quarter, tracer, mixing, own, beside, mixed, shared)
 
     tracer_new, height_new, third = call(
         ocean,
@@ -490,7 +502,7 @@
         ),
         [smem] + [vmem] * 9,
         [pltpu.VMEM((LEVELS, ROWS, LANES), F32)],
-    )(quarter, flux, flux_beside, own, opposite, outer, partner, near(base), near(reply), near(factors))
+    )(quarter, flux, flux_beside, own, beside, mixed, shared, near(base), near(reply), near(factors))
     third = near(lax.all_to_all(third, LINE, 0, 0, tiled=True))
 
     fourth = call(
@@ -506,8 +518,12 @@
             shaped((ROWS, LANES), F32),
         ),
         [vmem] * 4,
-        [pltpu.VMEM((2 * TERMS, LANES), F32), pltpu.SemaphoreType.DMA((2,))],
-        out_specs=(vmem, far, far),
+        [
+            pltpu.VMEM((2 * TERMS, LANES), F32),
+            pltpu.VMEM((2, 8 * LANES), BF),
+            pltpu.SemaphoreType.DMA((3,)),
+        ],
+        out_specs=(far, far, far),
     )(fourth, weights, near(tracer_new), near(height_new))
     return tracer_new, height_new, returned[None]
 

time: 78.8 us -> 78.9 us (level)
  starting transfers between devices: 23.9 us -> 19 us
  blocking collectives: 43.7 us -> 46.5 us
  waiting for transfers between devices: 2.61 us -> 5.11 us
    ppermute x4, starting transfers between devices: 15.7 us -> 10.8 us  [the longest x1 4.34 us: shards(): flux_beside = near(lax.ppermute(flux, ALL, flip))]
    all_to_all x1, waiting for transfers between devices: 0.01 us -> 3.34 us  [shards(): second = near(lax.all_to_all(second, ('c', 'h'), 0, 0, tiled=True))]
    all_to_all x1, blocking collectives: 11.9 us -> 14.2 us  [shards(): third = near(lax.all_to_all(third, LINE, 0, 0, tiled=True))]
    ppermute x4, waiting for transfers between devices: 2.61 us -> 1.77 us  [the longest x1 0.89 us: shards(): beside = near(lax.ppermute(leaving, ALL, flip))]
  transfers between devices with their start and end apart: 5 -> 5, of which waited for: 2 -> 3; matrix products, arithmetic and copies ran while one was open for 0% -> 0% of each run, Pallas kernels for 1% -> 1%
where the time goes in v5:
time: 78.9 us; the launch traced here: 78.5 us
  blocking collectives  46.5 us (59%)
  starting transfers between devices  19 us (24%)
  Pallas kernels  7.15 us (9%)
  waiting for transfers between devices  5.11 us (6%)
    all_to_all x1, blocking collectives, shards(): first = near(lax.all_to_all(first, PLANE, 0, 0, tiled=True))  18.9 us
    all_to_all x1, blocking collectives, shards(): third = near(lax.all_to_all(third, LINE, 0, 0, tiled=True))  14.2 us
    all_to_all x1, blocking collectives, shards(): fourth = near(lax.all_to_all(fourth, PLANE, 0, 0, tiled=True))  13.4 us
    all_to_all x1, starting transfers between devices, shards(): second = near(lax.all_to_all(second, ('c', 'h'), 0, 0, tiled=True))  8.2 us
    ppermute x1, starting transfers between devices, shards(): flux_beside = near(lax.ppermute(flux, ALL, flip))  4.34 us
    ppermute x1, starting transfers between devices, shards(): shared = near(lax.ppermute(mixed, ALL, flip))  3.5 us
    all_to_all x1, waiting for transfers between devices, shards(): second = near(lax.all_to_all(second, ('c', 'h'), 0, 0, tiled=True))  3.34 us
    pallas_call x1, Pallas kernels, shards(): call(prepare, (inside((224, LANES), BF), inside((32, LANES), F32), inside...  2.75 us
  transfers between devices with their start and end apart: 5, of which 3 were waited for; matrix products, arithmetic and copies ran while one was open for 0% of the time, Pallas kernels for 1%

profile of v5, /device:TPU:1, one launch (start us, length us, event | category | flops | bytes accessed | tf_op | source)
XLA Modules:
  0.0 78.5 jit_solution(1339487573685575088)
XLA Ops:
  0.6 2.7 %shard_map.103 = (bf16[224,128]{1,0:T(8,128)(2,1)S(1)}, f32[32,128]{1,0:T(8,128)S(1)}, bf16[8,4,128,128]{3,2,1,0:T(8,128)(2,1)S(1)}, bf16[16,144,128]{2,1,0:T(8,128)(2,1)}) custom-call(s32[1]{0:T(128)} %bitcast.place, f32[32,8,128]{2,1,0:T(8,128)} %tracer.1, f32[31,8,128]{2,1,0:T(8,128)} %mixing.1, f32[8,128]{1,0:T(8,128)} %height_far.1, ...), custom_call_target="tpu_custom_call" | custom-call | tf_op jit(solution)/shard_map/pallas_call | solution.py:430
  3.4 18.9 %all_to_all.20.received = bf16[16,144,128]{2,1,0:T(8,128)(2,1)S(1)} all-to-all(bf16[16,144,128]{2,1,0:T(8,128)(2,1)} %get-tuple-element.18), channel_id=1, replica_groups=mesh['c'=4,'y'=4,'x'=4,'h'=2,'k'=2] {'y','x'}, dimensions={0} | all-to-all | bytes 1179648 | tf_op jit(solution)/shard_map/all_to_all | solution.py:457
  22.3 1.1 %shard_map.104 = (bf16[8,160,128]{2,1,0:T(8,128)(2,1)}, f32[8,128]{1,0:T(8,128)S(1)}) custom-call(s32[1]{0:T(128)} %bitcast.place, bf16[16,144,128]{2,1,0:T(8,128)(2,1)S(1)} %all_to_all.20.received), custom_call_target="tpu_custom_call" | custom-call | tf_op jit(solution)/shard_map/pallas_call | solution.py:471
  23.4 8.2 %all-to-all-start.1 = ((bf16[8,160,128]{2,1,0:T(8,128)(2,1)}), bf16[8,160,128]{2,1,0:T(8,128)(2,1)S(1)}, u32[]{:S(2)}, u32[]{:S(2)}) async-start(bf16[8,160,128]{2,1,0:T(8,128)(2,1)} %get-tuple-element.20), calls=%async_computation.1 | async-start | bytes 655360 | tf_op jit(solution)/shard_map/all_to_all | solution.py:475
  31.6 2.2 %collective-permute-start.1 = (bf16[224,128]{1,0:T(8,128)(2,1)S(1)}, bf16[224,128]{1,0:T(8,128)(2,1)S(1)}, u32[]{:S(2)}, u32[]{:S(2)}) collective-permute-start(bf16[224,128]{1,0:T(8,128)(2,1)S(1)} %get-tuple-element.22.leaving), channel_id=1, source_target_pairs={{0,1},{1,0},{2,3},{3,2},{4,5},{5,4},{6,7},{7,6},{8,9},{9,8},{10,11... | collective-permute-start | bytes 172040 | tf_op jit(solution)/shard_map/ppermute | solution.py:465
  33.8 0.9 %collective-permute-done.1.beside = bf16[224,128]{1,0:T(8,128)(2,1)S(1)} collective-permute-done((bf16[224,128]{1,0:T(8,128)(2,1)S(1)}, bf16[224,128]{1,0:T(8,128)(2,1)S(1)}, u32[]{:S(2)}, u32[]{:S(2)}) %collective-permute-start.1) | collective-permute-done | bytes 57376 | tf_op jit(solution)/shard_map/ppermute | solution.py:465
  34.7 0.0 copy-start
  34.7 0.0 copy-start.1
  34.7 0.8 %collective-permute-start.2 = (bf16[160,128]{1,0:T(8,128)(2,1)S(1)}, bf16[160,128]{1,0:T(8,128)(2,1)S(1)}, u32[]{:S(2)}, u32[]{:S(2)}) collective-permute-start(bf16[160,128]{1,0:T(8,128)(2,1)S(1)} %shard_map.106), channel_id=1, source_target_pairs={{0,2},{2,0},{3,5},{4,6},{5,3},{6,4},{7,9},{8,10},{9,7},{10,8},{11,... | collective-permute-start | bytes 122888 | tf_op jit(solution)/shard_map/ppermute | solution.py:469
  35.5 3.3 %all-to-all-done.1.received = bf16[8,160,128]{2,1,0:T(8,128)(2,1)S(1)} async-done(((bf16[8,160,128]{2,1,0:T(8,128)(2,1)}), bf16[8,160,128]{2,1,0:T(8,128)(2,1)S(1)}, u32[]{:S(2)}, u32[]{:S(2)}) %all-to-all-start.1) | async-done | bytes 327712 | tf_op jit(solution)/shard_map/all_to_all | solution.py:475
  38.9 4.3 %collective-permute-start = (f32[160,128]{1,0:T(8,128)S(1)}, f32[160,128]{1,0:T(8,128)S(1)}, u32[]{:S(2)}, u32[]{:S(2)}) collective-permute-start(f32[160,128]{1,0:T(8,128)S(1)} %shard_map.105.flux), channel_id=1, source_target_pairs={{0,1},{1,0},{2,3},{3,2},{4,5},{5,4},{6,7},{7,6},{8,9},{9,8},{10,11... | collective-permute-start | bytes 245768 | tf_op jit(solution)/shard_map/ppermute | solution.py:477
  43.3 0.0 collective-permute-done.2.mixed
  43.3 3.5 %collective-permute-start.3 = (bf16[160,128]{1,0:T(8,128)(2,1)S(1)}, bf16[160,128]{1,0:T(8,128)(2,1)S(1)}, u32[]{:S(2)}, u32[]{:S(2)}) collective-permute-start(bf16[160,128]{1,0:T(8,128)(2,1)S(1)} %collective-permute-done.2.mixed), channel_id=1, source_target_pairs={{0,1},{1,0},{2,3},{3,2},{4,5},{5,4},{6,7},{7,6},{8,9},{9,8},{10,11... | collective-permute-start | bytes 122888 | tf_op jit(solution)/shard_map/ppermute | solution.py:479
  46.8 0.9 %collective-permute-done.3.shared = bf16[160,128]{1,0:T(8,128)(2,1)S(1)} collective-permute-done((bf16[160,128]{1,0:T(8,128)(2,1)S(1)}, bf16[160,128]{1,0:T(8,128)(2,1)S(1)}, u32[]{:S(2)}, u32[]{:S(2)}) %collective-permute-start.3) | collective-permute-done | bytes 40992 | tf_op jit(solution)/shard_map/ppermute | solution.py:479
  47.6 0.0 copy-done
  47.6 0.0 copy-done.1
  47.6 0.5 shard_map.107
  48.1 0.0 collective-permute-done.flux_beside
  48.1 1.3 %shard_map.108 = (f32[32,8,128]{2,1,0:T(8,128)S(1)}, f32[8,128]{1,0:T(8,128)S(1)}, bf16[16,16,128]{2,1,0:T(8,128)(2,1)S(1)}) custom-call(s32[1]{0:T(128)} %bitcast.5.quarter, f32[160,128]{1,0:T(8,128)S(1)} %shard_map.105.flux, f32[160,128]{1,0:T(8,128)S(1)} %collective-permute-done.flux_beside, f32[32,128]{1,0:T(8,128)S(1)} %get-tuple-element.21.own, ...), custom_call_target="tpu_custom_call" | custom-call | tf_op jit(solution)/shard_map/pallas_call | solution.py:496
  49.5 14.2 %all_to_all.21.received = bf16[16,16,128]{2,1,0:T(8,128)(2,1)S(1)} all-to-all(bf16[16,16,128]{2,1,0:T(8,128)(2,1)S(1)} %get-tuple-element.26), channel_id=1, replica_groups=mesh['c'=4,'y'=4,'x'=4,'h'=2,'k'=2] {'c','h','k'}, dimensions={0} | all-to-all | bytes 131072 | tf_op jit(solution)/shard_map/all_to_all | solution.py:506
  63.7 0.4 shard_map.109
  64.0 13.4 %all_to_all.22.received = bf16[16,64,128]{2,1,0:T(8,128)(2,1)S(1)} all-to-all(bf16[16,64,128]{2,1,0:T(8,128)(2,1)S(1)} %shard_map.109), channel_id=1, replica_groups=mesh['c'=4,'y'=4,'x'=4,'h'=2,'k'=2] {'y','x'}, dimensions={0} | all-to-all | bytes 524288 | tf_op jit(solution)/shard_map/all_to_all | solution.py:511
  77.4 1.0 %shard_map.110 = (bf16[2,1024]{1,0:T(2,128)(2,1)}, f32[32,8,128]{2,1,0:T(8,128)}, f32[8,128]{1,0:T(8,128)}) custom-call(bf16[16,64,128]{2,1,0:T(8,128)(2,1)S(1)} %all_to_all.22.received, bf16[8,4,128,128]{3,2,1,0:T(8,128)(2,1)S(1)} %get-tuple-element.27.weights, f32[32,8,128]{2,1,0:T(8,128)S(1)} %get-tuple-element.28.tracer, ...), custom_call_target="tpu_custom_call" | custom-call | tf_op jit(solution)/shard_map/pallas_call | solution.py:513
  (2 shorter events, 0.1 us)
Async XLA Ops:
  23.4 15.4 %all-to-all-start.1 = ((bf16[8,160,128]{2,1,0:T(8,128)(2,1)}), bf16[8,160,128]{2,1,0:T(8,128)(2,1)S(1)}, u32[]{:S(2)}, u32[]{:S(2)}) async-start(bf16[8,160,128]{2,1,0:T(8,128)(2,1)} %get-tuple-element.20), calls=%async_computation.1 | async-start | bytes 655360 | tf_op jit(solution)/shard_map/all_to_all | solution.py:475
  31.6 3.1 %collective-permute-start.1 = (bf16[224,128]{1,0:T(8,128)(2,1)S(1)}, bf16[224,128]{1,0:T(8,128)(2,1)S(1)}, u32[]{:S(2)}, u32[]{:S(2)}) collective-permute-start(bf16[224,128]{1,0:T(8,128)(2,1)S(1)} %get-tuple-element.22.leaving), channel_id=1, source_target_pairs={{0,1},{1,0},{2,3},{3,2},{4,5},{5,4},{6,7},{7,6},{8,9},{9,8},{10,11... | collective-permute-start | bytes 172040 | tf_op jit(solution)/shard_map/ppermute | solution.py:465
  34.7 12.9 %copy-start = (f32[32,8,128]{2,1,0:T(8,128)S(1)}, f32[32,8,128]{2,1,0:T(8,128)}, u32[]{:S(2)}) copy-start(f32[32,8,128]{2,1,0:T(8,128)} %tracer.1) | copy-start | bytes 393220
  34.7 12.9 %copy-start.1 = (f32[31,8,128]{2,1,0:T(8,128)S(1)}, f32[31,8,128]{2,1,0:T(8,128)}, u32[]{:S(2)}) copy-start(f32[31,8,128]{2,1,0:T(8,128)} %mixing.1) | copy-start | bytes 380932
  34.7 8.5 %collective-permute-start.2 = (bf16[160,128]{1,0:T(8,128)(2,1)S(1)}, bf16[160,128]{1,0:T(8,128)(2,1)S(1)}, u32[]{:S(2)}, u32[]{:S(2)}) collective-permute-start(bf16[160,128]{1,0:T(8,128)(2,1)S(1)} %shard_map.106), channel_id=1, source_target_pairs={{0,2},{2,0},{3,5},{4,6},{5,3},{6,4},{7,9},{8,10},{9,7},{10,8},{11,... | collective-permute-start | bytes 122888 | tf_op jit(solution)/shard_map/ppermute | solution.py:469
  38.9 9.2 %collective-permute-start = (f32[160,128]{1,0:T(8,128)S(1)}, f32[160,128]{1,0:T(8,128)S(1)}, u32[]{:S(2)}, u32[]{:S(2)}) collective-permute-start(f32[160,128]{1,0:T(8,128)S(1)} %shard_map.105.flux), channel_id=1, source_target_pairs={{0,1},{1,0},{2,3},{3,2},{4,5},{5,4},{6,7},{7,6},{8,9},{9,8},{10,11... | collective-permute-start | bytes 245768 | tf_op jit(solution)/shard_map/ppermute | solution.py:477
  43.3 4.4 %collective-permute-start.3 = (bf16[160,128]{1,0:T(8,128)(2,1)S(1)}, bf16[160,128]{1,0:T(8,128)(2,1)S(1)}, u32[]{:S(2)}, u32[]{:S(2)}) collective-permute-start(bf16[160,128]{1,0:T(8,128)(2,1)S(1)} %collective-permute-done.2.mixed), channel_id=1, source_target_pairs={{0,1},{1,0},{2,3},{3,2},{4,5},{5,4},{6,7},{7,6},{8,9},{9,8},{10,11... | collective-permute-start | bytes 122888 | tf_op jit(solution)/shard_map/ppermute | solution.py:479

commit v6 on v5

--- a/solution.py
+++ b/solution.py
@@ -72,8 +72,8 @@
 
 def prepare(
     place, tracer_far, mixing_far, height_far, flow_far, wet_far, targets_far, sources_far,
-    weights_far, leaving, own, weights, message,
-    tracer, mixing, wet, targets, sources, flat, packet, done, sent,
+    weights_far, leaving, own, weights, tracer, mixing, message,
+    wet, targets, sources, flat, packet, done, sent,
 ):
     def load(source, target, flag):
         copy = pltpu.make_async_copy(source, target, flag)
@@ -301,15 +301,19 @@
 
     wet = ring(3, own[24:32])
     rain = fresh_gain * window(0) * wet
-    push_e = stress_gain * window(48)
-    push_n = stress_gain * window(96)
     h = ring(0, own[0:8])
-    flow_e = ring(1, own[8:16])
-    flow_n = ring(2, own[16:24])
     face_e = wet * east(wet)
     face_n = wet * north(wet)
+    flow_e = wave_gain * ring(1, own[8:16])
+    flow_n = wave_gain * ring(2, own[16:24])
+    push_e = (wave_gain * stress_gain) * window(48)
+    push_n = (wave_gain * stress_gain) * window(96)
     face_w, flow_w, push_w = west(face_e), west(flow_e), west(push_e)
     face_s, flow_s, push_s = south(face_n), south(flow_n), south(push_n)
+    slope = wave_gain * wave_gain
+    slope_e, slope_w, slope_n, slope_s = (
+        slope * face for face in (face_e, face_w, face_n, face_s)
+    )
     for turn in range(NSTEP * NSUB):
         if turn == NSUB:
 
@@ -319,12 +323,13 @@
             h, flow_e, flow_w, flow_n, flow_s = map(inner, (h, flow_e, flow_w, flow_n, flow_s))
             face_e, face_w, face_n, face_s = map(inner, (face_e, face_w, face_n, face_s))
             push_e, push_w, push_n, push_s = map(inner, (push_e, push_w, push_n, push_s))
+            slope_e, slope_w, slope_n, slope_s = map(inner, (slope_e, slope_w, slope_n, slope_s))
             rain = inner(rain)
-        flow_e = face_e * (flow_e - wave_gain * (east(h) - h) + push_e)
-        flow_w = face_w * (flow_w - wave_gain * (h - west(h)) + push_w)
-        flow_n = face_n * (flow_n - wave_gain * (north(h) - h) + push_n)
-        flow_s = face_s * (flow_s - wave_gain * (h - south(h)) + push_s)
-        h = h - wave_gain * (flow_e - flow_w + flow_n - flow_s) + rain
+        flow_e = face_e * (flow_e + push_e) - slope_e * (east(h) - h)
+        flow_w = face_w * (flow_w + push_w) - slope_w * (h - west(h))
+        flow_n = face_n * (flow_n + push_n) - slope_n * (north(h) - h)
+        flow_s = face_s * (flow_s + push_s) - slope_s * (h - south(h))
+        h = (h + rain) - ((flow_e - flow_w) + (flow_n - flow_s))
     height_out[...] = h[0:ROWS]
 
     wet16 = jnp.concatenate([wet[0:ROWS], jnp.where(
@@ -427,18 +432,18 @@
     place, quarter = spot.reshape(1), turn.reshape(1)
     count = lax.axis_size(ALL)
 
-    leaving, own, weights, first = call(
+    leaving, own, weights, tracer, mixing, first = call(
         prepare,
         (
             inside((224, LANES), BF),
             inside((32, LANES), F32),
             inside((8, 4, LANES, LANES), BF),
+            inside((LEVELS, ROWS, LANES), F32),
+            inside((LEVELS - 1, ROWS, LANES), F32),
             shaped((GROUP, 144, LANES), BF),
         ),
         [smem] + [far] * 8,
         [
-            pltpu.VMEM((LEVELS, ROWS, LANES), F32),
-            pltpu.VMEM((LEVELS - 1, ROWS, LANES), F32),
             pltpu.VMEM((ROWS, LANES), jnp.int32),
             pltpu.VMEM((4, 8), jnp.int32),
             pltpu.VMEM((4, 8 * LANES), BF),
@@ -447,13 +452,13 @@
             pltpu.SemaphoreType.DMA((16,)),
             pltpu.SemaphoreType.DMA((16,)),
         ],
-        out_specs=(vmem, vmem, vmem, far),
+        out_specs=(vmem,) * 5 + (far,),
         room=60 * 1024,
     )(
         place, tracer, mixing, height, flow, marine,
         latitude[0].T, airside[0], matrices[0],
     )
-    leaving, own, weights = map(near, (leaving, own, weights))
+    leaving, own, weights, tracer, mixing = map(near, (leaving, own, weights, tracer, mixing))
     first = near(lax.all_to_all(first, PLANE, 0, 0, tiled=True))
     flip = [(i, i ^ 1) for i in range(count)]
     pairs = []

time: 78.9 us -> 78.6 us (level)
  no operation moved by 1% of the time
where the time goes in v6:
time: 78.6 us; the launch traced here: 78.2 us
  blocking collectives  46.3 us (59%)
  starting transfers between devices  18.9 us (24%)
  Pallas kernels  7.09 us (9%)
  waiting for transfers between devices  5.26 us (7%)
    all_to_all x1, blocking collectives, shards(): first = near(lax.all_to_all(first, PLANE, 0, 0, tiled=True))  18.9 us
    all_to_all x1, blocking collectives, shards(): third = near(lax.all_to_all(third, LINE, 0, 0, tiled=True))  13.8 us
    all_to_all x1, blocking collectives, shards(): fourth = near(lax.all_to_all(fourth, PLANE, 0, 0, tiled=True))  13.6 us
    all_to_all x1, starting transfers between devices, shards(): second = near(lax.all_to_all(second, ('c', 'h'), 0, 0, tiled=True))  8.18 us
    ppermute x1, starting transfers between devices, shards(): flux_beside = near(lax.ppermute(flux, ALL, flip))  4.34 us
    ppermute x1, starting transfers between devices, shards(): shared = near(lax.ppermute(mixed, ALL, flip))  3.5 us
    all_to_all x1, waiting for transfers between devices, shards(): second = near(lax.all_to_all(second, ('c', 'h'), 0, 0, tiled=True))  3.49 us
    pallas_call x1, Pallas kernels, shards(): call(prepare, (inside((224, LANES), BF), inside((32, LANES), F32), inside...  2.74 us
  transfers between devices with their start and end apart: 5, of which 3 were waited for; matrix products, arithmetic and copies ran while one was open for 0% of the time, Pallas kernels for 1%

profile of v6, /device:TPU:1, one launch (start us, length us, event | category | flops | bytes accessed | tf_op | source)
XLA Modules:
  0.0 78.2 jit_solution(1543932555804348926)
XLA Ops:
  0.6 2.7 %shard_map.103 = (bf16[224,128]{1,0:T(8,128)(2,1)S(1)}, f32[32,128]{1,0:T(8,128)S(1)}, bf16[8,4,128,128]{3,2,1,0:T(8,128)(2,1)S(1)}, f32[32,8,128]{2,1,0:T(8,128...) custom-call(s32[1]{0:T(128)} %bitcast.place, f32[32,8,128]{2,1,0:T(8,128)} %tracer_far.1, ...), custom_call_target="tpu_custom_call" | custom-call | tf_op jit(solution)/shard_map/pallas_call | solution.py:435
  3.4 18.9 %all_to_all.20.received = bf16[16,144,128]{2,1,0:T(8,128)(2,1)S(1)} all-to-all(bf16[16,144,128]{2,1,0:T(8,128)(2,1)} %get-tuple-element.20), channel_id=1, replica_groups=mesh['c'=4,'y'=4,'x'=4,'h'=2,'k'=2] {'y','x'}, dimensions={0} | all-to-all | bytes 1179648 | tf_op jit(solution)/shard_map/all_to_all | solution.py:462
  22.3 1.2 %shard_map.104 = (bf16[8,160,128]{2,1,0:T(8,128)(2,1)}, f32[8,128]{1,0:T(8,128)S(1)}) custom-call(s32[1]{0:T(128)} %bitcast.place, bf16[16,144,128]{2,1,0:T(8,128)(2,1)S(1)} %all_to_all.20.received), custom_call_target="tpu_custom_call" | custom-call | tf_op jit(solution)/shard_map/pallas_call | solution.py:476
  23.4 8.2 %all-to-all-start.1 = ((bf16[8,160,128]{2,1,0:T(8,128)(2,1)}), bf16[8,160,128]{2,1,0:T(8,128)(2,1)S(1)}, u32[]{:S(2)}, u32[]{:S(2)}) async-start(bf16[8,160,128]{2,1,0:T(8,128)(2,1)} %get-tuple-element.22), calls=%async_computation.1 | async-start | bytes 655360 | tf_op jit(solution)/shard_map/all_to_all | solution.py:480
  31.6 2.2 %collective-permute-start.1 = (bf16[224,128]{1,0:T(8,128)(2,1)S(1)}, bf16[224,128]{1,0:T(8,128)(2,1)S(1)}, u32[]{:S(2)}, u32[]{:S(2)}) collective-permute-start(bf16[224,128]{1,0:T(8,128)(2,1)S(1)} %get-tuple-element.24.leaving), channel_id=1, source_target_pairs={{0,1},{1,0},{2,3},{3,2},{4,5},{5,4},{6,7},{7,6},{8,9},{9,8},{10,11... | collective-permute-start | bytes 172040 | tf_op jit(solution)/shard_map/ppermute | solution.py:470
  33.8 0.9 %collective-permute-done.1.beside = bf16[224,128]{1,0:T(8,128)(2,1)S(1)} collective-permute-done((bf16[224,128]{1,0:T(8,128)(2,1)S(1)}, bf16[224,128]{1,0:T(8,128)(2,1)S(1)}, u32[]{:S(2)}, u32[]{:S(2)}) %collective-permute-start.1) | collective-permute-done | bytes 57376 | tf_op jit(solution)/shard_map/ppermute | solution.py:470
  34.7 0.7 collective-permute-start.2
  35.4 3.5 %all-to-all-done.1.received = bf16[8,160,128]{2,1,0:T(8,128)(2,1)S(1)} async-done(((bf16[8,160,128]{2,1,0:T(8,128)(2,1)}), bf16[8,160,128]{2,1,0:T(8,128)(2,1)S(1)}, u32[]{:S(2)}, u32[]{:S(2)}) %all-to-all-start.1) | async-done | bytes 327712 | tf_op jit(solution)/shard_map/all_to_all | solution.py:480
  38.9 4.3 %collective-permute-start = (f32[160,128]{1,0:T(8,128)S(1)}, f32[160,128]{1,0:T(8,128)S(1)}, u32[]{:S(2)}, u32[]{:S(2)}) collective-permute-start(f32[160,128]{1,0:T(8,128)S(1)} %shard_map.105.flux), channel_id=1, source_target_pairs={{0,1},{1,0},{2,3},{3,2},{4,5},{5,4},{6,7},{7,6},{8,9},{9,8},{10,11... | collective-permute-start | bytes 245768 | tf_op jit(solution)/shard_map/ppermute | solution.py:482
  43.2 0.0 collective-permute-done.2.mixed
  43.2 3.5 %collective-permute-start.3 = (bf16[160,128]{1,0:T(8,128)(2,1)S(1)}, bf16[160,128]{1,0:T(8,128)(2,1)S(1)}, u32[]{:S(2)}, u32[]{:S(2)}) collective-permute-start(bf16[160,128]{1,0:T(8,128)(2,1)S(1)} %collective-permute-done.2.mixed), channel_id=1, source_target_pairs={{0,1},{1,0},{2,3},{3,2},{4,5},{5,4},{6,7},{7,6},{8,9},{9,8},{10,11... | collective-permute-start | bytes 122888 | tf_op jit(solution)/shard_map/ppermute | solution.py:484
  46.7 0.9 %collective-permute-done.3.shared = bf16[160,128]{1,0:T(8,128)(2,1)S(1)} collective-permute-done((bf16[160,128]{1,0:T(8,128)(2,1)S(1)}, bf16[160,128]{1,0:T(8,128)(2,1)S(1)}, u32[]{:S(2)}, u32[]{:S(2)}) %collective-permute-start.3) | collective-permute-done | bytes 40992 | tf_op jit(solution)/shard_map/ppermute | solution.py:484
  47.6 0.5 shard_map.107
  48.1 0.0 collective-permute-done.flux_beside
  48.1 1.3 %shard_map.108 = (f32[32,8,128]{2,1,0:T(8,128)S(1)}, f32[8,128]{1,0:T(8,128)S(1)}, bf16[16,16,128]{2,1,0:T(8,128)(2,1)S(1)}) custom-call(s32[1]{0:T(128)} %bitcast.5.quarter, f32[160,128]{1,0:T(8,128)S(1)} %shard_map.105.flux, f32[160,128]{1,0:T(8,128)S(1)} %collective-permute-done.flux_beside, f32[32,128]{1,0:T(8,128)S(1)} %get-tuple-element.23.own, ...), custom_call_target="tpu_custom_call" | custom-call | tf_op jit(solution)/shard_map/pallas_call | solution.py:501
  49.4 13.8 %all_to_all.21.received = bf16[16,16,128]{2,1,0:T(8,128)(2,1)S(1)} all-to-all(bf16[16,16,128]{2,1,0:T(8,128)(2,1)S(1)} %get-tuple-element.30), channel_id=1, replica_groups=mesh['c'=4,'y'=4,'x'=4,'h'=2,'k'=2] {'c','h','k'}, dimensions={0} | all-to-all | bytes 131072 | tf_op jit(solution)/shard_map/all_to_all | solution.py:511
  63.2 0.4 shard_map.109
  63.6 13.6 %all_to_all.22.received = bf16[16,64,128]{2,1,0:T(8,128)(2,1)S(1)} all-to-all(bf16[16,64,128]{2,1,0:T(8,128)(2,1)S(1)} %shard_map.109), channel_id=1, replica_groups=mesh['c'=4,'y'=4,'x'=4,'h'=2,'k'=2] {'y','x'}, dimensions={0} | all-to-all | bytes 524288 | tf_op jit(solution)/shard_map/all_to_all | solution.py:516
  77.2 1.0 %shard_map.110 = (bf16[2,1024]{1,0:T(2,128)(2,1)}, f32[32,8,128]{2,1,0:T(8,128)}, f32[8,128]{1,0:T(8,128)}) custom-call(bf16[16,64,128]{2,1,0:T(8,128)(2,1)S(1)} %all_to_all.22.received, bf16[8,4,128,128]{3,2,1,0:T(8,128)(2,1)S(1)} %get-tuple-element.31.weights, f32[32,8,128]{2,1,0:T(8,128)S(1)} %get-tuple-element.32.tracer, ...), custom_call_target="tpu_custom_call" | custom-call | tf_op jit(solution)/shard_map/pallas_call | solution.py:518
  (2 shorter events, 0.1 us)
Async XLA Ops:
  23.4 15.4 %all-to-all-start.1 = ((bf16[8,160,128]{2,1,0:T(8,128)(2,1)}), bf16[8,160,128]{2,1,0:T(8,128)(2,1)S(1)}, u32[]{:S(2)}, u32[]{:S(2)}) async-start(bf16[8,160,128]{2,1,0:T(8,128)(2,1)} %get-tuple-element.22), calls=%async_computation.1 | async-start | bytes 655360 | tf_op jit(solution)/shard_map/all_to_all | solution.py:480
  31.6 3.1 %collective-permute-start.1 = (bf16[224,128]{1,0:T(8,128)(2,1)S(1)}, bf16[224,128]{1,0:T(8,128)(2,1)S(1)}, u32[]{:S(2)}, u32[]{:S(2)}) collective-permute-start(bf16[224,128]{1,0:T(8,128)(2,1)S(1)} %get-tuple-element.24.leaving), channel_id=1, source_target_pairs={{0,1},{1,0},{2,3},{3,2},{4,5},{5,4},{6,7},{7,6},{8,9},{9,8},{10,11... | collective-permute-start | bytes 172040 | tf_op jit(solution)/shard_map/ppermute | solution.py:470
  34.7 8.5 %collective-permute-start.2 = (bf16[160,128]{1,0:T(8,128)(2,1)S(1)}, bf16[160,128]{1,0:T(8,128)(2,1)S(1)}, u32[]{:S(2)}, u32[]{:S(2)}) collective-permute-start(bf16[160,128]{1,0:T(8,128)(2,1)S(1)} %shard_map.106), channel_id=1, source_target_pairs={{0,2},{2,0},{3,5},{4,6},{5,3},{6,4},{7,9},{8,10},{9,7},{10,8},{11,... | collective-permute-start | bytes 122888 | tf_op jit(solution)/shard_map/ppermute | solution.py:474
  38.9 9.2 %collective-permute-start = (f32[160,128]{1,0:T(8,128)S(1)}, f32[160,128]{1,0:T(8,128)S(1)}, u32[]{:S(2)}, u32[]{:S(2)}) collective-permute-start(f32[160,128]{1,0:T(8,128)S(1)} %shard_map.105.flux), channel_id=1, source_target_pairs={{0,1},{1,0},{2,3},{3,2},{4,5},{5,4},{6,7},{7,6},{8,9},{9,8},{10,11... | collective-permute-start | bytes 245768 | tf_op jit(solution)/shard_map/ppermute | solution.py:482
  43.2 4.4 %collective-permute-start.3 = (bf16[160,128]{1,0:T(8,128)(2,1)S(1)}, bf16[160,128]{1,0:T(8,128)(2,1)S(1)}, u32[]{:S(2)}, u32[]{:S(2)}) collective-permute-start(bf16[160,128]{1,0:T(8,128)(2,1)S(1)} %collective-permute-done.2.mixed), channel_id=1, source_target_pairs={{0,1},{1,0},{2,3},{3,2},{4,5},{5,4},{6,7},{7,6},{8,9},{9,8},{10,11... | collective-permute-start | bytes 122888 | tf_op jit(solution)/shard_map/ppermute | solution.py:484

commit v7 on v6

--- a/solution.py
+++ b/solution.py
@@ -148,36 +148,40 @@
         copy.wait()
 
 
-def chip_edges(quarter, leaving, beside, message):
+def chip_edges(quarter, leaving, beside, across, outward):
     mine = quarter[0]
     core = mine & 1
     own = pl.multiple_of(32 * core, 32)
     other = pl.multiple_of(32 - 32 * core, 32)
-    message[pl.ds(own, 32)] = leaving[0:32]
-    message[pl.ds(other, 32)] = beside[0:32]
-    for i, (source, start) in enumerate(
-        ((beside, 32), (beside, 128), (leaving, 128), (leaving, 32))
-    ):
-
-        @pl.when(mine == i)
-        def _(source=source, start=start):
-            message[64:160] = source[start : start + 96]
-
-
-def edge_sides(mine, beside, mixed, shared):
+    for message in (across, outward):
+        message[pl.ds(own, 32)] = leaving[0:32]
+        message[pl.ds(other, 32)] = beside[0:32]
+
+    @pl.when(mine < 2)
+    def _():
+        across[64:160] = beside[32:128]
+        outward[64:160] = beside[128:224]
+
+    @pl.when(mine >= 2)
+    def _():
+        across[64:160] = beside[128:224]
+        outward[64:160] = beside[32:128]
+
+
+def edge_sides(mine, beside, opposite, outer):
     first = (mine & 1) == 0
+    ends = (mine == 0) | (mine == 3)
     near_edge = jnp.where(first, beside[128:224].astype(F32), beside[32:128].astype(F32))
-    far_edge = jnp.where(mine < 2, shared[64:160].astype(F32), mixed[64:160].astype(F32))
+    far_edge = jnp.where(ends, outer[64:160].astype(F32), opposite[64:160].astype(F32))
     return jnp.where(first, far_edge, near_edge), jnp.where(first, near_edge, far_edge)
 
 
-def strips(mine, beside, mixed, shared):
+def strips(mine, beside, opposite, outer):
     first = (mine & 1) == 0
     low = mine < 2
-    ours, theirs = mixed[0:64].astype(F32), shared[0:64].astype(F32)
-    swap = first == low
-    prev = jnp.where(swap, theirs, ours)
-    follow = jnp.where(swap, ours, theirs)
+    inner, outside = opposite[0:64].astype(F32), outer[0:64].astype(F32)
+    prev = jnp.where(low, outside, inner)
+    follow = jnp.where(low, inner, outside)
     partner = beside[0:32].astype(F32)
     before2 = jnp.where(first, prev[0:32], prev[32:64])
     before = jnp.where(first, prev[32:64], partner)
@@ -226,10 +230,10 @@
     total[...] = some
 
 
-def first_step(quarter, tracer, mixing, own, beside, mixed, shared, base, reply, factors, halo, mix_halo, work):
+def first_step(quarter, tracer, mixing, own, beside, opposite, outer, base, reply, factors, halo, mix_halo, work):
     mine = quarter[0]
-    before, after = edge_sides(mine, beside, mixed, shared)
-    _, wet_before, wet_after, _ = (strip[24:32] for strip in strips(mine, beside, mixed, shared))
+    before, after = edge_sides(mine, beside, opposite, outer)
+    _, wet_before, wet_after, _ = (strip[24:32] for strip in strips(mine, beside, opposite, outer))
     halo[...] = jnp.zeros_like(halo)
     mix_halo[...] = jnp.zeros_like(mix_halo)
     halo[pl.ds(0, LEVELS, stride=ROWS), :] = after[0:32]
@@ -281,11 +285,11 @@
 
 
 def ocean(
-    quarter, flux, flux_beside, own, beside, mixed, shared, base, reply, factors,
+    quarter, flux, flux_beside, own, beside, opposite, outer, base, reply, factors,
     tracer_out, height_out, message, work,
 ):
     mine = quarter[0]
-    before2, before, after, after2 = strips(mine, beside, mixed, shared)
+    before2, before, after, after2 = strips(mine, beside, opposite, outer)
 
     def ring(i, own):
         r = slice(i * ROWS, (i + 1) * ROWS)
@@ -463,15 +467,15 @@
     flip = [(i, i ^ 1) for i in range(count)]
     pairs = []
     for i in range(count):
-        up = bool(i & 2) == bool(i & 1)
-        j = i + 2 if up else i - 2
+        j = i + 2 if i & 2 else i - 2
         if 0 <= j < count:
             pairs.append((i, j))
     beside = near(lax.ppermute(leaving, ALL, flip))
-    mixed = call(
-        chip_edges, inside((160, LANES), BF), [smem] + [vmem] * 2
+    across, outward = call(
+        chip_edges, (inside((160, LANES), BF), inside((160, LANES), BF)), [smem] + [vmem] * 2
     )(quarter, leaving, beside)
-    mixed = near(lax.ppermute(near(mixed), ALL, pairs))
+    opposite = near(lax.ppermute(near(across), ALL, [(i, i ^ 2) for i in range(count)]))
+    outer = near(lax.ppermute(near(outward), ALL, pairs))
 
     second, rows_named = call(
         sort_terms, (inside((8, 160, LANES), BF), inside((ROWS, LANES), F32)), [smem, vmem]
@@ -480,8 +484,6 @@
     second = near(lax.all_to_all(second, ("c", "h"), 0, 0, tiled=True))
     flux = near(call(add_up, inside((160, LANES), F32), [vmem])(second))
     flux_beside = near(lax.ppermute(flux, ALL, flip))
-
-    shared = near(lax.ppermute(mixed, ALL, flip))
 
     base, reply, factors = call(
         first_step,
@@ -496,7 +498,7 @@
             pltpu.VMEM((LEVELS * ROWS, LANES), F32),
             pltpu.VMEM((LEVELS, 2 * ROWS, LANES), F32),
         ],
-    )(quarter, tracer, mixing, own, beside, mixed, shared)
+    )(quarter, tracer, mixing, own, beside, opposite, outer)
 
     tracer_new, height_new, third = call(
         ocean,
@@ -507,7 +509,7 @@
         ),
         [smem] + [vmem] * 9,
         [pltpu.VMEM((LEVELS, ROWS, LANES), F32)],
-    )(quarter, flux, flux_beside, own, beside, mixed, shared, near(base), near(reply), near(factors))
+    )(quarter, flux, flux_beside, own, beside, opposite, outer, near(base), near(reply), near(factors))
     third = near(lax.all_to_all(third, LINE, 0, 0, tiled=True))
 
     fourth = call(

time: 78.6 us -> 87.6 us (1.11)
  blocking collectives: 46.3 us -> 52.8 us
  waiting for transfers between devices: 5.26 us -> 8.55 us
  starting transfers between devices: 18.9 us -> 18 us
    all_to_all x1, blocking collectives: 13.8 us -> 21.1 us  [shards(): third = near(lax.all_to_all(third, LINE, 0, 0, tiled=True))]
    ppermute x2, waiting for transfers between devices: 0.87 us -> 3.5 us  [the longest x1 3.5 us: shards(): lax.ppermute(near(across), ALL, [(i, i ^ 2) for i in range(count)])]
    all_to_all x1, waiting for transfers between devices: 3.49 us -> 5.04 us  [shards(): second = near(lax.all_to_all(second, ('c', 'h'), 0, 0, tiled=True))]
    ppermute x1, waiting for transfers between devices: 0.89 us -> 0.01 us  [shards(): beside = near(lax.ppermute(leaving, ALL, flip))]
  transfers between devices with their start and end apart: 5 -> 5, of which waited for: 3 -> 2; matrix products, arithmetic and copies ran while one was open for 0% -> 0% of each run, Pallas kernels for 1% -> 1%
where the time goes in v7:
time: 87.6 us; the launch traced here: 87.2 us
  blocking collectives  52.8 us (60%)
  starting transfers between devices  18 us (21%)
  waiting for transfers between devices  8.55 us (10%)
  Pallas kernels  7.1 us (8%)
    all_to_all x1, blocking collectives, shards(): third = near(lax.all_to_all(third, LINE, 0, 0, tiled=True))  21.1 us
    all_to_all x1, blocking collectives, shards(): first = near(lax.all_to_all(first, PLANE, 0, 0, tiled=True))  18.9 us
    all_to_all x1, blocking collectives, shards(): fourth = near(lax.all_to_all(fourth, PLANE, 0, 0, tiled=True))  12.8 us
    all_to_all x1, starting transfers between devices, shards(): second = near(lax.all_to_all(second, ('c', 'h'), 0, 0, tiled=True))  8.18 us
    all_to_all x1, waiting for transfers between devices, shards(): second = near(lax.all_to_all(second, ('c', 'h'), 0, 0, tiled=True))  5.04 us
    ppermute x1, starting transfers between devices, shards(): flux_beside = near(lax.ppermute(flux, ALL, flip))  4.34 us
    ppermute x1, waiting for transfers between devices, shards(): lax.ppermute(near(across), ALL, [(i, i ^ 2) for i in range(count)])  3.5 us
    pallas_call x1, Pallas kernels, shards(): call(prepare, (inside((224, LANES), BF), inside((32, LANES), F32), inside...  2.74 us
  transfers between devices with their start and end apart: 5, of which 2 were waited for; matrix products, arithmetic and copies ran while one was open for 0% of the time, Pallas kernels for 1%

profile of v7, /device:TPU:1, one launch (start us, length us, event | category | flops | bytes accessed | tf_op | source)
XLA Modules:
  0.0 87.2 jit_solution(11529761816727608653)
XLA Ops:
  0.6 2.7 %shard_map.103 = (bf16[224,128]{1,0:T(8,128)(2,1)S(1)}, f32[32,128]{1,0:T(8,128)S(1)}, bf16[8,4,128,128]{3,2,1,0:T(8,128)(2,1)S(1)}, f32[32,8,128]{2,1,0:T(8,128...) custom-call(s32[1]{0:T(128)} %bitcast.place, f32[32,8,128]{2,1,0:T(8,128)} %tracer_far.1, ...), custom_call_target="tpu_custom_call" | custom-call | tf_op jit(solution)/shard_map/pallas_call | solution.py:439
  3.4 18.9 %all_to_all.20.received = bf16[16,144,128]{2,1,0:T(8,128)(2,1)S(1)} all-to-all(bf16[16,144,128]{2,1,0:T(8,128)(2,1)} %get-tuple-element.22), channel_id=1, replica_groups=mesh['c'=4,'y'=4,'x'=4,'h'=2,'k'=2] {'y','x'}, dimensions={0} | all-to-all | bytes 1179648 | tf_op jit(solution)/shard_map/all_to_all | solution.py:466
  22.3 1.1 %shard_map.104 = (bf16[8,160,128]{2,1,0:T(8,128)(2,1)}, f32[8,128]{1,0:T(8,128)S(1)}) custom-call(s32[1]{0:T(128)} %bitcast.place, bf16[16,144,128]{2,1,0:T(8,128)(2,1)S(1)} %all_to_all.20.received), custom_call_target="tpu_custom_call" | custom-call | tf_op jit(solution)/shard_map/pallas_call | solution.py:480
  23.4 8.2 %all-to-all-start.1 = ((bf16[8,160,128]{2,1,0:T(8,128)(2,1)}), bf16[8,160,128]{2,1,0:T(8,128)(2,1)S(1)}, u32[]{:S(2)}, u32[]{:S(2)}) async-start(bf16[8,160,128]{2,1,0:T(8,128)(2,1)} %get-tuple-element.24), calls=%async_computation.1 | async-start | bytes 655360 | tf_op jit(solution)/shard_map/all_to_all | solution.py:484
  31.6 2.2 %collective-permute-start.1 = (bf16[224,128]{1,0:T(8,128)(2,1)S(1)}, bf16[224,128]{1,0:T(8,128)(2,1)S(1)}, u32[]{:S(2)}, u32[]{:S(2)}) collective-permute-start(bf16[224,128]{1,0:T(8,128)(2,1)S(1)} %get-tuple-element.26.leaving), channel_id=1, source_target_pairs={{0,1},{1,0},{2,3},{3,2},{4,5},{5,4},{6,7},{7,6},{8,9},{9,8},{10,11... | collective-permute-start | bytes 172040 | tf_op jit(solution)/shard_map/ppermute | solution.py:473
  33.8 5.0 %all-to-all-done.1.received = bf16[8,160,128]{2,1,0:T(8,128)(2,1)S(1)} async-done(((bf16[8,160,128]{2,1,0:T(8,128)(2,1)}), bf16[8,160,128]{2,1,0:T(8,128)(2,1)S(1)}, u32[]{:S(2)}, u32[]{:S(2)}) %all-to-all-start.1) | async-done | bytes 327712 | tf_op jit(solution)/shard_map/all_to_all | solution.py:484
  38.9 4.3 %collective-permute-start = (f32[160,128]{1,0:T(8,128)S(1)}, f32[160,128]{1,0:T(8,128)S(1)}, u32[]{:S(2)}, u32[]{:S(2)}) collective-permute-start(f32[160,128]{1,0:T(8,128)S(1)} %shard_map.105.flux), channel_id=1, source_target_pairs={{0,1},{1,0},{2,3},{3,2},{4,5},{5,4},{6,7},{7,6},{8,9},{9,8},{10,11... | collective-permute-start | bytes 245768 | tf_op jit(solution)/shard_map/ppermute | solution.py:486
  43.2 0.0 collective-permute-done.1.beside
  43.3 2.7 %collective-permute-start.2 = (bf16[160,128]{1,0:T(8,128)(2,1)S(1)}, bf16[160,128]{1,0:T(8,128)(2,1)S(1)}, u32[]{:S(2)}, u32[]{:S(2)}) collective-permute-start(bf16[160,128]{1,0:T(8,128)(2,1)S(1)} %get-tuple-element.27), channel_id=1, source_target_pairs={{0,2},{1,3},{2,0},{3,1},{4,6},{5,7},{6,4},{7,5},{8,10},{9,11},{10,... | collective-permute-start | bytes 122888 | tf_op jit(solution)/shard_map/ppermute | solution.py:477
  45.9 0.7 collective-permute-start.3
  46.6 3.5 %collective-permute-done.2.opposite = bf16[160,128]{1,0:T(8,128)(2,1)S(1)} collective-permute-done((bf16[160,128]{1,0:T(8,128)(2,1)S(1)}, bf16[160,128]{1,0:T(8,128)(2,1)S(1)}, u32[]{:S(2)}, u32[]{:S(2)}) %collective-permute-start.2) | collective-permute-done | bytes 40992 | tf_op jit(solution)/shard_map/ppermute | solution.py:477
  50.1 0.0 collective-permute-done.3.outer
  50.1 0.5 shard_map.107
  50.6 0.0 collective-permute-done.flux_beside
  50.6 1.3 %shard_map.108 = (f32[32,8,128]{2,1,0:T(8,128)S(1)}, f32[8,128]{1,0:T(8,128)S(1)}, bf16[16,16,128]{2,1,0:T(8,128)(2,1)S(1)}) custom-call(s32[1]{0:T(128)} %bitcast.5.quarter, f32[160,128]{1,0:T(8,128)S(1)} %shard_map.105.flux, f32[160,128]{1,0:T(8,128)S(1)} %collective-permute-done.flux_beside, f32[32,128]{1,0:T(8,128)S(1)} %get-tuple-element.25.own, ...), custom_call_target="tpu_custom_call" | custom-call | tf_op jit(solution)/shard_map/pallas_call | solution.py:503
  51.9 21.1 %all_to_all.21.received = bf16[16,16,128]{2,1,0:T(8,128)(2,1)S(1)} all-to-all(bf16[16,16,128]{2,1,0:T(8,128)(2,1)S(1)} %get-tuple-element.34), channel_id=1, replica_groups=mesh['c'=4,'y'=4,'x'=4,'h'=2,'k'=2] {'c','h','k'}, dimensions={0} | all-to-all | bytes 131072 | tf_op jit(solution)/shard_map/all_to_all | solution.py:513
  73.0 0.4 shard_map.109
  73.4 12.8 %all_to_all.22.received = bf16[16,64,128]{2,1,0:T(8,128)(2,1)S(1)} all-to-all(bf16[16,64,128]{2,1,0:T(8,128)(2,1)S(1)} %shard_map.109), channel_id=1, replica_groups=mesh['c'=4,'y'=4,'x'=4,'h'=2,'k'=2] {'y','x'}, dimensions={0} | all-to-all | bytes 524288 | tf_op jit(solution)/shard_map/all_to_all | solution.py:518
  86.2 1.0 %shard_map.110 = (bf16[2,1024]{1,0:T(2,128)(2,1)}, f32[32,8,128]{2,1,0:T(8,128)}, f32[8,128]{1,0:T(8,128)}) custom-call(bf16[16,64,128]{2,1,0:T(8,128)(2,1)S(1)} %all_to_all.22.received, bf16[8,4,128,128]{3,2,1,0:T(8,128)(2,1)S(1)} %get-tuple-element.35.weights, f32[32,8,128]{2,1,0:T(8,128)S(1)} %get-tuple-element.36.tracer, ...), custom_call_target="tpu_custom_call" | custom-call | tf_op jit(solution)/shard_map/pallas_call | solution.py:520
  (2 shorter events, 0.1 us)
Async XLA Ops:
  23.4 15.4 %all-to-all-start.1 = ((bf16[8,160,128]{2,1,0:T(8,128)(2,1)}), bf16[8,160,128]{2,1,0:T(8,128)(2,1)S(1)}, u32[]{:S(2)}, u32[]{:S(2)}) async-start(bf16[8,160,128]{2,1,0:T(8,128)(2,1)} %get-tuple-element.24), calls=%async_computation.1 | async-start | bytes 655360 | tf_op jit(solution)/shard_map/all_to_all | solution.py:484
  31.6 11.6 %collective-permute-start.1 = (bf16[224,128]{1,0:T(8,128)(2,1)S(1)}, bf16[224,128]{1,0:T(8,128)(2,1)S(1)}, u32[]{:S(2)}, u32[]{:S(2)}) collective-permute-start(bf16[224,128]{1,0:T(8,128)(2,1)S(1)} %get-tuple-element.26.leaving), channel_id=1, source_target_pairs={{0,1},{1,0},{2,3},{3,2},{4,5},{5,4},{6,7},{7,6},{8,9},{9,8},{10,11... | collective-permute-start | bytes 172040 | tf_op jit(solution)/shard_map/ppermute | solution.py:473
  38.9 11.7 %collective-permute-start = (f32[160,128]{1,0:T(8,128)S(1)}, f32[160,128]{1,0:T(8,128)S(1)}, u32[]{:S(2)}, u32[]{:S(2)}) collective-permute-start(f32[160,128]{1,0:T(8,128)S(1)} %shard_map.105.flux), channel_id=1, source_target_pairs={{0,1},{1,0},{2,3},{3,2},{4,5},{5,4},{6,7},{7,6},{8,9},{9,8},{10,11... | collective-permute-start | bytes 245768 | tf_op jit(solution)/shard_map/ppermute | solution.py:486
  43.3 6.8 %collective-permute-start.2 = (bf16[160,128]{1,0:T(8,128)(2,1)S(1)}, bf16[160,128]{1,0:T(8,128)(2,1)S(1)}, u32[]{:S(2)}, u32[]{:S(2)}) collective-permute-start(bf16[160,128]{1,0:T(8,128)(2,1)S(1)} %get-tuple-element.27), channel_id=1, source_target_pairs={{0,2},{1,3},{2,0},{3,1},{4,6},{5,7},{6,4},{7,5},{8,10},{9,11},{10,... | collective-permute-start | bytes 122888 | tf_op jit(solution)/shard_map/ppermute | solution.py:477
  45.9 4.2 %collective-permute-start.3 = (bf16[160,128]{1,0:T(8,128)(2,1)S(1)}, bf16[160,128]{1,0:T(8,128)(2,1)S(1)}, u32[]{:S(2)}, u32[]{:S(2)}) collective-permute-start(bf16[160,128]{1,0:T(8,128)(2,1)S(1)} %get-tuple-element.28), channel_id=1, source_target_pairs={{2,4},{3,5},{4,2},{5,3},{6,8},{7,9},{8,6},{9,7},{10,12},{11,13},{1... | collective-permute-start | bytes 122888 | tf_op jit(solution)/shard_map/ppermute | solution.py:478
